TPU v7x, 32 devices: a whole 2x2x4 slice. The times are simulated.
32 devices in a mesh: parts: 2 (over x), rows: 16 (over z, y, core).
Axes of the slice: x: 2, y: 2, z: 4, core: 2. Of those that a mesh axis runs over, the one named last changes fastest.
Arguments:
- traces: bfloat16 [16, 4096, 2048], P('parts', 'rows'), parts along dimension 0, may hold values from -6 to 6
- offset_bin: int32 [16, 4096], P('parts', 'rows'), parts along dimension 0, may hold values from 0 to 15
- filters: float32 [16, 32], replicated, may hold values from -1 to 1
- data_matrix: bfloat16 [128, 2, 64, 4096], P('parts', None, 'rows'), parts along dimension 0, may hold values from -0.0625 to 0.0625
Outputs:
- multiples: bfloat16 [128, 2, 8, 64], P(('parts', 'rows')), parts along dimension 0
There are 2 independent parts, one for each index of `parts`. A program takes and returns all parts, laid end to end along the dimension named above; an argument that names none is the same for every part. Nothing has to cross between parts.
All inputs are finite; a program needn't handle non-finite values.
Results may differ from a plain program's by a relative error of at most 0.0067.
Values may be sent and summed in bfloat16 or wider, within the bound.
No kernel may reach another device: no remote copies, remote signals or barrier semaphores. Data moves between devices by JAX's collectives and lax.ppermute only.
A program may use at most 128 MiB of HBM per device.

v0:
```python
import functools
import math

import jax
import jax.numpy as jnp
import numpy as np
from jax import lax
from jax.experimental import pallas as pl
from jax.experimental.pallas import tpu as pltpu
from jax.sharding import PartitionSpec as P


FIRST = 64
BAND = 16
F32 = jnp.float32
BF16 = jnp.bfloat16


def dot(a, b, dims=((1,), (0,)), **kw):
    return lax.dot_general(a, b, (dims, ((), ())), preferred_element_type=F32, **kw)


def split(x, parts):
    pieces = []
    for _ in range(parts):
        piece = x.astype(BF16)
        pieces.append(piece)
        x = x - piece.astype(F32)
    return pieces


def transform_tables(freqs, length, taps):
    bands = freqs // BAND
    order = FIRST + np.arange(freqs).reshape(bands, 1, BAND)
    lanes = 2 * freqs

    def wave(samples, norm):
        angle = 2.0 * np.pi * ((samples[:, None, None, None] * order) % length) / length
        re, im = np.cos(angle) * norm, -np.sin(angle) * norm
        plain = np.concatenate([re, im], axis=2).reshape(len(samples), -1)
        swapped = np.concatenate([im, re], axis=2).reshape(len(samples), -1)
        return plain, swapped

    plain, swapped = wave(np.arange(length), 1.0 / math.sqrt(length))
    main = np.concatenate([plain, swapped], axis=1)
    main[length - taps :] = 0.0
    one, _ = wave(np.arange(taps), 1.0)
    one = one.reshape(taps, bands, 2, BAND)
    resp_a = np.concatenate([one[:, :, :1], one[:, :, :1]], axis=2).reshape(taps, -1)
    resp_b = np.concatenate([-one[:, :, 1:], one[:, :, 1:]], axis=2).reshape(taps, -1)
    resp = np.concatenate([resp_a, resp_b], axis=1)
    u = np.arange(taps)
    tail = np.zeros((taps, taps, lanes))
    for j in range(taps):
        live = u + j < taps
        tail[j, live] = plain[length - taps + u[live] + j]
    return (
        jnp.asarray(main, BF16),
        jnp.asarray(resp, F32),
        jnp.asarray(tail.reshape(taps, -1), BF16),
    )


def spectra_kernel(
    bands, trace, bin_of, filt, main_hbm, resp_hbm, tail_hbm, out,
    main, resp, tail, select, last_rows, last, binned, sems,
):
    step = pl.program_id(0)
    bins, taps = filt.shape
    width = main.shape[1] // 2
    shots, count = bin_of.shape
    group, _, length = trace.shape
    copies = [
        pltpu.make_async_copy(a, b, sems.at[i])
        for i, (a, b) in enumerate(((main_hbm, main), (resp_hbm, resp), (tail_hbm, tail)))
    ]

    @pl.when(step == 0)
    def _():
        for copy in copies:
            copy.start()
        column = jnp.transpose(bin_of[...].astype(F32), (1, 0))
        for shot in range(shots):
            value = jnp.broadcast_to(column[:, shot : shot + 1], (count, width))
            binned[shot] = value.astype(BF16)
        copies[1].wait()
        copies[2].wait()
        table = dot(filt[...], resp[...], precision=lax.Precision.HIGHEST)
        select[...] = jnp.zeros_like(select)
        for i, piece in enumerate(split(table, 3)):
            select[i * bins : (i + 1) * bins, :] = piece
        high, low = split(filt[...], 2)
        for u in range(taps):
            cols = tail[:, u * width : (u + 1) * width]
            last_rows[pl.ds(u, bins, stride=taps), :] = dot(high, cols) + dot(low, cols)
        last[...] = last_rows[...].astype(BF16)
        copies[0].wait()

    signal = trace[...].reshape(group * count, length)
    of = binned[pl.ds(step * group, group)].reshape(group * count, width).astype(F32)
    lane = lax.broadcasted_iota(jnp.int32, (1, width), 1)
    lane_bin = jnp.where(lane < 3 * bins, lane % bins, -1).astype(F32)
    chosen = jnp.where(of == lane_bin, 1.0, 0.0).astype(BF16)
    looked = dot(chosen, select[...])
    ends = signal[:, length - width :].astype(F32)
    shift = taps
    while shift < width:
        ends = jnp.where(lane >= width - shift, ends, pltpu.roll(ends, width - shift, 1))
        shift *= 2
    every = width // taps
    ending = [
        jnp.where(of == (lane // taps + base).astype(F32), ends, 0.0).astype(BF16)
        for base in range(0, bins, every)
    ]
    ending = jnp.concatenate(ending, axis=1)
    spectrum = dot(signal, main[...])
    value = (
        spectrum[:, :width] * looked[:, :width]
        + spectrum[:, width:] * looked[:, width:]
        + dot(ending, last[...])
    )
    chunk = 2 * BAND
    per = width // chunk
    place = lax.broadcasted_iota(jnp.int32, (count, width), 1) // chunk
    for phase in range(max(per // group, 1)):

        @pl.when(step % max(per // group, 1) == phase)
        def _():
            moved = []
            for i in range(group):
                j = (phase * group + i) % per
                part = value[i * count : (i + 1) * count]
                moved.append(part if j == 0 else pltpu.roll(part, j * chunk, 1))
            for band in range(bands):
                result = moved[0] if phase == 0 else out[band].astype(F32)
                for i in range(group):
                    j = (phase * group + i) % per
                    if phase or i:
                        result = jnp.where(place == (band + j) % per, moved[i], result)
                out[band] = result.astype(BF16)


def chunk_of(shot, band, per):
    return shot // per * per + (band + shot % per) % per


def spectra_of(traces, offset_bin, filters, freqs):
    shots, count, length = traces.shape
    bins, taps = filters.shape
    bands = freqs // BAND
    width = 2 * freqs
    group = 2
    tables = transform_tables(freqs, length, taps)
    per = width // (2 * BAND)
    hbm = pl.BlockSpec(memory_space=pltpu.HBM)
    return pl.pallas_call(
        functools.partial(spectra_kernel, bands),
        grid=(shots // group,),
        in_specs=[
            pl.BlockSpec((group, count, length), lambda s: (s, 0, 0)),
            pl.BlockSpec((shots, count), lambda s: (0, 0)),
            pl.BlockSpec((bins, taps), lambda s: (0, 0)),
            hbm,
            hbm,
            hbm,
        ],
        out_specs=pl.BlockSpec((bands, count, width), lambda s: (0, 0, s * group // per)),
        out_shape=jax.ShapeDtypeStruct((bands, count, shots * 2 * BAND), BF16),
        scratch_shapes=[
            pltpu.VMEM(tables[0].shape, BF16),
            pltpu.VMEM(tables[1].shape, F32),
            pltpu.VMEM(tables[2].shape, BF16),
            pltpu.VMEM((width, 2 * width), BF16),
            pltpu.VMEM((taps * bins, width), F32),
            pltpu.VMEM((taps * bins, width), BF16),
            pltpu.VMEM((shots, count, width), BF16),
            pltpu.SemaphoreType.DMA((3,)),
        ],
        compiler_params=pltpu.CompilerParams(vmem_limit_bytes=56 << 20),
        cost_estimate=pl.CostEstimate(
            flops=2 * shots * count * length * 2 * width,
            bytes_accessed=traces.size * 2,
            transcendentals=0,
        ),
        name="spectra",
    )(traces, offset_bin, filters, *tables)


def rows_kernel(block, head, starts, source, first, rest, buffer, in_sems, out_sems):
    slots = buffer.shape[1]
    bands = buffer.shape[0]
    ins = []
    device = lax.axis_index("rows")
    for i in range(slots):
        start = jnp.int32(0)
        for d, row in enumerate(starts):
            start = jnp.where(device == d, jnp.int32(int(row[i]) * block), start)
        column = pl.multiple_of(start, block)
        ins.append(
            pltpu.make_async_copy(
                source.at[:, :, :, :, pl.ds(column, block)], buffer.at[:, i], in_sems.at[i]
            )
        )
        ins[-1].start()
    outs = []
    for i in range(slots):
        ins[i].wait()
        for k, (low, high, target) in enumerate(((0, head, first), (head, bands, rest))):
            copy = pltpu.make_async_copy(
                buffer.at[low:high, i], target.at[:, i], out_sems.at[i, k]
            )
            copy.start()
            outs.append(copy)
    for copy in outs:
        copy.wait()


def rows_for(data_matrix, starts, block, head):
    freqs, parts, rows, _ = data_matrix.shape
    bands = freqs // BAND
    slots = starts.shape[1]
    source = data_matrix.reshape(bands, BAND, parts, rows, -1)
    if block % 128:
        starts = jnp.asarray(starts)[lax.axis_index("rows")]
        pieces = [
            lax.dynamic_slice_in_dim(source, starts[i] * block, block, 4) for i in range(slots)
        ]
        both = jnp.stack(pieces, axis=1)
        return both[:head], both[head:]
    shape = (slots, BAND, parts, rows, block)
    kind = data_matrix.dtype
    return pl.pallas_call(
        functools.partial(rows_kernel, block, head, starts),
        in_specs=[pl.BlockSpec(memory_space=pltpu.HBM)],
        out_specs=[pl.BlockSpec(memory_space=pltpu.HBM)] * 2,
        out_shape=[
            jax.ShapeDtypeStruct((head,) + shape, kind),
            jax.ShapeDtypeStruct((bands - head,) + shape, kind),
        ],
        scratch_shapes=[
            pltpu.VMEM((bands,) + shape, kind),
            pltpu.SemaphoreType.DMA((slots,)),
            pltpu.SemaphoreType.DMA((slots, 2)),
        ],
        name="rows_for",
    )(source)


def predict_kernel(members, slots, *refs):
    rows_in, spectra_in = refs[:members], refs[members : members + slots]
    mask_ref, fold_a, fold_b, out = refs[members + slots :]
    columns = []
    for i in range(rows_in[0].shape[1]):
        part = jnp.concatenate([r[0, i] for r in rows_in], axis=2)
        columns.append(part.reshape(-1, part.shape[-1]))
    matrix = columns[0] if len(columns) == 1 else jnp.concatenate(columns, axis=1)
    spectra = [r[0] for r in spectra_in]
    spectra = spectra[0] if slots == 1 else jnp.concatenate(spectra, axis=0)
    rows = rows_in[0].shape[4] * members
    total = dot(matrix, spectra)
    total = total.reshape(BAND, 2, rows, -1)
    acc = None
    for c, fold in enumerate((fold_a, fold_b)):
        value = total[:, c].reshape(BAND * rows, -1)
        value = jnp.where(mask_ref[...] != 0, value, 0.0)
        for piece in split(value, 2):
            term = dot(piece, fold[0])
            acc = term if acc is None else acc + term
    dests = out.shape[0]
    acc = acc.reshape(dests, BAND // dests, rows, -1)
    value = acc[:, 0]
    for i in range(1, BAND // dests):
        value = value + acc[:, i]
    out[...] = value.astype(out.dtype)


def predict(row_parts, spectra_parts, share, first):
    number, pieces, _, _, rows, depth = row_parts[0].shape
    bands, block, cols = spectra_parts[0].shape
    shots = cols // (2 * BAND)
    per = 2 * BAND * bands // (2 * BAND)
    members, slots = len(row_parts), len(spectra_parts)
    all_rows = members * rows
    lanes = share * 2 * shots
    index = np.arange(cols)
    col_c, col_f = index // BAND % 2, index % BAND
    row_f = np.arange(BAND * all_rows) // all_rows
    mask = (row_f[:, None] == col_f[None, :]).astype(np.float32)
    fold_a = np.zeros((bands, cols, share, 2, shots), np.float32)
    fold_b = np.zeros((bands, cols, share, 2, shots), np.float32)
    for band in range(bands):
        shot_at = np.zeros(shots, np.int64)
        for shot in range(shots):
            shot_at[chunk_of(shot, band, per)] = shot
        col_s = shot_at[index // (2 * BAND)]
        fold_a[band, index, col_f % share, col_c, col_s] = 1.0
        fold_b[band, index, col_f % share, 1 - col_c, col_s] = np.where(col_c == 1, -1.0, 1.0)
    consts = (
        jnp.asarray(mask, F32),
        jnp.asarray(fold_a.reshape(bands, cols, lanes), BF16),
        jnp.asarray(fold_b.reshape(bands, cols, lanes), BF16),
    )
    dests = BAND // share
    return pl.pallas_call(
        functools.partial(predict_kernel, members, slots),
        grid=(number,),
        in_specs=[pl.BlockSpec((1, pieces, BAND, 2, rows, depth), lambda q: (q, 0, 0, 0, 0, 0))]
        * members
        + [pl.BlockSpec((1, block, cols), lambda q: (first + q, 0, 0))] * slots
        + [pl.BlockSpec(mask.shape, lambda q: (0, 0))]
        + [pl.BlockSpec((1, cols, lanes), lambda q: (first + q, 0, 0))] * 2,
        out_specs=pl.BlockSpec((dests, all_rows, lanes), lambda q: (q, 0, 0)),
        out_shape=jax.ShapeDtypeStruct((number * dests, all_rows, lanes), BF16),
        compiler_params=pltpu.CompilerParams(vmem_limit_bytes=48 << 20),
        name="predict",
    )(*row_parts, *spectra_parts, *consts)


def ring_of(length):
    return list(range(0, length, 2)) + list(range(1, length, 2))[::-1]


def shards(devices, members, traces, offset_bin, filters, data_matrix):
    shot_count, block, _ = traces.shape
    freqs, _, row_count, _ = data_matrix.shape
    lines = devices // members
    ring = ring_of(lines)
    after = {ring[i]: ring[(i + 1) % lines] for i in range(lines)}
    before = {b: a for a, b in after.items()}
    blocks = np.zeros((devices, members, lines), np.int32)
    for device in range(devices):
        line, member = divmod(device, members)
        for slot in range(lines):
            for m in range(members):
                blocks[device, m, slot] = line * members + (member ^ m)
            line = before[line]

    bands = freqs // BAND
    head = max(bands - 1, 1)
    first_parts, rest_parts = [None] * members, [None] * members

    def exchange(m):
        first, rest = rows_for(data_matrix, blocks[:, m], block, head)
        pairs = [(i, i ^ m) for i in range(devices)]
        if m:
            first = lax.ppermute(first, "rows", pairs)
            rest = lax.ppermute(rest, "rows", pairs)
        first_parts[m], rest_parts[m] = first, rest

    for m in range(members - 1, -1, -1):
        exchange(m)

    spectra = spectra_of(traces, offset_bin, filters, freqs)
    spectra_parts = [spectra]
    step = [(i, after[i // members] * members + i % members) for i in range(devices)]
    for _ in range(lines - 1):
        spectra_parts.append(lax.ppermute(spectra_parts[-1], "rows", step))
    if block % 128:
        spectra_parts = [jnp.concatenate(spectra_parts, axis=1)]
        joined = lambda x: jnp.concatenate([x[:, i : i + 1] for i in range(lines)], axis=5)
        first_parts = [joined(x) for x in first_parts]
        rest_parts = [joined(x) for x in rest_parts]

    share = freqs // devices
    early = predict(first_parts, spectra_parts, share, 0)
    late = predict(rest_parts, spectra_parts, share, head)
    partial_value = jnp.concatenate([early, late], axis=0)
    received = lax.all_to_all(partial_value, "rows", split_axis=0, concat_axis=0, tiled=True)
    choose = np.zeros((lines, members, members, row_count, lines, members, row_count))
    for line in range(lines):
        for member in range(members):
            for j in range(members):
                for r in range(row_count):
                    choose[line, member, member ^ j, r, line, j, r] = 1.0
    rows = devices * members * row_count
    choose = jnp.asarray(choose.reshape(rows, devices * row_count), BF16)
    final = dot(received.reshape(rows, -1), choose, ((0,), (0,)))
    return final.astype(BF16).reshape(share, 2, shot_count, devices * row_count)


def solution(mesh):
    devices = mesh.shape["rows"]
    members = math.gcd(devices, 4)
    in_specs = (P("parts", "rows", None), P("parts", "rows"), P(), P("parts", None, "rows", None))
    out_specs = P(("parts", "rows"), None, None, None)
    return jax.shard_map(
        functools.partial(shards, devices, members),
        mesh=mesh,
        in_specs=in_specs,
        out_specs=out_specs,
        check_vma=False,
    )
```

profile of v0, /device:TPU:0, one launch (start us, length us, event | category | flops | bytes accessed | tf_op | source)
XLA Modules:
  0.0 99.0 jit_solution(7228176990755759949)
XLA Ops:
  0.0 9.2 %spectra.1.refs_4_ = bf16[4,256,256]{2,1,0:T(8,128)(2,1)} custom-call(bf16[8,256,2048]{2,1,0:T(8,128)(2,1)} %trace.1, s32[8,256]{1,0:T(8,128)} %bin_of.1, f32[16,32]{1,0:T(8,128)} %filt.1, bf16[2048,256]{1,0:T(8,128)(2,1)} %constant.14.clone.main_hbm, f32[32,256]{1,0:T(8,128)} %constant.15.clone.resp_hbm, bf16[32,4096]{1,0:T(8,128)(2,1)} %constant.16.clone.tail_hbm), custom_call_target="tpu_custom_call" | custom-call | flops 2147483648 | bytes 8388608 | tf_op jit(solution)/shard_map/spectra/pallas_call | solution.py:156
  9.2 4.1 %collective-permute-start.3 = (bf16[4,256,256]{2,1,0:T(8,128)(2,1)}, bf16[4,256,256]{2,1,0:T(8,128)(2,1)S(1)}, u32[]{:S(2)}, u32[]{:S(2)}) collective-permute-start(bf16[4,256,256]{2,1,0:T(8,128)(2,1)} %spectra.1.refs_4_), channel_id=1, source_target_pairs={{0,8},{1,9},{2,10},{3,11},{4,0},{5,1},{6,2},{7,3},{8,12},{9,13},{1... | collective-permute-start | bytes 1572872 | tf_op jit(solution)/shard_map/ppermute | solution.py:357
  13.3 11.5 %collective-permute-done.3.refs_5_ = bf16[4,256,256]{2,1,0:T(8,128)(2,1)S(1)} collective-permute-done((bf16[4,256,256]{2,1,0:T(8,128)(2,1)}, bf16[4,256,256]{2,1,0:T(8,128)(2,1)S(1)}, u32[]{:S(2)}, u32[]{:S(2)}) %collective-permute-start.3) | collective-permute-done | bytes 524320 | tf_op jit(solution)/shard_map/ppermute | solution.py:357
  24.8 3.3 %collective-permute-start.4 = (bf16[4,256,256]{2,1,0:T(8,128)(2,1)S(1)}, bf16[4,256,256]{2,1,0:T(8,128)(2,1)S(1)}, u32[]{:S(2)}, u32[]{:S(2)}) collective-permute-start(bf16[4,256,256]{2,1,0:T(8,128)(2,1)S(1)} %collective-permute-done.3.refs_5_), channel_id=1, source_target_pairs={{0,8},{1,9},{2,10},{3,11},{4,0},{5,1},{6,2},{7,3},{8,12},{9,13},{1... | collective-permute-start | bytes 1572872 | tf_op jit(solution)/shard_map/ppermute | solution.py:357
  28.1 0.0 copy-start
  28.1 0.0 copy-start.1
  28.1 0.0 copy-start.2
  28.1 0.0 copy-start.3
  28.1 2.2 %rows_for.7 = (bf16[3,4,16,2,4,256]{5,4,3,2,1,0:T(4,128)(2,1)}, bf16[1,4,16,2,4,256]{5,4,3,2,1,0:T(4,128)(2,1)}) custom-call(bf16[4,16,2,4,4096]{4,3,2,1,0:T(4,128)(2,1)} %bitcast.5), custom_call_target="tpu_custom_call" | custom-call | tf_op jit(solution)/shard_map/rows_for/pallas_call | solution.py:232
  30.3 0.1 collective-permute-start.8
  30.4 1.7 %collective-permute-start.2 = (bf16[3,4,16,2,4,256]{5,4,3,2,1,0:T(4,128)(2,1)}, bf16[3,4,16,2,4,256]{5,4,3,2,1,0:T(4,128)(2,1)}, u32[]{:S(2)}, u32[]{:S(2)}) collective-permute-start(bf16[3,4,16,2,4,256]{5,4,3,2,1,0:T(4,128)(2,1)} %get-tuple-element.16), channel_id=1, source_target_pairs={{0,3},{1,2},{2,1},{3,0},{4,7},{5,6},{6,5},{7,4},{8,11},{9,10},{10,... | collective-permute-start | bytes 2359304 | tf_op jit(solution)/shard_map/ppermute | solution.py:346
  32.1 2.1 %rows_for.6 = (bf16[3,4,16,2,4,256]{5,4,3,2,1,0:T(4,128)(2,1)}, bf16[1,4,16,2,4,256]{5,4,3,2,1,0:T(4,128)(2,1)}) custom-call(bf16[4,16,2,4,4096]{4,3,2,1,0:T(4,128)(2,1)} %bitcast.6), custom_call_target="tpu_custom_call" | custom-call | tf_op jit(solution)/shard_map/rows_for/pallas_call | solution.py:232
  34.2 0.0 copy-start.6
  34.2 1.6 %collective-permute-start.1 = (bf16[3,4,16,2,4,256]{5,4,3,2,1,0:T(4,128)(2,1)}, bf16[3,4,16,2,4,256]{5,4,3,2,1,0:T(4,128)(2,1)}, u32[]{:S(2)}, u32[]{:S(2)}) collective-permute-start(bf16[3,4,16,2,4,256]{5,4,3,2,1,0:T(4,128)(2,1)} %get-tuple-element.15), channel_id=1, source_target_pairs={{0,2},{1,3},{2,0},{3,1},{4,6},{5,7},{6,4},{7,5},{8,10},{9,11},{10,... | collective-permute-start | bytes 2359304 | tf_op jit(solution)/shard_map/ppermute | solution.py:346
  35.8 2.1 %rows_for.5 = (bf16[3,4,16,2,4,256]{5,4,3,2,1,0:T(4,128)(2,1)}, bf16[1,4,16,2,4,256]{5,4,3,2,1,0:T(4,128)(2,1)}) custom-call(bf16[4,16,2,4,4096]{4,3,2,1,0:T(4,128)(2,1)} %bitcast.7), custom_call_target="tpu_custom_call" | custom-call | tf_op jit(solution)/shard_map/rows_for/pallas_call | solution.py:232
  37.8 0.1 collective-permute-start
  37.9 1.2 %collective-permute-done.8.refs_3_ = bf16[1,4,16,2,4,256]{5,4,3,2,1,0:T(4,128)(2,1)S(1)} collective-permute-done((bf16[1,4,16,2,4,256]{5,4,3,2,1,0:T(4,128)(2,1)}, bf16[1,4,16,2,4,256]{5,4,3,2,1,0:T(4,128)(2,1)S(1)}, u32[]{:S(2)}, u32[]{:S(2)}) %collective-permute-start.8) | collective-permute-done | bytes 262176 | tf_op jit(solution)/shard_map/ppermute | solution.py:347
  39.1 1.6 %collective-permute-start.7 = (bf16[1,4,16,2,4,256]{5,4,3,2,1,0:T(4,128)(2,1)}, bf16[1,4,16,2,4,256]{5,4,3,2,1,0:T(4,128)(2,1)S(1)}, u32[]{:S(2)}, u32[]{:S(2)}) collective-permute-start(bf16[1,4,16,2,4,256]{5,4,3,2,1,0:T(4,128)(2,1)} %get-tuple-element.19), channel_id=1, source_target_pairs={{0,2},{1,3},{2,0},{3,1},{4,6},{5,7},{6,4},{7,5},{8,10},{9,11},{10,... | collective-permute-start | bytes 786440 | tf_op jit(solution)/shard_map/ppermute | solution.py:347
  40.7 0.0 collective-permute-done.4.refs_6_
  40.7 1.1 %collective-permute-start.5 = (bf16[4,256,256]{2,1,0:T(8,128)(2,1)S(1)}, bf16[4,256,256]{2,1,0:T(8,128)(2,1)S(1)}, u32[]{:S(2)}, u32[]{:S(2)}) collective-permute-start(bf16[4,256,256]{2,1,0:T(8,128)(2,1)S(1)} %collective-permute-done.4.refs_6_), channel_id=1, source_target_pairs={{0,8},{1,9},{2,10},{3,11},{4,0},{5,1},{6,2},{7,3},{8,12},{9,13},{1... | collective-permute-start | bytes 1572872 | tf_op jit(solution)/shard_map/ppermute | solution.py:357
  41.8 36.7 %collective-permute-done.7.refs_2_ = bf16[1,4,16,2,4,256]{5,4,3,2,1,0:T(4,128)(2,1)S(1)} collective-permute-done((bf16[1,4,16,2,4,256]{5,4,3,2,1,0:T(4,128)(2,1)}, bf16[1,4,16,2,4,256]{5,4,3,2,1,0:T(4,128)(2,1)S(1)}, u32[]{:S(2)}, u32[]{:S(2)}) %collective-permute-start.7) | collective-permute-done | bytes 262176 | tf_op jit(solution)/shard_map/ppermute | solution.py:347
  78.5 0.0 collective-permute-start.6
  78.5 2.1 %rows_for.4 = (bf16[3,4,16,2,4,256]{5,4,3,2,1,0:T(4,128)(2,1)}, bf16[1,4,16,2,4,256]{5,4,3,2,1,0:T(4,128)(2,1)}) custom-call(bf16[4,16,2,4,4096]{4,3,2,1,0:T(4,128)(2,1)} %bitcast.8), custom_call_target="tpu_custom_call" | custom-call | tf_op jit(solution)/shard_map/rows_for/pallas_call | solution.py:232
  80.6 0.0 collective-permute-done.6.refs_1_
  80.6 0.0 collective-permute-done.5.refs_7_
  80.7 0.0 copy-done
  80.7 0.0 copy-done.1
  80.7 0.0 copy-done.2
  80.7 0.0 copy-done.3
  80.7 0.0 copy-start.5
  80.7 0.9 copy-done.5
  81.6 1.8 %predict.3 = bf16[4,16,64]{2,1,0:T(8,128)(2,1)S(1)} custom-call(bf16[1,4,16,2,4,256]{5,4,3,2,1,0:T(4,128)(2,1)S(1)} %copy-done.5, bf16[1,4,16,2,4,256]{5,4,3,2,1,0:T(4,128)(2,1)} %collective-permute-done.6.refs_1_, bf16[1,4,16,2,4,256]{5,4,3,2,1,0:T(4,128)(2,1)S(1)} %collective-permute-done.7.refs_2_, ...), custom_call_target="tpu_custom_call" | custom-call | tf_op jit(solution)/shard_map/predict/pallas_call | solution.py:304
  83.5 0.0 collective-permute-done.2.refs_3_
  83.5 0.0 collective-permute-done.1.refs_2_
  83.5 0.0 collective-permute-done.refs_1_
  83.5 0.0 copy-start.4
  83.5 1.1 %copy-done.4 = bf16[3,4,16,2,4,256]{5,4,3,2,1,0:T(4,128)(2,1)S(1)} copy-done((bf16[3,4,16,2,4,256]{5,4,3,2,1,0:T(4,128)(2,1)S(1)}, bf16[3,4,16,2,4,256]{5,4,3,2,1,0:T(4,128)(2,1)}, u32[]{:S(2)}) %copy-start.4) | copy-done | bytes 786456
  84.6 4.0 %predict.2 = bf16[12,16,64]{2,1,0:T(8,128)(2,1)S(1)} custom-call(bf16[3,4,16,2,4,256]{5,4,3,2,1,0:T(4,128)(2,1)S(1)} %copy-done.4, bf16[3,4,16,2,4,256]{5,4,3,2,1,0:T(4,128)(2,1)} %collective-permute-done.refs_1_, bf16[3,4,16,2,4,256]{5,4,3,2,1,0:T(4,128)(2,1)} %collective-permute-done.1.refs_2_, ...), custom_call_target="tpu_custom_call" | custom-call | tf_op jit(solution)/shard_map/predict/pallas_call | solution.py:304
  88.7 0.1 reshape.15
  88.8 9.2 %all_to_all.5 = bf16[16,2,512]{2,1,0:T(2,128)(2,1)S(1)} all-to-all(bf16[16,2,512]{2,1,0:T(2,128)(2,1)S(1)} %reshape.15), channel_id=1, replica_groups=mesh['parts'=2,'rows'=16] {'rows'}, dimensions={0} | all-to-all | bytes 65536 | tf_op jit(solution)/shard_map/all_to_all | solution.py:368
  98.0 0.1 reshape.16
  98.2 0.0 copy-done.6
  98.2 0.8 convolution_convert_fusion
  (1 shorter events, 0.0 us)
Async XLA Ops:
  9.2 15.6 %collective-permute-start.3 = (bf16[4,256,256]{2,1,0:T(8,128)(2,1)}, bf16[4,256,256]{2,1,0:T(8,128)(2,1)S(1)}, u32[]{:S(2)}, u32[]{:S(2)}) collective-permute-start(bf16[4,256,256]{2,1,0:T(8,128)(2,1)} %spectra.1.refs_4_), channel_id=1, source_target_pairs={{0,8},{1,9},{2,10},{3,11},{4,0},{5,1},{6,2},{7,3},{8,12},{9,13},{1... | collective-permute-start | bytes 1572872 | tf_op jit(solution)/shard_map/ppermute | solution.py:357
  24.8 15.9 %collective-permute-start.4 = (bf16[4,256,256]{2,1,0:T(8,128)(2,1)S(1)}, bf16[4,256,256]{2,1,0:T(8,128)(2,1)S(1)}, u32[]{:S(2)}, u32[]{:S(2)}) collective-permute-start(bf16[4,256,256]{2,1,0:T(8,128)(2,1)S(1)} %collective-permute-done.3.refs_5_), channel_id=1, source_target_pairs={{0,8},{1,9},{2,10},{3,11},{4,0},{5,1},{6,2},{7,3},{8,12},{9,13},{1... | collective-permute-start | bytes 1572872 | tf_op jit(solution)/shard_map/ppermute | solution.py:357
  28.1 52.6 %copy-start = (bf16[4,256,256]{2,1,0:T(8,128)(2,1)S(1)}, bf16[4,256,256]{2,1,0:T(8,128)(2,1)}, u32[]{:S(2)}) copy-start(bf16[4,256,256]{2,1,0:T(8,128)(2,1)} %spectra.1.refs_4_) | copy-start | bytes 1572868
  28.1 52.6 %copy-start.1 = (bf16[4,256,64]{2,1,0:T(8,128)(2,1)S(1)}, bf16[4,256,64]{2,1,0:T(8,128)(2,1)}, u32[]{:S(2)}) copy-start(bf16[4,256,64]{2,1,0:T(8,128)(2,1)} %constant.19.clone.refs_10_) | copy-start | bytes 393220
  28.1 52.6 %copy-start.2 = (bf16[4,256,64]{2,1,0:T(8,128)(2,1)S(1)}, bf16[4,256,64]{2,1,0:T(8,128)(2,1)}, u32[]{:S(2)}) copy-start(bf16[4,256,64]{2,1,0:T(8,128)(2,1)} %constant.18.clone.refs_9_) | copy-start | bytes 393220
  28.1 52.6 %copy-start.3 = (f32[256,256]{1,0:T(8,128)S(1)}, f32[256,256]{1,0:T(8,128)}, u32[]{:S(2)}) copy-start(f32[256,256]{1,0:T(8,128)} %constant.17.clone.refs_8_) | copy-start | bytes 786436
  30.3 8.8 %collective-permute-start.8 = (bf16[1,4,16,2,4,256]{5,4,3,2,1,0:T(4,128)(2,1)}, bf16[1,4,16,2,4,256]{5,4,3,2,1,0:T(4,128)(2,1)S(1)}, u32[]{:S(2)}, u32[]{:S(2)}) collective-permute-start(bf16[1,4,16,2,4,256]{5,4,3,2,1,0:T(4,128)(2,1)} %get-tuple-element.20), channel_id=1, source_target_pairs={{0,3},{1,2},{2,1},{3,0},{4,7},{5,6},{6,5},{7,4},{8,11},{9,10},{10,... | collective-permute-start | bytes 786440 | tf_op jit(solution)/shard_map/ppermute | solution.py:347
  30.4 53.1 %collective-permute-start.2 = (bf16[3,4,16,2,4,256]{5,4,3,2,1,0:T(4,128)(2,1)}, bf16[3,4,16,2,4,256]{5,4,3,2,1,0:T(4,128)(2,1)}, u32[]{:S(2)}, u32[]{:S(2)}) collective-permute-start(bf16[3,4,16,2,4,256]{5,4,3,2,1,0:T(4,128)(2,1)} %get-tuple-element.16), channel_id=1, source_target_pairs={{0,3},{1,2},{2,1},{3,0},{4,7},{5,6},{6,5},{7,4},{8,11},{9,10},{10,... | collective-permute-start | bytes 2359304 | tf_op jit(solution)/shard_map/ppermute | solution.py:346
  34.2 64.0 %copy-start.6 = (bf16[256,64]{1,0:T(8,128)(2,1)S(1)}, bf16[256,64]{1,0:T(8,128)(2,1)}, u32[]{:S(2)}) copy-start(bf16[256,64]{1,0:T(8,128)(2,1)} %constant.20.clone) | copy-start | bytes 98308
  34.2 49.3 %collective-permute-start.1 = (bf16[3,4,16,2,4,256]{5,4,3,2,1,0:T(4,128)(2,1)}, bf16[3,4,16,2,4,256]{5,4,3,2,1,0:T(4,128)(2,1)}, u32[]{:S(2)}, u32[]{:S(2)}) collective-permute-start(bf16[3,4,16,2,4,256]{5,4,3,2,1,0:T(4,128)(2,1)} %get-tuple-element.15), channel_id=1, source_target_pairs={{0,2},{1,3},{2,0},{3,1},{4,6},{5,7},{6,4},{7,5},{8,10},{9,11},{10,... | collective-permute-start | bytes 2359304 | tf_op jit(solution)/shard_map/ppermute | solution.py:346
  37.8 45.7 %collective-permute-start = (bf16[3,4,16,2,4,256]{5,4,3,2,1,0:T(4,128)(2,1)}, bf16[3,4,16,2,4,256]{5,4,3,2,1,0:T(4,128)(2,1)}, u32[]{:S(2)}, u32[]{:S(2)}) collective-permute-start(bf16[3,4,16,2,4,256]{5,4,3,2,1,0:T(4,128)(2,1)} %get-tuple-element.14), channel_id=1, source_target_pairs={{0,1},{1,0},{2,3},{3,2},{4,5},{5,4},{6,7},{7,6},{8,9},{9,8},{10,11... | collective-permute-start | bytes 2359304 | tf_op jit(solution)/shard_map/ppermute | solution.py:346
  39.1 39.4 %collective-permute-start.7 = (bf16[1,4,16,2,4,256]{5,4,3,2,1,0:T(4,128)(2,1)}, bf16[1,4,16,2,4,256]{5,4,3,2,1,0:T(4,128)(2,1)S(1)}, u32[]{:S(2)}, u32[]{:S(2)}) collective-permute-start(bf16[1,4,16,2,4,256]{5,4,3,2,1,0:T(4,128)(2,1)} %get-tuple-element.19), channel_id=1, source_target_pairs={{0,2},{1,3},{2,0},{3,1},{4,6},{5,7},{6,4},{7,5},{8,10},{9,11},{10,... | collective-permute-start | bytes 786440 | tf_op jit(solution)/shard_map/ppermute | solution.py:347
  40.7 39.9 %collective-permute-start.5 = (bf16[4,256,256]{2,1,0:T(8,128)(2,1)S(1)}, bf16[4,256,256]{2,1,0:T(8,128)(2,1)S(1)}, u32[]{:S(2)}, u32[]{:S(2)}) collective-permute-start(bf16[4,256,256]{2,1,0:T(8,128)(2,1)S(1)} %collective-permute-done.4.refs_6_), channel_id=1, source_target_pairs={{0,8},{1,9},{2,10},{3,11},{4,0},{5,1},{6,2},{7,3},{8,12},{9,13},{1... | collective-permute-start | bytes 1572872 | tf_op jit(solution)/shard_map/ppermute | solution.py:357
  78.5 2.1 %collective-permute-start.6 = (bf16[1,4,16,2,4,256]{5,4,3,2,1,0:T(4,128)(2,1)}, bf16[1,4,16,2,4,256]{5,4,3,2,1,0:T(4,128)(2,1)}, u32[]{:S(2)}, u32[]{:S(2)}) collective-permute-start(bf16[1,4,16,2,4,256]{5,4,3,2,1,0:T(4,128)(2,1)} %get-tuple-element.18), channel_id=1, source_target_pairs={{0,1},{1,0},{2,3},{3,2},{4,5},{5,4},{6,7},{7,6},{8,9},{9,8},{10,11... | collective-permute-start | bytes 786440 | tf_op jit(solution)/shard_map/ppermute | solution.py:347
  80.7 1.0 copy-start.5
  83.5 1.1 %copy-start.4 = (bf16[3,4,16,2,4,256]{5,4,3,2,1,0:T(4,128)(2,1)S(1)}, bf16[3,4,16,2,4,256]{5,4,3,2,1,0:T(4,128)(2,1)}, u32[]{:S(2)}) copy-start(bf16[3,4,16,2,4,256]{5,4,3,2,1,0:T(4,128)(2,1)} %get-tuple-element.13.refs_0_) | copy-start | bytes 2359300
where the time goes:
time: 99.4 us; the launch traced here: 99 us
  waiting for transfers between devices  49.4 us (50%)
  Pallas kernels  23.4 us (24%)
  starting transfers between devices  13.6 us (14%)
  blocking collectives  9.24 us (9%)
  local copies, waits for them, and re-layouts  2.31 us (2%)
    ppermute x3, waiting for transfers between devices, exchange(): rest = lax.ppermute(rest, 'rows', pairs)  37.9 us
    ppermute x3, waiting for transfers between devices, shards(): spectra_parts.append(lax.ppermute(spectra_parts[-1], 'rows', step))  11.5 us
    all_to_all x1, blocking collectives, shards(): lax.all_to_all(partial_value, 'rows', split_axis=0, concat_axis=0, tiled=...  9.24 us
    pallas_call x1, Pallas kernels, spectra_of(): pl.pallas_call(functools.partial(spectra_kernel, bands), grid=(shots // g...  9.18 us
    ppermute x3, starting transfers between devices, shards(): spectra_parts.append(lax.ppermute(spectra_parts[-1], 'rows', step))  8.47 us
    pallas_call x4, Pallas kernels, rows_for(): pl.pallas_call(functools.partial(rows_kernel, block, head, starts), in_sp...  8.41 us
    pallas_call x2, Pallas kernels, predict(): pl.pallas_call(functools.partial(predict_kernel, members, slots), grid=(n...  5.85 us
    ppermute x3, starting transfers between devices, exchange(): first = lax.ppermute(first, 'rows', pairs)  3.39 us
  transfers between devices with their start and end apart: 9, of which 3 were waited for; matrix products, arithmetic and copies ran while one was open for 0% of the time, Pallas kernels for 10%

commit v1 on v0

--- a/solution.py
+++ b/solution.py
@@ -49,57 +49,61 @@
     resp_a = np.concatenate([one[:, :, :1], one[:, :, :1]], axis=2).reshape(taps, -1)
     resp_b = np.concatenate([-one[:, :, 1:], one[:, :, 1:]], axis=2).reshape(taps, -1)
     resp = np.concatenate([resp_a, resp_b], axis=1)
-    u = np.arange(taps)
-    tail = np.zeros((taps, taps, lanes))
-    for j in range(taps):
-        live = u + j < taps
-        tail[j, live] = plain[length - taps + u[live] + j]
-    return (
-        jnp.asarray(main, BF16),
-        jnp.asarray(resp, F32),
-        jnp.asarray(tail.reshape(taps, -1), BF16),
+    tail = np.zeros((lanes, lanes))
+    tail[:taps] = plain[length - taps :]
+    return jnp.asarray(main, BF16), jnp.asarray(resp, F32), jnp.asarray(tail, BF16)
+
+
+def prepare(bins, taps, width, filt, resp, tail, select, last):
+    filt_parts, resp_parts = split(filt[...], 2), split(resp[...], 2)
+    table = dot(
+        jnp.concatenate([filt_parts[0], filt_parts[1], filt_parts[0]], axis=1),
+        jnp.concatenate([resp_parts[0], resp_parts[0], resp_parts[1]], axis=0),
     )
-
-
-def spectra_kernel(
-    bands, trace, bin_of, filt, main_hbm, resp_hbm, tail_hbm, out,
-    main, resp, tail, select, last_rows, last, binned, sems,
-):
+    select[...] = jnp.zeros_like(select)
+    for i, piece in enumerate(split(table, 2)):
+        select[i * bins : (i + 1) * bins, :] = piece
+    rows = []
+    for b in range(bins):
+        row = jnp.pad(filt[b : b + 1, :], ((0, 0), (0, width - taps)))
+        row = jnp.broadcast_to(row, (taps, width))
+        rows.append(pltpu.roll(row, 0, 1, stride=1, stride_axis=0))
+    rows = jnp.concatenate(rows, axis=0)
+    high, low = split(rows, 2)
+    last[...] = (dot(high, tail[...]) + dot(low, tail[...])).astype(BF16)
+
+
+def chunk_of(shot, band, per):
+    return shot // per * per + (band + shot % per) % per
+
+
+def spectra_kernel(bands, bins, taps, first, *refs):
+    trace, bin_of, main_hbm = refs[:3]
+    if first:
+        filt, resp, tail, out, select, last, main, binned, sem = refs[3:]
+    else:
+        select, last, out, main, binned, sem = refs[3:]
     step = pl.program_id(0)
-    bins, taps = filt.shape
     width = main.shape[1] // 2
-    shots, count = bin_of.shape
+    shots, count = bin_of.shape[1:]
     group, _, length = trace.shape
-    copies = [
-        pltpu.make_async_copy(a, b, sems.at[i])
-        for i, (a, b) in enumerate(((main_hbm, main), (resp_hbm, resp), (tail_hbm, tail)))
-    ]
+    copy = pltpu.make_async_copy(main_hbm, main, sem)
 
     @pl.when(step == 0)
     def _():
-        for copy in copies:
-            copy.start()
-        column = jnp.transpose(bin_of[...].astype(F32), (1, 0))
+        copy.start()
+        column = jnp.transpose(bin_of[0].astype(F32), (1, 0))
         for shot in range(shots):
             value = jnp.broadcast_to(column[:, shot : shot + 1], (count, width))
             binned[shot] = value.astype(BF16)
-        copies[1].wait()
-        copies[2].wait()
-        table = dot(filt[...], resp[...], precision=lax.Precision.HIGHEST)
-        select[...] = jnp.zeros_like(select)
-        for i, piece in enumerate(split(table, 3)):
-            select[i * bins : (i + 1) * bins, :] = piece
-        high, low = split(filt[...], 2)
-        for u in range(taps):
-            cols = tail[:, u * width : (u + 1) * width]
-            last_rows[pl.ds(u, bins, stride=taps), :] = dot(high, cols) + dot(low, cols)
-        last[...] = last_rows[...].astype(BF16)
-        copies[0].wait()
+        if first:
+            prepare(bins, taps, width, filt, resp, tail, select, last)
+        copy.wait()
 
     signal = trace[...].reshape(group * count, length)
     of = binned[pl.ds(step * group, group)].reshape(group * count, width).astype(F32)
     lane = lax.broadcasted_iota(jnp.int32, (1, width), 1)
-    lane_bin = jnp.where(lane < 3 * bins, lane % bins, -1).astype(F32)
+    lane_bin = jnp.where(lane < 2 * bins, lane % bins, -1).astype(F32)
     chosen = jnp.where(of == lane_bin, 1.0, 0.0).astype(BF16)
     looked = dot(chosen, select[...])
     ends = signal[:, length - width :].astype(F32)
@@ -122,26 +126,22 @@
     chunk = 2 * BAND
     per = width // chunk
     place = lax.broadcasted_iota(jnp.int32, (count, width), 1) // chunk
-    for phase in range(max(per // group, 1)):
-
-        @pl.when(step % max(per // group, 1) == phase)
+    for phase in range(per // group):
+
+        @pl.when(step == phase)
         def _():
             moved = []
             for i in range(group):
-                j = (phase * group + i) % per
+                j = phase * group + i
                 part = value[i * count : (i + 1) * count]
                 moved.append(part if j == 0 else pltpu.roll(part, j * chunk, 1))
             for band in range(bands):
                 result = moved[0] if phase == 0 else out[band].astype(F32)
                 for i in range(group):
-                    j = (phase * group + i) % per
-                    if phase or i:
+                    j = phase * group + i
+                    if j:
                         result = jnp.where(place == (band + j) % per, moved[i], result)
                 out[band] = result.astype(BF16)
-
-
-def chunk_of(shot, band, per):
-    return shot // per * per + (band + shot % per) % per
 
 
 def spectra_of(traces, offset_bin, filters, freqs):
@@ -150,40 +150,50 @@
     bands = freqs // BAND
     width = 2 * freqs
     group = 2
-    tables = transform_tables(freqs, length, taps)
+    main, resp, tail = transform_tables(freqs, length, taps)
     per = width // (2 * BAND)
-    hbm = pl.BlockSpec(memory_space=pltpu.HBM)
-    return pl.pallas_call(
-        functools.partial(spectra_kernel, bands),
-        grid=(shots // group,),
-        in_specs=[
-            pl.BlockSpec((group, count, length), lambda s: (s, 0, 0)),
-            pl.BlockSpec((shots, count), lambda s: (0, 0)),
-            pl.BlockSpec((bins, taps), lambda s: (0, 0)),
-            hbm,
-            hbm,
-            hbm,
-        ],
-        out_specs=pl.BlockSpec((bands, count, width), lambda s: (0, 0, s * group // per)),
-        out_shape=jax.ShapeDtypeStruct((bands, count, shots * 2 * BAND), BF16),
-        scratch_shapes=[
-            pltpu.VMEM(tables[0].shape, BF16),
-            pltpu.VMEM(tables[1].shape, F32),
-            pltpu.VMEM(tables[2].shape, BF16),
-            pltpu.VMEM((width, 2 * width), BF16),
-            pltpu.VMEM((taps * bins, width), F32),
-            pltpu.VMEM((taps * bins, width), BF16),
-            pltpu.VMEM((shots, count, width), BF16),
-            pltpu.SemaphoreType.DMA((3,)),
-        ],
-        compiler_params=pltpu.CompilerParams(vmem_limit_bytes=56 << 20),
-        cost_estimate=pl.CostEstimate(
-            flops=2 * shots * count * length * 2 * width,
-            bytes_accessed=traces.size * 2,
-            transcendentals=0,
-        ),
-        name="spectra",
-    )(traces, offset_bin, filters, *tables)
+    out_shape = jax.ShapeDtypeStruct((bands, count, width), BF16)
+    made = [
+        jax.ShapeDtypeStruct((width, 2 * width), BF16),
+        jax.ShapeDtypeStruct((taps * bins, width), BF16),
+    ]
+    whole = lambda x: pl.BlockSpec(x.shape, lambda s: (0,) * len(x.shape))
+    binned = offset_bin.reshape(shots // per, per, count)
+    results, extra = [], None
+    for part in range(shots // per):
+        first = part == 0
+        more = [filters, resp, tail] if first else extra
+        outs = pl.pallas_call(
+            functools.partial(spectra_kernel, bands, bins, taps, first),
+            grid=(per // group,),
+            in_specs=[
+                pl.BlockSpec(
+                    (group, count, length),
+                    functools.partial(lambda p, s: (p + s, 0, 0), part * per // group),
+                ),
+                pl.BlockSpec((1, per, count), functools.partial(lambda p, s: (p, 0, 0), part)),
+                pl.BlockSpec(memory_space=pltpu.HBM),
+            ]
+            + [whole(x) for x in more],
+            out_specs=[whole(out_shape)] + ([whole(x) for x in made] if first else []),
+            out_shape=[out_shape] + (made if first else []),
+            scratch_shapes=[
+                pltpu.VMEM(main.shape, BF16),
+                pltpu.VMEM((per, count, width), BF16),
+                pltpu.SemaphoreType.DMA,
+            ],
+            compiler_params=pltpu.CompilerParams(vmem_limit_bytes=60 << 20),
+            cost_estimate=pl.CostEstimate(
+                flops=2 * per * count * length * 2 * width,
+                bytes_accessed=per * count * length * 2,
+                transcendentals=0,
+            ),
+            name="spectra",
+        )(traces, binned, main, *more)
+        if first:
+            extra = outs[1:]
+        results.append(outs[0])
+    return results
 
 
 def rows_kernel(block, head, starts, source, first, rest, buffer, in_sems, out_sems):
@@ -246,15 +256,18 @@
     )(source)
 
 
-def predict_kernel(members, slots, *refs):
-    rows_in, spectra_in = refs[:members], refs[members : members + slots]
-    mask_ref, fold_a, fold_b, out = refs[members + slots :]
+def predict_kernel(members, slots, parts, *refs):
+    rows_in, spectra_in = refs[:members], refs[members : members + slots * parts]
+    mask_ref, fold_a, fold_b, out = refs[members + slots * parts :]
     columns = []
     for i in range(rows_in[0].shape[1]):
         part = jnp.concatenate([r[0, i] for r in rows_in], axis=2)
         columns.append(part.reshape(-1, part.shape[-1]))
     matrix = columns[0] if len(columns) == 1 else jnp.concatenate(columns, axis=1)
-    spectra = [r[0] for r in spectra_in]
+    spectra = [
+        jnp.concatenate([spectra_in[p * slots + i][0] for p in range(parts)], axis=1)
+        for i in range(slots)
+    ]
     spectra = spectra[0] if slots == 1 else jnp.concatenate(spectra, axis=0)
     rows = rows_in[0].shape[4] * members
     total = dot(matrix, spectra)
@@ -276,10 +289,12 @@
 
 def predict(row_parts, spectra_parts, share, first):
     number, pieces, _, _, rows, depth = row_parts[0].shape
-    bands, block, cols = spectra_parts[0].shape
+    parts, slots = len(spectra_parts), len(spectra_parts[0])
+    bands, block, width = spectra_parts[0][0].shape
+    cols = width * parts
     shots = cols // (2 * BAND)
-    per = 2 * BAND * bands // (2 * BAND)
-    members, slots = len(row_parts), len(spectra_parts)
+    per = width // (2 * BAND)
+    members = len(row_parts)
     all_rows = members * rows
     lanes = share * 2 * shots
     index = np.arange(cols)
@@ -302,18 +317,18 @@
     )
     dests = BAND // share
     return pl.pallas_call(
-        functools.partial(predict_kernel, members, slots),
+        functools.partial(predict_kernel, members, slots, parts),
         grid=(number,),
         in_specs=[pl.BlockSpec((1, pieces, BAND, 2, rows, depth), lambda q: (q, 0, 0, 0, 0, 0))]
         * members
-        + [pl.BlockSpec((1, block, cols), lambda q: (first + q, 0, 0))] * slots
+        + [pl.BlockSpec((1, block, width), lambda q: (first + q, 0, 0))] * (slots * parts)
         + [pl.BlockSpec(mask.shape, lambda q: (0, 0))]
         + [pl.BlockSpec((1, cols, lanes), lambda q: (first + q, 0, 0))] * 2,
         out_specs=pl.BlockSpec((dests, all_rows, lanes), lambda q: (q, 0, 0)),
         out_shape=jax.ShapeDtypeStruct((number * dests, all_rows, lanes), BF16),
         compiler_params=pltpu.CompilerParams(vmem_limit_bytes=48 << 20),
         name="predict",
-    )(*row_parts, *spectra_parts, *consts)
+    )(*row_parts, *[x for part in spectra_parts for x in part], *consts)
 
 
 def ring_of(length):
@@ -350,13 +365,13 @@
     for m in range(members - 1, -1, -1):
         exchange(m)
 
-    spectra = spectra_of(traces, offset_bin, filters, freqs)
-    spectra_parts = [spectra]
+    spectra_parts = [[x] for x in spectra_of(traces, offset_bin, filters, freqs)]
     step = [(i, after[i // members] * members + i % members) for i in range(devices)]
     for _ in range(lines - 1):
-        spectra_parts.append(lax.ppermute(spectra_parts[-1], "rows", step))
+        for part in spectra_parts:
+            part.append(lax.ppermute(part[-1], "rows", step))
     if block % 128:
-        spectra_parts = [jnp.concatenate(spectra_parts, axis=1)]
+        spectra_parts = [[jnp.concatenate(part, axis=1)] for part in spectra_parts]
         joined = lambda x: jnp.concatenate([x[:, i : i + 1] for i in range(lines)], axis=5)
         first_parts = [joined(x) for x in first_parts]
         rest_parts = [joined(x) for x in rest_parts]

time: 99.4 us -> 85.1 us (0.86)
  waiting for transfers between devices: 49.4 us -> 30.5 us
  local copies, waits for them, and re-layouts: 2.31 us -> 5.28 us
  Pallas kernels: 23.4 us -> 25 us
    ppermute x3, waiting for transfers between devices: 37.9 us -> 5.46 us  [exchange(): rest = lax.ppermute(rest, 'rows', pairs)]
    ppermute x3 -> x6, waiting for transfers between devices: 11.5 us -> 19.1 us  [shards(): part.append(lax.ppermute(part[-1], 'rows', step))]
    ppermute x3, waiting for transfers between devices: 0.01 us -> 5.9 us  [exchange(): first = lax.ppermute(first, 'rows', pairs)]
    unnamed x16 -> x22, local copies, waits for them, and re-layouts: 2.31 us -> 3.98 us
    pallas_call x3 -> x4, Pallas kernels: 15 us -> 16.6 us  [the longest x2 11.7 us: spectra_of(): pl.pallas_call(functools.partial(spectra_kernel, bands, bins, taps, first...]
    reshape x0 -> x1, local copies, waits for them, and re-layouts: none -> 1.3 us  [spectra_of(): binned = offset_bin.reshape(shots // per, per, count)]
    ppermute x3 -> x6, starting transfers between devices: 8.47 us -> 8.95 us  [shards(): part.append(lax.ppermute(part[-1], 'rows', step))]
  transfers between devices with their start and end apart: 9 -> 12, of which waited for: 3 -> 7; matrix products, arithmetic and copies ran while one was open for 0% -> 0% of each run, Pallas kernels for 10% -> 11%
where the time goes in v1:
time: 85.1 us; the launch traced here: 84.7 us
  waiting for transfers between devices  30.5 us (36%)
  Pallas kernels  25 us (29%)
  starting transfers between devices  13.7 us (16%)
  blocking collectives  9.2 us (11%)
  local copies, waits for them, and re-layouts  5.28 us (6%)
    ppermute x6, waiting for transfers between devices, shards(): part.append(lax.ppermute(part[-1], 'rows', step))  19.1 us
    pallas_call x2, Pallas kernels, spectra_of(): pl.pallas_call(functools.partial(spectra_kernel, bands, bins, taps, first...  11.7 us
    all_to_all x1, blocking collectives, shards(): lax.all_to_all(partial_value, 'rows', split_axis=0, concat_axis=0, tiled=...  9.2 us
    ppermute x6, starting transfers between devices, shards(): part.append(lax.ppermute(part[-1], 'rows', step))  8.95 us
    pallas_call x4, Pallas kernels, rows_for(): pl.pallas_call(functools.partial(rows_kernel, block, head, starts), in_sp...  8.43 us
    ppermute x3, waiting for transfers between devices, exchange(): first = lax.ppermute(first, 'rows', pairs)  5.9 us
    ppermute x3, waiting for transfers between devices, exchange(): rest = lax.ppermute(rest, 'rows', pairs)  5.46 us
    pallas_call x2, Pallas kernels, predict(): pl.pallas_call(functools.partial(predict_kernel, members, slots, parts),...  4.9 us
  transfers between devices with their start and end apart: 12, of which 7 were waited for; matrix products, arithmetic and copies ran while one was open for 0% of the time, Pallas kernels for 11%

profile of v1, /device:TPU:0, one launch (start us, length us, event | category | flops | bytes accessed | tf_op | source)
XLA Modules:
  0.0 84.7 jit_solution(10322258701894245537)
XLA Ops:
  0.0 1.3 %reshape.16.refs_1_ = s32[2,4,256]{2,1,0:T(4,128)} reshape(s32[8,256]{1,0:T(8,128)} %param.15) | data formatting | bytes 16384 | tf_op jit(solution)/shard_map/reshape | solution.py:161
  1.3 5.9 %spectra.2 = (bf16[4,256,128]{2,1,0:T(8,128)(2,1)}, bf16[128,256]{1,0:T(8,128)(2,1)}, bf16[512,128]{1,0:T(8,128)(2,1)}) custom-call(bf16[8,256,2048]{2,1,0:T(8,128)(2,1)} %refs_0_.3, s32[2,4,256]{2,1,0:T(4,128)} %reshape.16.refs_1_, bf16[2048,256]{1,0:T(8,128)(2,1)} %constant.14.clone.refs_2_, f32[16,32]{1,0:T(8,128)} %refs_3_.1, ...), custom_call_target="tpu_custom_call" | custom-call | flops 1073741824 | bytes 4194304 | tf_op jit(solution)/shard_map/spectra/pallas_call | solution.py:166
  7.2 0.0 copy-start.4
  7.2 5.8 %spectra.3.refs_8_ = bf16[4,256,128]{2,1,0:T(8,128)(2,1)} custom-call(bf16[8,256,2048]{2,1,0:T(8,128)(2,1)} %refs_0_.3, s32[2,4,256]{2,1,0:T(4,128)} %reshape.16.refs_1_, bf16[2048,256]{1,0:T(8,128)(2,1)} %constant.14.clone.refs_2_, bf16[128,256]{1,0:T(8,128)(2,1)} %get-tuple-element.21.refs_3_, bf16[512,128]{1,0:T(8,128)(2,1)} %get-tuple-element.22.refs_4_), custom_call_target="tpu_custom_call" | custom-call | flops 1073741824 | bytes 4194304 | tf_op jit(solution)/shard_map/spectra/pallas_call | solution.py:166
  13.0 4.1 %collective-permute-start.6 = (bf16[4,256,128]{2,1,0:T(8,128)(2,1)}, bf16[4,256,128]{2,1,0:T(8,128)(2,1)S(1)}, u32[]{:S(2)}, u32[]{:S(2)}) collective-permute-start(bf16[4,256,128]{2,1,0:T(8,128)(2,1)} %spectra.3.refs_8_), channel_id=1, source_target_pairs={{0,8},{1,9},{2,10},{3,11},{4,0},{5,1},{6,2},{7,3},{8,12},{9,13},{1... | collective-permute-start | bytes 786440 | tf_op jit(solution)/shard_map/ppermute | solution.py:372
  17.1 0.0 copy-done.4
  17.1 1.6 %collective-permute-start.3 = (bf16[4,256,128]{2,1,0:T(8,128)(2,1)S(1)}, bf16[4,256,128]{2,1,0:T(8,128)(2,1)S(1)}, u32[]{:S(2)}, u32[]{:S(2)}) collective-permute-start(bf16[4,256,128]{2,1,0:T(8,128)(2,1)S(1)} %copy-done.4), channel_id=1, source_target_pairs={{0,8},{1,9},{2,10},{3,11},{4,0},{5,1},{6,2},{7,3},{8,12},{9,13},{1... | collective-permute-start | bytes 786440 | tf_op jit(solution)/shard_map/ppermute | solution.py:372
  18.7 2.2 %rows_for.7 = (bf16[3,4,16,2,4,256]{5,4,3,2,1,0:T(4,128)(2,1)}, bf16[1,4,16,2,4,256]{5,4,3,2,1,0:T(4,128)(2,1)}) custom-call(bf16[4,16,2,4,4096]{4,3,2,1,0:T(4,128)(2,1)} %bitcast.5), custom_call_target="tpu_custom_call" | custom-call | tf_op jit(solution)/shard_map/rows_for/pallas_call | solution.py:242
  20.9 0.5 collective-permute-start.11
  21.4 2.1 %rows_for.6 = (bf16[3,4,16,2,4,256]{5,4,3,2,1,0:T(4,128)(2,1)}, bf16[1,4,16,2,4,256]{5,4,3,2,1,0:T(4,128)(2,1)}) custom-call(bf16[4,16,2,4,4096]{4,3,2,1,0:T(4,128)(2,1)} %bitcast.6), custom_call_target="tpu_custom_call" | custom-call | tf_op jit(solution)/shard_map/rows_for/pallas_call | solution.py:242
  23.5 0.0 copy-start.9
  23.5 1.2 %collective-permute-start.10 = (bf16[1,4,16,2,4,256]{5,4,3,2,1,0:T(4,128)(2,1)}, bf16[1,4,16,2,4,256]{5,4,3,2,1,0:T(4,128)(2,1)S(1)}, u32[]{:S(2)}, u32[]{:S(2)}) collective-permute-start(bf16[1,4,16,2,4,256]{5,4,3,2,1,0:T(4,128)(2,1)} %get-tuple-element.25), channel_id=1, source_target_pairs={{0,2},{1,3},{2,0},{3,1},{4,6},{5,7},{6,4},{7,5},{8,10},{9,11},{10,... | collective-permute-start | bytes 786440 | tf_op jit(solution)/shard_map/ppermute | solution.py:362
  24.7 2.1 %rows_for.5 = (bf16[3,4,16,2,4,256]{5,4,3,2,1,0:T(4,128)(2,1)}, bf16[1,4,16,2,4,256]{5,4,3,2,1,0:T(4,128)(2,1)}) custom-call(bf16[4,16,2,4,4096]{4,3,2,1,0:T(4,128)(2,1)} %bitcast.7), custom_call_target="tpu_custom_call" | custom-call | tf_op jit(solution)/shard_map/rows_for/pallas_call | solution.py:242
  26.8 0.4 collective-permute-start.9
  27.2 0.0 collective-permute-done.6.refs_9_
  27.2 1.2 %collective-permute-start.2 = (bf16[3,4,16,2,4,256]{5,4,3,2,1,0:T(4,128)(2,1)}, bf16[3,4,16,2,4,256]{5,4,3,2,1,0:T(4,128)(2,1)}, u32[]{:S(2)}, u32[]{:S(2)}) collective-permute-start(bf16[3,4,16,2,4,256]{5,4,3,2,1,0:T(4,128)(2,1)} %get-tuple-element.19), channel_id=1, source_target_pairs={{0,3},{1,2},{2,1},{3,0},{4,7},{5,6},{6,5},{7,4},{8,11},{9,10},{10,... | collective-permute-start | bytes 2359304 | tf_op jit(solution)/shard_map/ppermute | solution.py:361
  28.4 0.1 collective-permute-done.3.refs_5_
  28.5 1.5 %collective-permute-start.1 = (bf16[3,4,16,2,4,256]{5,4,3,2,1,0:T(4,128)(2,1)}, bf16[3,4,16,2,4,256]{5,4,3,2,1,0:T(4,128)(2,1)}, u32[]{:S(2)}, u32[]{:S(2)}) collective-permute-start(bf16[3,4,16,2,4,256]{5,4,3,2,1,0:T(4,128)(2,1)} %get-tuple-element.18), channel_id=1, source_target_pairs={{0,2},{1,3},{2,0},{3,1},{4,6},{5,7},{6,4},{7,5},{8,10},{9,11},{10,... | collective-permute-start | bytes 2359304 | tf_op jit(solution)/shard_map/ppermute | solution.py:361
  30.1 0.0 collective-permute-done.11.refs_3_
  30.1 0.0 collective-permute-start
  30.1 5.5 %collective-permute-done.10.refs_2_ = bf16[1,4,16,2,4,256]{5,4,3,2,1,0:T(4,128)(2,1)S(1)} collective-permute-done((bf16[1,4,16,2,4,256]{5,4,3,2,1,0:T(4,128)(2,1)}, bf16[1,4,16,2,4,256]{5,4,3,2,1,0:T(4,128)(2,1)S(1)}, u32[]{:S(2)}, u32[]{:S(2)}) %collective-permute-start.10) | collective-permute-done | bytes 262176 | tf_op jit(solution)/shard_map/ppermute | solution.py:362
  35.5 0.3 collective-permute-start.7
  35.8 0.0 collective-permute-done.9.refs_1_
  35.9 0.7 copy-done.6
  36.6 0.5 collective-permute-start.4
  37.0 7.7 %collective-permute-done.7.refs_10_ = bf16[4,256,128]{2,1,0:T(8,128)(2,1)S(1)} collective-permute-done((bf16[4,256,128]{2,1,0:T(8,128)(2,1)S(1)}, bf16[4,256,128]{2,1,0:T(8,128)(2,1)S(1)}, u32[]{:S(2)}, u32[]{:S(2)}) %collective-permute-start.7) | collective-permute-done | bytes 262176 | tf_op jit(solution)/shard_map/ppermute | solution.py:372
  44.7 1.2 %collective-permute-start.8 = (bf16[4,256,128]{2,1,0:T(8,128)(2,1)S(1)}, bf16[4,256,128]{2,1,0:T(8,128)(2,1)S(1)}, u32[]{:S(2)}, u32[]{:S(2)}) collective-permute-start(bf16[4,256,128]{2,1,0:T(8,128)(2,1)S(1)} %collective-permute-done.7.refs_10_), channel_id=1, source_target_pairs={{0,8},{1,9},{2,10},{3,11},{4,0},{5,1},{6,2},{7,3},{8,12},{9,13},{1... | collective-permute-start | bytes 786440 | tf_op jit(solution)/shard_map/ppermute | solution.py:372
  45.9 4.4 %collective-permute-done.4.refs_6_ = bf16[4,256,128]{2,1,0:T(8,128)(2,1)S(1)} collective-permute-done((bf16[4,256,128]{2,1,0:T(8,128)(2,1)S(1)}, bf16[4,256,128]{2,1,0:T(8,128)(2,1)S(1)}, u32[]{:S(2)}, u32[]{:S(2)}) %collective-permute-start.4) | collective-permute-done | bytes 262176 | tf_op jit(solution)/shard_map/ppermute | solution.py:372
  50.3 1.2 %collective-permute-start.5 = (bf16[4,256,128]{2,1,0:T(8,128)(2,1)S(1)}, bf16[4,256,128]{2,1,0:T(8,128)(2,1)S(1)}, u32[]{:S(2)}, u32[]{:S(2)}) collective-permute-start(bf16[4,256,128]{2,1,0:T(8,128)(2,1)S(1)} %collective-permute-done.4.refs_6_), channel_id=1, source_target_pairs={{0,8},{1,9},{2,10},{3,11},{4,0},{5,1},{6,2},{7,3},{8,12},{9,13},{1... | collective-permute-start | bytes 786440 | tf_op jit(solution)/shard_map/ppermute | solution.py:372
  51.5 2.1 %rows_for.4 = (bf16[3,4,16,2,4,256]{5,4,3,2,1,0:T(4,128)(2,1)}, bf16[1,4,16,2,4,256]{5,4,3,2,1,0:T(4,128)(2,1)}) custom-call(bf16[4,16,2,4,4096]{4,3,2,1,0:T(4,128)(2,1)} %bitcast.8), custom_call_target="tpu_custom_call" | custom-call | tf_op jit(solution)/shard_map/rows_for/pallas_call | solution.py:242
  53.6 2.3 %collective-permute-done.8.refs_11_ = bf16[4,256,128]{2,1,0:T(8,128)(2,1)S(1)} collective-permute-done((bf16[4,256,128]{2,1,0:T(8,128)(2,1)S(1)}, bf16[4,256,128]{2,1,0:T(8,128)(2,1)S(1)}, u32[]{:S(2)}, u32[]{:S(2)}) %collective-permute-start.8) | collective-permute-done | bytes 262176 | tf_op jit(solution)/shard_map/ppermute | solution.py:372
  55.9 4.6 %collective-permute-done.5.refs_7_ = bf16[4,256,128]{2,1,0:T(8,128)(2,1)S(1)} collective-permute-done((bf16[4,256,128]{2,1,0:T(8,128)(2,1)S(1)}, bf16[4,256,128]{2,1,0:T(8,128)(2,1)S(1)}, u32[]{:S(2)}, u32[]{:S(2)}) %collective-permute-start.5) | collective-permute-done | bytes 262176 | tf_op jit(solution)/shard_map/ppermute | solution.py:372
  60.5 0.0 copy-done
  60.5 0.0 copy-done.1
  60.6 0.0 copy-done.3
  60.6 0.0 copy-start.7
  60.6 0.9 %copy-done.7 = bf16[1,4,16,2,4,256]{5,4,3,2,1,0:T(4,128)(2,1)S(1)} copy-done((bf16[1,4,16,2,4,256]{5,4,3,2,1,0:T(4,128)(2,1)S(1)}, bf16[1,4,16,2,4,256]{5,4,3,2,1,0:T(4,128)(2,1)}, u32[]{:S(2)}) %copy-start.7) | copy-done | bytes 262168
  61.5 0.9 %copy-done.8 = bf16[1,4,16,2,4,256]{5,4,3,2,1,0:T(4,128)(2,1)S(1)} copy-done((bf16[1,4,16,2,4,256]{5,4,3,2,1,0:T(4,128)(2,1)S(1)}, bf16[1,4,16,2,4,256]{5,4,3,2,1,0:T(4,128)(2,1)}, u32[]{:S(2)}) %copy-start.8) | copy-done | bytes 262168
  62.5 0.9 %predict.3 = bf16[4,16,64]{2,1,0:T(8,128)(2,1)S(1)} custom-call(bf16[1,4,16,2,4,256]{5,4,3,2,1,0:T(4,128)(2,1)S(1)} %copy-done.8, bf16[1,4,16,2,4,256]{5,4,3,2,1,0:T(4,128)(2,1)S(1)} %copy-done.7, bf16[1,4,16,2,4,256]{5,4,3,2,1,0:T(4,128)(2,1)S(1)} %collective-permute-done.10.refs_2_, bf16[1,4,16,2,4,256]{5,4,3,2,1,0:T(4,128)(2,1)S(1)} %collective-permute-done.11.refs_3_, ...), custom_call_target="tpu_custom_call" | custom-call | tf_op jit(solution)/shard_map/predict/pallas_call | solution.py:319
  63.4 0.0 collective-permute-done.2.refs_3_
  63.4 5.9 %collective-permute-done.1.refs_2_ = bf16[3,4,16,2,4,256]{5,4,3,2,1,0:T(4,128)(2,1)} collective-permute-done((bf16[3,4,16,2,4,256]{5,4,3,2,1,0:T(4,128)(2,1)}, bf16[3,4,16,2,4,256]{5,4,3,2,1,0:T(4,128)(2,1)}, u32[]{:S(2)}, u32[]{:S(2)}) %collective-permute-start.1) | collective-permute-done | bytes 786464 | tf_op jit(solution)/shard_map/ppermute | solution.py:361
  69.3 0.0 collective-permute-done.refs_1_
  69.3 1.1 %copy-done.5 = bf16[3,4,16,2,4,256]{5,4,3,2,1,0:T(4,128)(2,1)S(1)} copy-done((bf16[3,4,16,2,4,256]{5,4,3,2,1,0:T(4,128)(2,1)S(1)}, bf16[3,4,16,2,4,256]{5,4,3,2,1,0:T(4,128)(2,1)}, u32[]{:S(2)}) %copy-start.5) | copy-done | bytes 786456
  70.4 4.0 %predict.2 = bf16[12,16,64]{2,1,0:T(8,128)(2,1)S(1)} custom-call(bf16[3,4,16,2,4,256]{5,4,3,2,1,0:T(4,128)(2,1)S(1)} %copy-done.5, bf16[3,4,16,2,4,256]{5,4,3,2,1,0:T(4,128)(2,1)} %collective-permute-done.refs_1_, bf16[3,4,16,2,4,256]{5,4,3,2,1,0:T(4,128)(2,1)} %collective-permute-done.1.refs_2_, ...), custom_call_target="tpu_custom_call" | custom-call | tf_op jit(solution)/shard_map/predict/pallas_call | solution.py:319
  74.4 0.1 reshape.19
  74.6 9.2 %all_to_all.5 = bf16[16,2,512]{2,1,0:T(2,128)(2,1)S(1)} all-to-all(bf16[16,2,512]{2,1,0:T(2,128)(2,1)S(1)} %reshape.19), channel_id=1, replica_groups=mesh['parts'=2,'rows'=16] {'rows'}, dimensions={0} | all-to-all | bytes 65536 | tf_op jit(solution)/shard_map/all_to_all | solution.py:383
  83.8 0.1 reshape.20
  83.9 0.8 convolution_convert_fusion
  (10 shorter events, 0.0 us)
Async XLA Ops:
  7.2 10.0 %copy-start.4 = (bf16[4,256,128]{2,1,0:T(8,128)(2,1)S(1)}, bf16[4,256,128]{2,1,0:T(8,128)(2,1)}, u32[]{:S(2)}) copy-start(bf16[4,256,128]{2,1,0:T(8,128)(2,1)} %get-tuple-element.20.refs_4_) | copy-start | bytes 786436
  13.0 14.2 %collective-permute-start.6 = (bf16[4,256,128]{2,1,0:T(8,128)(2,1)}, bf16[4,256,128]{2,1,0:T(8,128)(2,1)S(1)}, u32[]{:S(2)}, u32[]{:S(2)}) collective-permute-start(bf16[4,256,128]{2,1,0:T(8,128)(2,1)} %spectra.3.refs_8_), channel_id=1, source_target_pairs={{0,8},{1,9},{2,10},{3,11},{4,0},{5,1},{6,2},{7,3},{8,12},{9,13},{1... | collective-permute-start | bytes 786440 | tf_op jit(solution)/shard_map/ppermute | solution.py:372
  17.1 11.4 %collective-permute-start.3 = (bf16[4,256,128]{2,1,0:T(8,128)(2,1)S(1)}, bf16[4,256,128]{2,1,0:T(8,128)(2,1)S(1)}, u32[]{:S(2)}, u32[]{:S(2)}) collective-permute-start(bf16[4,256,128]{2,1,0:T(8,128)(2,1)S(1)} %copy-done.4), channel_id=1, source_target_pairs={{0,8},{1,9},{2,10},{3,11},{4,0},{5,1},{6,2},{7,3},{8,12},{9,13},{1... | collective-permute-start | bytes 786440 | tf_op jit(solution)/shard_map/ppermute | solution.py:372
  18.7 41.8 %copy-start = (bf16[4,256,128]{2,1,0:T(8,128)(2,1)S(1)}, bf16[4,256,128]{2,1,0:T(8,128)(2,1)}, u32[]{:S(2)}) copy-start(bf16[4,256,128]{2,1,0:T(8,128)(2,1)} %spectra.3.refs_8_) | copy-start | bytes 786436
  18.7 41.8 %copy-start.1 = (bf16[4,256,64]{2,1,0:T(8,128)(2,1)S(1)}, bf16[4,256,64]{2,1,0:T(8,128)(2,1)}, u32[]{:S(2)}) copy-start(bf16[4,256,64]{2,1,0:T(8,128)(2,1)} %constant.19.clone.refs_14_) | copy-start | bytes 393220
  18.7 41.8 %copy-start.2 = (bf16[4,256,64]{2,1,0:T(8,128)(2,1)S(1)}, bf16[4,256,64]{2,1,0:T(8,128)(2,1)}, u32[]{:S(2)}) copy-start(bf16[4,256,64]{2,1,0:T(8,128)(2,1)} %constant.18.clone.refs_13_) | copy-start | bytes 393220
  18.7 41.8 %copy-start.3 = (f32[256,256]{1,0:T(8,128)S(1)}, f32[256,256]{1,0:T(8,128)}, u32[]{:S(2)}) copy-start(f32[256,256]{1,0:T(8,128)} %constant.17.clone.refs_12_) | copy-start | bytes 786436
  20.9 9.1 %collective-permute-start.11 = (bf16[1,4,16,2,4,256]{5,4,3,2,1,0:T(4,128)(2,1)}, bf16[1,4,16,2,4,256]{5,4,3,2,1,0:T(4,128)(2,1)S(1)}, u32[]{:S(2)}, u32[]{:S(2)}) collective-permute-start(bf16[1,4,16,2,4,256]{5,4,3,2,1,0:T(4,128)(2,1)} %get-tuple-element.26), channel_id=1, source_target_pairs={{0,3},{1,2},{2,1},{3,0},{4,7},{5,6},{6,5},{7,4},{8,11},{9,10},{10,... | collective-permute-start | bytes 786440 | tf_op jit(solution)/shard_map/ppermute | solution.py:362
  23.5 60.4 %copy-start.9 = (bf16[256,64]{1,0:T(8,128)(2,1)S(1)}, bf16[256,64]{1,0:T(8,128)(2,1)}, u32[]{:S(2)}) copy-start(bf16[256,64]{1,0:T(8,128)(2,1)} %constant.20.clone) | copy-start | bytes 98308
  23.5 12.0 %collective-permute-start.10 = (bf16[1,4,16,2,4,256]{5,4,3,2,1,0:T(4,128)(2,1)}, bf16[1,4,16,2,4,256]{5,4,3,2,1,0:T(4,128)(2,1)S(1)}, u32[]{:S(2)}, u32[]{:S(2)}) collective-permute-start(bf16[1,4,16,2,4,256]{5,4,3,2,1,0:T(4,128)(2,1)} %get-tuple-element.25), channel_id=1, source_target_pairs={{0,2},{1,3},{2,0},{3,1},{4,6},{5,7},{6,4},{7,5},{8,10},{9,11},{10,... | collective-permute-start | bytes 786440 | tf_op jit(solution)/shard_map/ppermute | solution.py:362
  26.8 9.0 %collective-permute-start.9 = (bf16[1,4,16,2,4,256]{5,4,3,2,1,0:T(4,128)(2,1)}, bf16[1,4,16,2,4,256]{5,4,3,2,1,0:T(4,128)(2,1)S(1)}, u32[]{:S(2)}, u32[]{:S(2)}) collective-permute-start(bf16[1,4,16,2,4,256]{5,4,3,2,1,0:T(4,128)(2,1)} %get-tuple-element.24), channel_id=1, source_target_pairs={{0,1},{1,0},{2,3},{3,2},{4,5},{5,4},{6,7},{7,6},{8,9},{9,8},{10,11... | collective-permute-start | bytes 786440 | tf_op jit(solution)/shard_map/ppermute | solution.py:362
  27.2 36.2 %collective-permute-start.2 = (bf16[3,4,16,2,4,256]{5,4,3,2,1,0:T(4,128)(2,1)}, bf16[3,4,16,2,4,256]{5,4,3,2,1,0:T(4,128)(2,1)}, u32[]{:S(2)}, u32[]{:S(2)}) collective-permute-start(bf16[3,4,16,2,4,256]{5,4,3,2,1,0:T(4,128)(2,1)} %get-tuple-element.19), channel_id=1, source_target_pairs={{0,3},{1,2},{2,1},{3,0},{4,7},{5,6},{6,5},{7,4},{8,11},{9,10},{10,... | collective-permute-start | bytes 2359304 | tf_op jit(solution)/shard_map/ppermute | solution.py:361
  28.5 40.7 %collective-permute-start.1 = (bf16[3,4,16,2,4,256]{5,4,3,2,1,0:T(4,128)(2,1)}, bf16[3,4,16,2,4,256]{5,4,3,2,1,0:T(4,128)(2,1)}, u32[]{:S(2)}, u32[]{:S(2)}) collective-permute-start(bf16[3,4,16,2,4,256]{5,4,3,2,1,0:T(4,128)(2,1)} %get-tuple-element.18), channel_id=1, source_target_pairs={{0,2},{1,3},{2,0},{3,1},{4,6},{5,7},{6,4},{7,5},{8,10},{9,11},{10,... | collective-permute-start | bytes 2359304 | tf_op jit(solution)/shard_map/ppermute | solution.py:361
  30.1 39.2 %collective-permute-start = (bf16[3,4,16,2,4,256]{5,4,3,2,1,0:T(4,128)(2,1)}, bf16[3,4,16,2,4,256]{5,4,3,2,1,0:T(4,128)(2,1)}, u32[]{:S(2)}, u32[]{:S(2)}) collective-permute-start(bf16[3,4,16,2,4,256]{5,4,3,2,1,0:T(4,128)(2,1)} %get-tuple-element.17), channel_id=1, source_target_pairs={{0,1},{1,0},{2,3},{3,2},{4,5},{5,4},{6,7},{7,6},{8,9},{9,8},{10,11... | collective-permute-start | bytes 2359304 | tf_op jit(solution)/shard_map/ppermute | solution.py:361
  35.5 9.2 %collective-permute-start.7 = (bf16[4,256,128]{2,1,0:T(8,128)(2,1)S(1)}, bf16[4,256,128]{2,1,0:T(8,128)(2,1)S(1)}, u32[]{:S(2)}, u32[]{:S(2)}) collective-permute-start(bf16[4,256,128]{2,1,0:T(8,128)(2,1)S(1)} %collective-permute-done.6.refs_9_), channel_id=1, source_target_pairs={{0,8},{1,9},{2,10},{3,11},{4,0},{5,1},{6,2},{7,3},{8,12},{9,13},{1... | collective-permute-start | bytes 786440 | tf_op jit(solution)/shard_map/ppermute | solution.py:372
  35.9 0.7 copy-start.6
  36.6 13.7 %collective-permute-start.4 = (bf16[4,256,128]{2,1,0:T(8,128)(2,1)S(1)}, bf16[4,256,128]{2,1,0:T(8,128)(2,1)S(1)}, u32[]{:S(2)}, u32[]{:S(2)}) collective-permute-start(bf16[4,256,128]{2,1,0:T(8,128)(2,1)S(1)} %collective-permute-done.3.refs_5_), channel_id=1, source_target_pairs={{0,8},{1,9},{2,10},{3,11},{4,0},{5,1},{6,2},{7,3},{8,12},{9,13},{1... | collective-permute-start | bytes 786440 | tf_op jit(solution)/shard_map/ppermute | solution.py:372
  44.7 11.2 %collective-permute-start.8 = (bf16[4,256,128]{2,1,0:T(8,128)(2,1)S(1)}, bf16[4,256,128]{2,1,0:T(8,128)(2,1)S(1)}, u32[]{:S(2)}, u32[]{:S(2)}) collective-permute-start(bf16[4,256,128]{2,1,0:T(8,128)(2,1)S(1)} %collective-permute-done.7.refs_10_), channel_id=1, source_target_pairs={{0,8},{1,9},{2,10},{3,11},{4,0},{5,1},{6,2},{7,3},{8,12},{9,13},{1... | collective-permute-start | bytes 786440 | tf_op jit(solution)/shard_map/ppermute | solution.py:372
  50.3 10.2 %collective-permute-start.5 = (bf16[4,256,128]{2,1,0:T(8,128)(2,1)S(1)}, bf16[4,256,128]{2,1,0:T(8,128)(2,1)S(1)}, u32[]{:S(2)}, u32[]{:S(2)}) collective-permute-start(bf16[4,256,128]{2,1,0:T(8,128)(2,1)S(1)} %collective-permute-done.4.refs_6_), channel_id=1, source_target_pairs={{0,8},{1,9},{2,10},{3,11},{4,0},{5,1},{6,2},{7,3},{8,12},{9,13},{1... | collective-permute-start | bytes 786440 | tf_op jit(solution)/shard_map/ppermute | solution.py:372
  60.6 1.0 %copy-start.7 = (bf16[1,4,16,2,4,256]{5,4,3,2,1,0:T(4,128)(2,1)S(1)}, bf16[1,4,16,2,4,256]{5,4,3,2,1,0:T(4,128)(2,1)}, u32[]{:S(2)}) copy-start(bf16[1,4,16,2,4,256]{5,4,3,2,1,0:T(4,128)(2,1)} %copy-done.6) | copy-start | bytes 786436
  61.5 0.9 %copy-start.8 = (bf16[1,4,16,2,4,256]{5,4,3,2,1,0:T(4,128)(2,1)S(1)}, bf16[1,4,16,2,4,256]{5,4,3,2,1,0:T(4,128)(2,1)}, u32[]{:S(2)}) copy-start(bf16[1,4,16,2,4,256]{5,4,3,2,1,0:T(4,128)(2,1)} %get-tuple-element.23.refs_0_) | copy-start | bytes 786436
  69.3 1.1 %copy-start.5 = (bf16[3,4,16,2,4,256]{5,4,3,2,1,0:T(4,128)(2,1)S(1)}, bf16[3,4,16,2,4,256]{5,4,3,2,1,0:T(4,128)(2,1)}, u32[]{:S(2)}) copy-start(bf16[3,4,16,2,4,256]{5,4,3,2,1,0:T(4,128)(2,1)} %get-tuple-element.16.refs_0_) | copy-start | bytes 2359300

commit v2 on v1

--- a/solution.py
+++ b/solution.py
@@ -77,24 +77,31 @@
     return shot // per * per + (band + shot % per) % per
 
 
-def spectra_kernel(bands, bins, taps, first, *refs):
+def spectra_kernel(bands, bins, taps, part, outs, *refs):
     trace, bin_of, main_hbm = refs[:3]
+    first = part == 0
+    main, binned, sem = refs[-3:]
     if first:
-        filt, resp, tail, out, select, last, main, binned, sem = refs[3:]
+        filt, resp, tail = refs[3:6]
+        out_refs, (select, last) = refs[6 : 6 + outs], refs[6 + outs : 8 + outs]
     else:
-        select, last, out, main, binned, sem = refs[3:]
+        select, last = refs[3:5]
+        out_refs = refs[5 : 5 + outs]
+    places = [(ref, i) for ref in out_refs for i in range(ref.shape[0])]
     step = pl.program_id(0)
     width = main.shape[1] // 2
-    shots, count = bin_of.shape[1:]
+    count = bin_of.shape[1]
+    shots = binned.shape[0]
     group, _, length = trace.shape
     copy = pltpu.make_async_copy(main_hbm, main, sem)
 
     @pl.when(step == 0)
     def _():
         copy.start()
-        column = jnp.transpose(bin_of[0].astype(F32), (1, 0))
+        column = jnp.transpose(bin_of[...].astype(F32), (1, 0))
         for shot in range(shots):
-            value = jnp.broadcast_to(column[:, shot : shot + 1], (count, width))
+            at = part * shots + shot
+            value = jnp.broadcast_to(column[:, at : at + 1], (count, width))
             binned[shot] = value.astype(BF16)
         if first:
             prepare(bins, taps, width, filt, resp, tail, select, last)
@@ -136,15 +143,16 @@
                 part = value[i * count : (i + 1) * count]
                 moved.append(part if j == 0 else pltpu.roll(part, j * chunk, 1))
             for band in range(bands):
-                result = moved[0] if phase == 0 else out[band].astype(F32)
+                out, at = places[band]
+                result = moved[0] if phase == 0 else out[at].astype(F32)
                 for i in range(group):
                     j = phase * group + i
                     if j:
                         result = jnp.where(place == (band + j) % per, moved[i], result)
-                out[band] = result.astype(BF16)
-
-
-def spectra_of(traces, offset_bin, filters, freqs):
+                out[at] = result.astype(BF16)
+
+
+def spectra_of(traces, offset_bin, filters, freqs, cuts):
     shots, count, length = traces.shape
     bins, taps = filters.shape
     bands = freqs // BAND
@@ -152,31 +160,31 @@
     group = 2
     main, resp, tail = transform_tables(freqs, length, taps)
     per = width // (2 * BAND)
-    out_shape = jax.ShapeDtypeStruct((bands, count, width), BF16)
     made = [
         jax.ShapeDtypeStruct((width, 2 * width), BF16),
         jax.ShapeDtypeStruct((taps * bins, width), BF16),
     ]
     whole = lambda x: pl.BlockSpec(x.shape, lambda s: (0,) * len(x.shape))
-    binned = offset_bin.reshape(shots // per, per, count)
     results, extra = [], None
     for part in range(shots // per):
         first = part == 0
         more = [filters, resp, tail] if first else extra
+        cut = cuts[part]
+        shapes = [jax.ShapeDtypeStruct((b - a, count, width), BF16) for a, b in cut]
         outs = pl.pallas_call(
-            functools.partial(spectra_kernel, bands, bins, taps, first),
+            functools.partial(spectra_kernel, bands, bins, taps, part, len(cut)),
             grid=(per // group,),
             in_specs=[
                 pl.BlockSpec(
                     (group, count, length),
                     functools.partial(lambda p, s: (p + s, 0, 0), part * per // group),
                 ),
-                pl.BlockSpec((1, per, count), functools.partial(lambda p, s: (p, 0, 0), part)),
+                whole(offset_bin),
                 pl.BlockSpec(memory_space=pltpu.HBM),
             ]
             + [whole(x) for x in more],
-            out_specs=[whole(out_shape)] + ([whole(x) for x in made] if first else []),
-            out_shape=[out_shape] + (made if first else []),
+            out_specs=[whole(x) for x in shapes] + ([whole(x) for x in made] if first else []),
+            out_shape=shapes + (made if first else []),
             scratch_shapes=[
                 pltpu.VMEM(main.shape, BF16),
                 pltpu.VMEM((per, count, width), BF16),
@@ -189,10 +197,10 @@
                 transcendentals=0,
             ),
             name="spectra",
-        )(traces, binned, main, *more)
+        )(traces, offset_bin, main, *more)
         if first:
-            extra = outs[1:]
-        results.append(outs[0])
+            extra = outs[len(cut) :]
+        results.append(outs[: len(cut)])
     return results
 
 
@@ -256,21 +264,42 @@
     )(source)
 
 
-def predict_kernel(members, slots, parts, *refs):
-    rows_in, spectra_in = refs[:members], refs[members : members + slots * parts]
-    mask_ref, fold_a, fold_b, out = refs[members + slots * parts :]
-    columns = []
+def merge_kernel(*refs):
+    rows_in, out = refs[:-1], refs[-1]
+    block = rows_in[0].shape[-1]
     for i in range(rows_in[0].shape[1]):
         part = jnp.concatenate([r[0, i] for r in rows_in], axis=2)
-        columns.append(part.reshape(-1, part.shape[-1]))
-    matrix = columns[0] if len(columns) == 1 else jnp.concatenate(columns, axis=1)
+        out[0, :, i * block : (i + 1) * block] = part.reshape(-1, block)
+
+
+def merge(row_parts):
+    number, pieces, _, parts, rows, block = row_parts[0].shape
+    shape = (BAND * parts * rows * len(row_parts), pieces * block)
+    return pl.pallas_call(
+        merge_kernel,
+        grid=(number,),
+        in_specs=[
+            pl.BlockSpec((1, pieces, BAND, parts, rows, block), lambda q: (q, 0, 0, 0, 0, 0))
+        ]
+        * len(row_parts),
+        out_specs=pl.BlockSpec((1,) + shape, lambda q: (q, 0, 0)),
+        out_shape=jax.ShapeDtypeStruct((number,) + shape, row_parts[0].dtype),
+        compiler_params=pltpu.CompilerParams(vmem_limit_bytes=40 << 20),
+        name="merge",
+    )(*row_parts)
+
+
+def predict_kernel(parts, slots, before, matrix, *refs):
+    spectra_in = refs[: slots * parts]
+    mask_ref, fold_a, fold_b = refs[slots * parts : slots * parts + 3]
+    out = refs[-1]
     spectra = [
         jnp.concatenate([spectra_in[p * slots + i][0] for p in range(parts)], axis=1)
         for i in range(slots)
     ]
     spectra = spectra[0] if slots == 1 else jnp.concatenate(spectra, axis=0)
-    rows = rows_in[0].shape[4] * members
-    total = dot(matrix, spectra)
+    dests, rows, _ = out.shape
+    total = dot(matrix[0], spectra)
     total = total.reshape(BAND, 2, rows, -1)
     acc = None
     for c, fold in enumerate((fold_a, fold_b)):
@@ -279,56 +308,61 @@
         for piece in split(value, 2):
             term = dot(piece, fold[0])
             acc = term if acc is None else acc + term
-    dests = out.shape[0]
     acc = acc.reshape(dests, BAND // dests, rows, -1)
     value = acc[:, 0]
     for i in range(1, BAND // dests):
         value = value + acc[:, i]
+    if before:
+        value = value + refs[-2][...].astype(F32)
     out[...] = value.astype(out.dtype)
 
 
-def predict(row_parts, spectra_parts, share, first):
-    number, pieces, _, _, rows, depth = row_parts[0].shape
+def predict(matrix, spectra_parts, share, shots, first, part, before=None):
+    number, wide, depth = matrix.shape
     parts, slots = len(spectra_parts), len(spectra_parts[0])
-    bands, block, width = spectra_parts[0][0].shape
+    _, block, width = spectra_parts[0][0].shape
     cols = width * parts
-    shots = cols // (2 * BAND)
     per = width // (2 * BAND)
-    members = len(row_parts)
-    all_rows = members * rows
+    all_rows = wide // (2 * BAND)
     lanes = share * 2 * shots
     index = np.arange(cols)
     col_c, col_f = index // BAND % 2, index % BAND
     row_f = np.arange(BAND * all_rows) // all_rows
     mask = (row_f[:, None] == col_f[None, :]).astype(np.float32)
-    fold_a = np.zeros((bands, cols, share, 2, shots), np.float32)
-    fold_b = np.zeros((bands, cols, share, 2, shots), np.float32)
-    for band in range(bands):
+    fold_a = np.zeros((number, cols, share, 2, shots), np.float32)
+    fold_b = np.zeros((number, cols, share, 2, shots), np.float32)
+    for band in range(number):
         shot_at = np.zeros(shots, np.int64)
         for shot in range(shots):
-            shot_at[chunk_of(shot, band, per)] = shot
-        col_s = shot_at[index // (2 * BAND)]
+            shot_at[chunk_of(shot, first + band, per)] = shot
+        col_s = shot_at[part * per + index // (2 * BAND)]
         fold_a[band, index, col_f % share, col_c, col_s] = 1.0
         fold_b[band, index, col_f % share, 1 - col_c, col_s] = np.where(col_c == 1, -1.0, 1.0)
-    consts = (
+    consts = [
         jnp.asarray(mask, F32),
-        jnp.asarray(fold_a.reshape(bands, cols, lanes), BF16),
-        jnp.asarray(fold_b.reshape(bands, cols, lanes), BF16),
-    )
+        jnp.asarray(fold_a.reshape(number, cols, lanes), BF16),
+        jnp.asarray(fold_b.reshape(number, cols, lanes), BF16),
+    ]
     dests = BAND // share
+    out_spec = pl.BlockSpec((dests, all_rows, lanes), lambda q: (q, 0, 0))
+    flat = [x for spectra in spectra_parts for x in spectra]
+    starts = [first * (x.shape[0] > number) for x in flat]
     return pl.pallas_call(
-        functools.partial(predict_kernel, members, slots, parts),
+        functools.partial(predict_kernel, parts, slots, before is not None),
         grid=(number,),
-        in_specs=[pl.BlockSpec((1, pieces, BAND, 2, rows, depth), lambda q: (q, 0, 0, 0, 0, 0))]
-        * members
-        + [pl.BlockSpec((1, block, width), lambda q: (first + q, 0, 0))] * (slots * parts)
+        in_specs=[pl.BlockSpec((1, wide, depth), lambda q: (q, 0, 0))]
+        + [
+            pl.BlockSpec((1, block, width), functools.partial(lambda a, q: (a + q, 0, 0), a))
+            for a in starts
+        ]
         + [pl.BlockSpec(mask.shape, lambda q: (0, 0))]
-        + [pl.BlockSpec((1, cols, lanes), lambda q: (first + q, 0, 0))] * 2,
-        out_specs=pl.BlockSpec((dests, all_rows, lanes), lambda q: (q, 0, 0)),
+        + [pl.BlockSpec((1, cols, lanes), lambda q: (q, 0, 0))] * 2
+        + ([] if before is None else [out_spec]),
+        out_specs=out_spec,
         out_shape=jax.ShapeDtypeStruct((number * dests, all_rows, lanes), BF16),
-        compiler_params=pltpu.CompilerParams(vmem_limit_bytes=48 << 20),
+        compiler_params=pltpu.CompilerParams(vmem_limit_bytes=40 << 20),
         name="predict",
-    )(*row_parts, *[x for part in spectra_parts for x in part], *consts)
+    )(matrix, *flat, *consts, *([] if before is None else [before]))
 
 
 def ring_of(length):
@@ -365,20 +399,28 @@
     for m in range(members - 1, -1, -1):
         exchange(m)
 
-    spectra_parts = [[x] for x in spectra_of(traces, offset_bin, filters, freqs)]
+    per = 2 * freqs // (2 * BAND)
+    quads = shot_count // per
+    cuts = [[(0, bands)]] * (quads - 1) + [[(0, head), (head, bands)] if bands > head else [(0, bands)]]
+    pieces = [(p, [x]) for p, cut in enumerate(spectra_of(traces, offset_bin, filters, freqs, cuts)) for x in cut]
     step = [(i, after[i // members] * members + i % members) for i in range(devices)]
     for _ in range(lines - 1):
-        for part in spectra_parts:
-            part.append(lax.ppermute(part[-1], "rows", step))
+        for _, piece in pieces:
+            piece.append(lax.ppermute(piece[-1], "rows", step))
     if block % 128:
-        spectra_parts = [[jnp.concatenate(part, axis=1)] for part in spectra_parts]
+        pieces = [(p, [jnp.concatenate(piece, axis=1)]) for p, piece in pieces]
         joined = lambda x: jnp.concatenate([x[:, i : i + 1] for i in range(lines)], axis=5)
         first_parts = [joined(x) for x in first_parts]
         rest_parts = [joined(x) for x in rest_parts]
 
     share = freqs // devices
-    early = predict(first_parts, spectra_parts, share, 0)
-    late = predict(rest_parts, spectra_parts, share, head)
+    first_matrix = merge(first_parts)
+    rest_matrix = merge(rest_parts)
+    whole_pieces = [piece for _, piece in pieces[: quads - 1]]
+    head_piece, rest_piece = pieces[quads - 1][1], pieces[-1][1]
+    early = predict(first_matrix, whole_pieces, share, shot_count, 0, 0)
+    early = predict(first_matrix, [head_piece], share, shot_count, 0, quads - 1, early)
+    late = predict(rest_matrix, whole_pieces + [rest_piece], share, shot_count, head, 0)
     partial_value = jnp.concatenate([early, late], axis=0)
     received = lax.all_to_all(partial_value, "rows", split_axis=0, concat_axis=0, tiled=True)
     choose = np.zeros((lines, members, members, row_count, lines, members, row_count))

time: 85.1 us -> 90.7 us (1.066)
  waiting for transfers between devices: 30.5 us -> 22.1 us
  local copies, waits for them, and re-layouts: 5.28 us -> 11.9 us
  starting transfers between devices: 13.7 us -> 18.2 us
  Pallas kernels: 25 us -> 27.4 us
    unnamed x22 -> x58, local copies, waits for them, and re-layouts: 3.98 us -> 11.9 us
    ppermute x6 -> x9, waiting for transfers between devices: 19.1 us -> 14.2 us  [shards(): piece.append(lax.ppermute(piece[-1], 'rows', step))]
    ppermute x3, waiting for transfers between devices: 5.46 us -> 0.8 us  [exchange(): rest = lax.ppermute(rest, 'rows', pairs)]
    ppermute x6 -> x9, starting transfers between devices: 8.95 us -> 12.8 us  [shards(): piece.append(lax.ppermute(piece[-1], 'rows', step))]
    pallas_call x4 -> x7, Pallas kernels: 16.6 us -> 19.1 us  [the longest x2 11.7 us: spectra_of(): pl.pallas_call(functools.partial(spectra_kernel, bands, bins, taps, part,...]
    reshape x1 -> x0, local copies, waits for them, and re-layouts: 1.3 us -> none  [spectra_of(): binned = offset_bin.reshape(shots // per, per, count)]
    ppermute x3, waiting for transfers between devices: 5.9 us -> 7.03 us  [exchange(): first = lax.ppermute(first, 'rows', pairs)]
  transfers between devices with their start and end apart: 12 -> 15, of which waited for: 7 -> 5; matrix products, arithmetic and copies ran while one was open for 0% -> 0% of each run, Pallas kernels for 11% -> 20%
where the time goes in v2:
time: 90.7 us; the launch traced here: 90 us
  Pallas kernels  27.4 us (30%)
  waiting for transfers between devices  22.1 us (24%)
  starting transfers between devices  18.2 us (20%)
  local copies, waits for them, and re-layouts  11.9 us (13%)
  blocking collectives  9.2 us (10%)
    ppermute x9, waiting for transfers between devices, shards(): piece.append(lax.ppermute(piece[-1], 'rows', step))  14.2 us
    ppermute x9, starting transfers between devices, shards(): piece.append(lax.ppermute(piece[-1], 'rows', step))  12.8 us
    unnamed x58, local copies, waits for them, and re-layouts  11.9 us
    pallas_call x2, Pallas kernels, spectra_of(): pl.pallas_call(functools.partial(spectra_kernel, bands, bins, taps, part,...  11.7 us
    all_to_all x1, blocking collectives, shards(): lax.all_to_all(partial_value, 'rows', split_axis=0, concat_axis=0, tiled=...  9.2 us
    pallas_call x4, Pallas kernels, rows_for(): pl.pallas_call(functools.partial(rows_kernel, block, head, starts), in_sp...  8.32 us
    ppermute x3, waiting for transfers between devices, exchange(): first = lax.ppermute(first, 'rows', pairs)  7.03 us
    pallas_call x3, Pallas kernels, predict(): pl.pallas_call(functools.partial(predict_kernel, parts, slots, before is...  6.38 us
  transfers between devices with their start and end apart: 15, of which 5 were waited for; matrix products, arithmetic and copies ran while one was open for 0% of the time, Pallas kernels for 20%

profile of v2, /device:TPU:0, one launch (start us, length us, event | category | flops | bytes accessed | tf_op | source)
XLA Modules:
  0.0 90.0 jit_solution(9570681061113989625)
XLA Ops:
  0.0 5.9 %spectra.2 = (bf16[4,256,128]{2,1,0:T(8,128)(2,1)}, bf16[128,256]{1,0:T(8,128)(2,1)}, bf16[512,128]{1,0:T(8,128)(2,1)}) custom-call(bf16[8,256,2048]{2,1,0:T(8,128)(2,1)} %refs_0_.3, s32[8,256]{1,0:T(8,128)} %refs_1_.3, bf16[2048,256]{1,0:T(8,128)(2,1)} %constant.24.clone.refs_2_, f32[16,32]{1,0:T(8,128)} %refs_3_.1, f32[32,256]{1,0:T(8,128)} %constant.25.clone.refs_4_, ...), custom_call_target="tpu_custom_call" | custom-call | flops 1073741824 | bytes 4194304 | tf_op jit(solution)/shard_map/spectra/pallas_call | solution.py:174
  5.9 4.1 %collective-permute-start.6 = (bf16[4,256,128]{2,1,0:T(8,128)(2,1)}, bf16[4,256,128]{2,1,0:T(8,128)(2,1)S(1)}, u32[]{:S(2)}, u32[]{:S(2)}) collective-permute-start(bf16[4,256,128]{2,1,0:T(8,128)(2,1)} %get-tuple-element.25.refs_0_), channel_id=1, source_target_pairs={{0,8},{1,9},{2,10},{3,11},{4,0},{5,1},{6,2},{7,3},{8,12},{9,13},{1... | collective-permute-start | bytes 786440 | tf_op jit(solution)/shard_map/ppermute | solution.py:409
  10.0 5.8 %spectra.3 = (bf16[3,256,128]{2,1,0:T(8,128)(2,1)}, bf16[1,256,128]{2,1,0:T(8,128)(2,1)}) custom-call(bf16[8,256,2048]{2,1,0:T(8,128)(2,1)} %refs_0_.3, s32[8,256]{1,0:T(8,128)} %refs_1_.3, bf16[2048,256]{1,0:T(8,128)(2,1)} %constant.24.clone.refs_2_, bf16[128,256]{1,0:T(8,128)(2,1)} %get-tuple-element.22.refs_3_, bf16[512,128]{1,0:T(8,128)(2,1)} %get-tuple-element.23.refs_4_), custom_call_target="tpu_custom_call" | custom-call | flops 1073741824 | bytes 4194304 | tf_op jit(solution)/shard_map/spectra/pallas_call | solution.py:174
  15.8 1.6 %collective-permute-start.12 = (bf16[1,256,128]{2,1,0:T(8,128)(2,1)}, bf16[1,256,128]{2,1,0:T(8,128)(2,1)S(1)}, u32[]{:S(2)}, u32[]{:S(2)}) collective-permute-start(bf16[1,256,128]{2,1,0:T(8,128)(2,1)} %get-tuple-element.30.refs_4_), channel_id=1, source_target_pairs={{0,8},{1,9},{2,10},{3,11},{4,0},{5,1},{6,2},{7,3},{8,12},{9,13},{1... | collective-permute-start | bytes 196616 | tf_op jit(solution)/shard_map/ppermute | solution.py:409
  17.4 0.3 collective-permute-start.3
  17.8 3.3 %collective-permute-done.12.refs_5_ = bf16[1,256,128]{2,1,0:T(8,128)(2,1)S(1)} collective-permute-done((bf16[1,256,128]{2,1,0:T(8,128)(2,1)}, bf16[1,256,128]{2,1,0:T(8,128)(2,1)S(1)}, u32[]{:S(2)}, u32[]{:S(2)}) %collective-permute-start.12) | collective-permute-done | bytes 65568 | tf_op jit(solution)/shard_map/ppermute | solution.py:409
  21.0 2.5 %collective-permute-start.13 = (bf16[1,256,128]{2,1,0:T(8,128)(2,1)S(1)}, bf16[1,256,128]{2,1,0:T(8,128)(2,1)S(1)}, u32[]{:S(2)}, u32[]{:S(2)}) collective-permute-start(bf16[1,256,128]{2,1,0:T(8,128)(2,1)S(1)} %collective-permute-done.12.refs_5_), channel_id=1, source_target_pairs={{0,8},{1,9},{2,10},{3,11},{4,0},{5,1},{6,2},{7,3},{8,12},{9,13},{1... | collective-permute-start | bytes 196616 | tf_op jit(solution)/shard_map/ppermute | solution.py:409
  23.5 2.1 %rows_for.6 = (bf16[3,4,16,2,4,256]{5,4,3,2,1,0:T(4,128)(2,1)}, bf16[1,4,16,2,4,256]{5,4,3,2,1,0:T(4,128)(2,1)}) custom-call(bf16[4,16,2,4,4096]{4,3,2,1,0:T(4,128)(2,1)} %bitcast.5), custom_call_target="tpu_custom_call" | custom-call | tf_op jit(solution)/shard_map/rows_for/pallas_call | solution.py:250
  25.6 1.6 %collective-permute-start.10 = (bf16[1,4,16,2,4,256]{5,4,3,2,1,0:T(4,128)(2,1)}, bf16[1,4,16,2,4,256]{5,4,3,2,1,0:T(4,128)(2,1)S(1)}, u32[]{:S(2)}, u32[]{:S(2)}) collective-permute-start(bf16[1,4,16,2,4,256]{5,4,3,2,1,0:T(4,128)(2,1)} %get-tuple-element.28), channel_id=1, source_target_pairs={{0,2},{1,3},{2,0},{3,1},{4,6},{5,7},{6,4},{7,5},{8,10},{9,11},{10,... | collective-permute-start | bytes 786440 | tf_op jit(solution)/shard_map/ppermute | solution.py:396
  27.2 1.5 %collective-permute-start.14 = (bf16[1,256,128]{2,1,0:T(8,128)(2,1)S(1)}, bf16[1,256,128]{2,1,0:T(8,128)(2,1)S(1)}, u32[]{:S(2)}, u32[]{:S(2)}) collective-permute-start(bf16[1,256,128]{2,1,0:T(8,128)(2,1)S(1)} %collective-permute-done.13.refs_6_), channel_id=1, source_target_pairs={{0,8},{1,9},{2,10},{3,11},{4,0},{5,1},{6,2},{7,3},{8,12},{9,13},{1... | collective-permute-start | bytes 196616 | tf_op jit(solution)/shard_map/ppermute | solution.py:409
  28.7 2.1 %rows_for.7 = (bf16[3,4,16,2,4,256]{5,4,3,2,1,0:T(4,128)(2,1)}, bf16[1,4,16,2,4,256]{5,4,3,2,1,0:T(4,128)(2,1)}) custom-call(bf16[4,16,2,4,4096]{4,3,2,1,0:T(4,128)(2,1)} %bitcast.6), custom_call_target="tpu_custom_call" | custom-call | tf_op jit(solution)/shard_map/rows_for/pallas_call | solution.py:250
  30.7 0.1 collective-permute-start.11
  30.8 2.1 %rows_for.5 = (bf16[3,4,16,2,4,256]{5,4,3,2,1,0:T(4,128)(2,1)}, bf16[1,4,16,2,4,256]{5,4,3,2,1,0:T(4,128)(2,1)}) custom-call(bf16[4,16,2,4,4096]{4,3,2,1,0:T(4,128)(2,1)} %bitcast.7), custom_call_target="tpu_custom_call" | custom-call | tf_op jit(solution)/shard_map/rows_for/pallas_call | solution.py:250
  33.0 0.6 copy-done.25
  33.6 1.6 %collective-permute-start = (bf16[3,4,16,2,4,256]{5,4,3,2,1,0:T(4,128)(2,1)}, bf16[3,4,16,2,4,256]{5,4,3,2,1,0:T(4,128)(2,1)S(1)}, u32[]{:S(2)}, u32[]{:S(2)}) collective-permute-start(bf16[3,4,16,2,4,256]{5,4,3,2,1,0:T(4,128)(2,1)} %get-tuple-element.19), channel_id=1, source_target_pairs={{0,1},{1,0},{2,3},{3,2},{4,5},{5,4},{6,7},{7,6},{8,9},{9,8},{10,11... | collective-permute-start | bytes 2359304 | tf_op jit(solution)/shard_map/ppermute | solution.py:395
  35.2 0.7 copy-done.12
  35.9 0.5 collective-permute-start.1
  36.4 0.8 collective-permute-start.2
  37.3 0.7 copy-done.4
  38.0 0.8 collective-permute-start.9
  38.8 0.8 collective-permute-done.11.refs_3_
  39.6 0.7 copy-done.6
  40.3 0.7 copy-done.8
  41.0 0.9 collective-permute-start.4
  41.8 7.6 %collective-permute-done.7.refs_2_ = bf16[4,256,128]{2,1,0:T(8,128)(2,1)S(1)} collective-permute-done((bf16[4,256,128]{2,1,0:T(8,128)(2,1)S(1)}, bf16[4,256,128]{2,1,0:T(8,128)(2,1)S(1)}, u32[]{:S(2)}, u32[]{:S(2)}) %collective-permute-start.7) | collective-permute-done | bytes 262176 | tf_op jit(solution)/shard_map/ppermute | solution.py:409
  49.4 0.9 %collective-permute-start.8 = (bf16[4,256,128]{2,1,0:T(8,128)(2,1)S(1)}, bf16[4,256,128]{2,1,0:T(8,128)(2,1)S(1)}, u32[]{:S(2)}, u32[]{:S(2)}) collective-permute-start(bf16[4,256,128]{2,1,0:T(8,128)(2,1)S(1)} %collective-permute-done.7.refs_2_), channel_id=1, source_target_pairs={{0,8},{1,9},{2,10},{3,11},{4,0},{5,1},{6,2},{7,3},{8,12},{9,13},{1... | collective-permute-start | bytes 786440 | tf_op jit(solution)/shard_map/ppermute | solution.py:409
  50.4 3.4 %collective-permute-done.4.refs_2_ = bf16[3,256,128]{2,1,0:T(8,128)(2,1)} collective-permute-done((bf16[3,256,128]{2,1,0:T(8,128)(2,1)}, bf16[3,256,128]{2,1,0:T(8,128)(2,1)}, u32[]{:S(2)}, u32[]{:S(2)}) %collective-permute-start.4) | collective-permute-done | bytes 196640 | tf_op jit(solution)/shard_map/ppermute | solution.py:409
  53.7 0.9 %collective-permute-start.5 = (bf16[3,256,128]{2,1,0:T(8,128)(2,1)}, bf16[3,256,128]{2,1,0:T(8,128)(2,1)}, u32[]{:S(2)}, u32[]{:S(2)}) collective-permute-start(bf16[3,256,128]{2,1,0:T(8,128)(2,1)} %collective-permute-done.4.refs_2_), channel_id=1, source_target_pairs={{0,8},{1,9},{2,10},{3,11},{4,0},{5,1},{6,2},{7,3},{8,12},{9,13},{1... | collective-permute-start | bytes 589832 | tf_op jit(solution)/shard_map/ppermute | solution.py:409
  54.7 2.1 %rows_for.4 = (bf16[3,4,16,2,4,256]{5,4,3,2,1,0:T(4,128)(2,1)}, bf16[1,4,16,2,4,256]{5,4,3,2,1,0:T(4,128)(2,1)}) custom-call(bf16[4,16,2,4,4096]{4,3,2,1,0:T(4,128)(2,1)} %bitcast.8), custom_call_target="tpu_custom_call" | custom-call | tf_op jit(solution)/shard_map/rows_for/pallas_call | solution.py:250
  56.8 1.0 %copy-done.5 = bf16[1,4,16,2,4,256]{5,4,3,2,1,0:T(4,128)(2,1)S(1)} copy-done((bf16[1,4,16,2,4,256]{5,4,3,2,1,0:T(4,128)(2,1)S(1)}, bf16[1,4,16,2,4,256]{5,4,3,2,1,0:T(4,128)(2,1)}, u32[]{:S(2)}) %copy-start.5) | copy-done | bytes 262168
  57.8 0.9 %copy-done.7 = bf16[1,4,16,2,4,256]{5,4,3,2,1,0:T(4,128)(2,1)S(1)} copy-done((bf16[1,4,16,2,4,256]{5,4,3,2,1,0:T(4,128)(2,1)S(1)}, bf16[1,4,16,2,4,256]{5,4,3,2,1,0:T(4,128)(2,1)}, u32[]{:S(2)}) %copy-start.7) | copy-done | bytes 262168
  58.8 0.9 %copy-done.9 = bf16[1,4,16,2,4,256]{5,4,3,2,1,0:T(4,128)(2,1)S(1)} copy-done((bf16[1,4,16,2,4,256]{5,4,3,2,1,0:T(4,128)(2,1)S(1)}, bf16[1,4,16,2,4,256]{5,4,3,2,1,0:T(4,128)(2,1)}, u32[]{:S(2)}) %copy-start.9) | copy-done | bytes 262168
  59.7 0.9 %copy-done.10 = bf16[1,4,16,2,4,256]{5,4,3,2,1,0:T(4,128)(2,1)S(1)} copy-done((bf16[1,4,16,2,4,256]{5,4,3,2,1,0:T(4,128)(2,1)S(1)}, bf16[1,4,16,2,4,256]{5,4,3,2,1,0:T(4,128)(2,1)}, u32[]{:S(2)}) %copy-start.10) | copy-done | bytes 262168
  60.7 0.3 merge.3.matrix
  61.0 1.0 %copy-done.3 = f32[256,256]{1,0:T(8,128)S(1)} copy-done((f32[256,256]{1,0:T(8,128)S(1)}, f32[256,256]{1,0:T(8,128)}, u32[]{:S(2)}) %copy-start.3) | copy-done | bytes 262168
  62.0 0.8 copy-done.20
  62.8 0.8 copy-done.22
  63.6 0.8 copy-done.24
  64.5 0.8 copy-done.26
  65.3 0.9 predict.5
  66.2 7.0 %collective-permute-done.2.refs_3_ = bf16[3,4,16,2,4,256]{5,4,3,2,1,0:T(4,128)(2,1)S(1)} collective-permute-done((bf16[3,4,16,2,4,256]{5,4,3,2,1,0:T(4,128)(2,1)}, bf16[3,4,16,2,4,256]{5,4,3,2,1,0:T(4,128)(2,1)S(1)}, u32[]{:S(2)}, u32[]{:S(2)}) %collective-permute-start.2) | collective-permute-done | bytes 786464 | tf_op jit(solution)/shard_map/ppermute | solution.py:395
  73.3 0.8 merge.2.matrix
  74.2 2.2 %predict.3.refs_7_ = bf16[12,16,64]{2,1,0:T(8,128)(2,1)S(1)} custom-call(bf16[3,512,1024]{2,1,0:T(8,128)(2,1)S(1)} %merge.2.matrix, bf16[4,256,128]{2,1,0:T(8,128)(2,1)S(1)} %copy-done, bf16[4,256,128]{2,1,0:T(8,128)(2,1)S(1)} %collective-permute-done.6.refs_1_, bf16[4,256,128]{2,1,0:T(8,128)(2,1)S(1)} %collective-permute-done.7.refs_2_, ...), custom_call_target="tpu_custom_call" | custom-call | tf_op jit(solution)/shard_map/predict/pallas_call | solution.py:350
  76.5 3.3 %predict.4 = bf16[12,16,64]{2,1,0:T(8,128)(2,1)S(1)} custom-call(bf16[3,512,1024]{2,1,0:T(8,128)(2,1)S(1)} %merge.2.matrix, bf16[3,256,128]{2,1,0:T(8,128)(2,1)S(1)} %copy-done.11, bf16[3,256,128]{2,1,0:T(8,128)(2,1)S(1)} %copy-done.13, bf16[3,256,128]{2,1,0:T(8,128)(2,1)} %collective-permute-done.4.refs_2_, ...), custom_call_target="tpu_custom_call" | custom-call | tf_op jit(solution)/shard_map/predict/pallas_call | solution.py:350
  79.8 0.1 reshape.15
  79.9 9.2 %all_to_all.5 = bf16[16,2,512]{2,1,0:T(2,128)(2,1)S(1)} all-to-all(bf16[16,2,512]{2,1,0:T(2,128)(2,1)S(1)} %reshape.15), channel_id=1, replica_groups=mesh['parts'=2,'rows'=16] {'rows'}, dimensions={0} | all-to-all | bytes 65536 | tf_op jit(solution)/shard_map/all_to_all | solution.py:425
  89.1 0.1 reshape.16
  89.2 0.8 convolution_convert_fusion
  (54 shorter events, 0.2 us)
Async XLA Ops:
  5.9 30.6 %collective-permute-start.6 = (bf16[4,256,128]{2,1,0:T(8,128)(2,1)}, bf16[4,256,128]{2,1,0:T(8,128)(2,1)S(1)}, u32[]{:S(2)}, u32[]{:S(2)}) collective-permute-start(bf16[4,256,128]{2,1,0:T(8,128)(2,1)} %get-tuple-element.25.refs_0_), channel_id=1, source_target_pairs={{0,8},{1,9},{2,10},{3,11},{4,0},{5,1},{6,2},{7,3},{8,12},{9,13},{1... | collective-permute-start | bytes 786440 | tf_op jit(solution)/shard_map/ppermute | solution.py:409
  15.8 5.2 %collective-permute-start.12 = (bf16[1,256,128]{2,1,0:T(8,128)(2,1)}, bf16[1,256,128]{2,1,0:T(8,128)(2,1)S(1)}, u32[]{:S(2)}, u32[]{:S(2)}) collective-permute-start(bf16[1,256,128]{2,1,0:T(8,128)(2,1)} %get-tuple-element.30.refs_4_), channel_id=1, source_target_pairs={{0,8},{1,9},{2,10},{3,11},{4,0},{5,1},{6,2},{7,3},{8,12},{9,13},{1... | collective-permute-start | bytes 196616 | tf_op jit(solution)/shard_map/ppermute | solution.py:409
  17.4 17.8 %collective-permute-start.3 = (bf16[3,256,128]{2,1,0:T(8,128)(2,1)}, bf16[3,256,128]{2,1,0:T(8,128)(2,1)S(1)}, u32[]{:S(2)}, u32[]{:S(2)}) collective-permute-start(bf16[3,256,128]{2,1,0:T(8,128)(2,1)} %get-tuple-element.24.refs_0_), channel_id=1, source_target_pairs={{0,8},{1,9},{2,10},{3,11},{4,0},{5,1},{6,2},{7,3},{8,12},{9,13},{1... | collective-permute-start | bytes 589832 | tf_op jit(solution)/shard_map/ppermute | solution.py:409
  21.0 9.7 %copy-start.21 = (bf16[1,256,128]{2,1,0:T(8,128)(2,1)}, bf16[1,256,128]{2,1,0:T(8,128)(2,1)S(1)}, u32[]{:S(2)}) copy-start(bf16[1,256,128]{2,1,0:T(8,128)(2,1)S(1)} %collective-permute-done.12.refs_5_) | copy-start | bytes 196612
  21.0 6.1 %collective-permute-start.13 = (bf16[1,256,128]{2,1,0:T(8,128)(2,1)S(1)}, bf16[1,256,128]{2,1,0:T(8,128)(2,1)S(1)}, u32[]{:S(2)}, u32[]{:S(2)}) collective-permute-start(bf16[1,256,128]{2,1,0:T(8,128)(2,1)S(1)} %collective-permute-done.12.refs_5_), channel_id=1, source_target_pairs={{0,8},{1,9},{2,10},{3,11},{4,0},{5,1},{6,2},{7,3},{8,12},{9,13},{1... | collective-permute-start | bytes 196616 | tf_op jit(solution)/shard_map/ppermute | solution.py:409
  25.6 11.7 %collective-permute-start.10 = (bf16[1,4,16,2,4,256]{5,4,3,2,1,0:T(4,128)(2,1)}, bf16[1,4,16,2,4,256]{5,4,3,2,1,0:T(4,128)(2,1)S(1)}, u32[]{:S(2)}, u32[]{:S(2)}) collective-permute-start(bf16[1,4,16,2,4,256]{5,4,3,2,1,0:T(4,128)(2,1)} %get-tuple-element.28), channel_id=1, source_target_pairs={{0,2},{1,3},{2,0},{3,1},{4,6},{5,7},{6,4},{7,5},{8,10},{9,11},{10,... | collective-permute-start | bytes 786440 | tf_op jit(solution)/shard_map/ppermute | solution.py:396
  27.2 5.8 %copy-start.23 = (bf16[1,256,128]{2,1,0:T(8,128)(2,1)}, bf16[1,256,128]{2,1,0:T(8,128)(2,1)S(1)}, u32[]{:S(2)}) copy-start(bf16[1,256,128]{2,1,0:T(8,128)(2,1)S(1)} %collective-permute-done.13.refs_6_) | copy-start | bytes 196612
  27.2 5.8 %collective-permute-start.14 = (bf16[1,256,128]{2,1,0:T(8,128)(2,1)S(1)}, bf16[1,256,128]{2,1,0:T(8,128)(2,1)S(1)}, u32[]{:S(2)}, u32[]{:S(2)}) collective-permute-start(bf16[1,256,128]{2,1,0:T(8,128)(2,1)S(1)} %collective-permute-done.13.refs_6_), channel_id=1, source_target_pairs={{0,8},{1,9},{2,10},{3,11},{4,0},{5,1},{6,2},{7,3},{8,12},{9,13},{1... | collective-permute-start | bytes 196616 | tf_op jit(solution)/shard_map/ppermute | solution.py:409
  30.7 8.8 %collective-permute-start.11 = (bf16[1,4,16,2,4,256]{5,4,3,2,1,0:T(4,128)(2,1)}, bf16[1,4,16,2,4,256]{5,4,3,2,1,0:T(4,128)(2,1)S(1)}, u32[]{:S(2)}, u32[]{:S(2)}) collective-permute-start(bf16[1,4,16,2,4,256]{5,4,3,2,1,0:T(4,128)(2,1)} %get-tuple-element.29), channel_id=1, source_target_pairs={{0,3},{1,2},{2,1},{3,0},{4,7},{5,6},{6,5},{7,4},{8,11},{9,10},{10,... | collective-permute-start | bytes 786440 | tf_op jit(solution)/shard_map/ppermute | solution.py:396
  32.9 28.0 %copy-start = (bf16[4,256,128]{2,1,0:T(8,128)(2,1)S(1)}, bf16[4,256,128]{2,1,0:T(8,128)(2,1)}, u32[]{:S(2)}) copy-start(bf16[4,256,128]{2,1,0:T(8,128)(2,1)} %get-tuple-element.25.refs_0_) | copy-start | bytes 786436
  32.9 28.0 %copy-start.18 = (bf16[1,256,64]{2,1,0:T(8,128)(2,1)S(1)}, bf16[1,256,64]{2,1,0:T(8,128)(2,1)}, u32[]{:S(2)}) copy-start(bf16[1,256,64]{2,1,0:T(8,128)(2,1)} %constant.33.clone.refs_9_) | copy-start | bytes 98308
  33.0 28.0 %copy-start.19 = (bf16[1,256,64]{2,1,0:T(8,128)(2,1)S(1)}, bf16[1,256,64]{2,1,0:T(8,128)(2,1)}, u32[]{:S(2)}) copy-start(bf16[1,256,64]{2,1,0:T(8,128)(2,1)} %constant.34.clone.refs_10_) | copy-start | bytes 98308
  33.0 0.6 copy-start.25
  33.6 32.6 %collective-permute-start = (bf16[3,4,16,2,4,256]{5,4,3,2,1,0:T(4,128)(2,1)}, bf16[3,4,16,2,4,256]{5,4,3,2,1,0:T(4,128)(2,1)S(1)}, u32[]{:S(2)}, u32[]{:S(2)}) collective-permute-start(bf16[3,4,16,2,4,256]{5,4,3,2,1,0:T(4,128)(2,1)} %get-tuple-element.19), channel_id=1, source_target_pairs={{0,1},{1,0},{2,3},{3,2},{4,5},{5,4},{6,7},{7,6},{8,9},{9,8},{10,11... | collective-permute-start | bytes 2359304 | tf_op jit(solution)/shard_map/ppermute | solution.py:395
  35.2 0.7 copy-start.12
  35.9 30.3 %collective-permute-start.1 = (bf16[3,4,16,2,4,256]{5,4,3,2,1,0:T(4,128)(2,1)}, bf16[3,4,16,2,4,256]{5,4,3,2,1,0:T(4,128)(2,1)S(1)}, u32[]{:S(2)}, u32[]{:S(2)}) collective-permute-start(bf16[3,4,16,2,4,256]{5,4,3,2,1,0:T(4,128)(2,1)} %get-tuple-element.20), channel_id=1, source_target_pairs={{0,2},{1,3},{2,0},{3,1},{4,6},{5,7},{6,4},{7,5},{8,10},{9,11},{10,... | collective-permute-start | bytes 2359304 | tf_op jit(solution)/shard_map/ppermute | solution.py:395
  36.4 36.8 %collective-permute-start.2 = (bf16[3,4,16,2,4,256]{5,4,3,2,1,0:T(4,128)(2,1)}, bf16[3,4,16,2,4,256]{5,4,3,2,1,0:T(4,128)(2,1)S(1)}, u32[]{:S(2)}, u32[]{:S(2)}) collective-permute-start(bf16[3,4,16,2,4,256]{5,4,3,2,1,0:T(4,128)(2,1)} %get-tuple-element.21), channel_id=1, source_target_pairs={{0,3},{1,2},{2,1},{3,0},{4,7},{5,6},{6,5},{7,4},{8,11},{9,10},{10,... | collective-permute-start | bytes 2359304 | tf_op jit(solution)/shard_map/ppermute | solution.py:395
  37.3 0.7 copy-start.4
  38.0 2.3 %collective-permute-start.9 = (bf16[1,4,16,2,4,256]{5,4,3,2,1,0:T(4,128)(2,1)}, bf16[1,4,16,2,4,256]{5,4,3,2,1,0:T(4,128)(2,1)S(1)}, u32[]{:S(2)}, u32[]{:S(2)}) collective-permute-start(bf16[1,4,16,2,4,256]{5,4,3,2,1,0:T(4,128)(2,1)} %get-tuple-element.27), channel_id=1, source_target_pairs={{0,1},{1,0},{2,3},{3,2},{4,5},{5,4},{6,7},{7,6},{8,9},{9,8},{10,11... | collective-permute-start | bytes 786440 | tf_op jit(solution)/shard_map/ppermute | solution.py:396
  39.6 0.7 copy-start.6
  40.3 9.2 %collective-permute-start.7 = (bf16[4,256,128]{2,1,0:T(8,128)(2,1)S(1)}, bf16[4,256,128]{2,1,0:T(8,128)(2,1)S(1)}, u32[]{:S(2)}, u32[]{:S(2)}) collective-permute-start(bf16[4,256,128]{2,1,0:T(8,128)(2,1)S(1)} %collective-permute-done.6.refs_1_), channel_id=1, source_target_pairs={{0,8},{1,9},{2,10},{3,11},{4,0},{5,1},{6,2},{7,3},{8,12},{9,13},{1... | collective-permute-start | bytes 786440 | tf_op jit(solution)/shard_map/ppermute | solution.py:409
  40.3 0.7 copy-start.8
  41.0 12.8 %collective-permute-start.4 = (bf16[3,256,128]{2,1,0:T(8,128)(2,1)}, bf16[3,256,128]{2,1,0:T(8,128)(2,1)}, u32[]{:S(2)}, u32[]{:S(2)}) collective-permute-start(bf16[3,256,128]{2,1,0:T(8,128)(2,1)} %copy-done.12), channel_id=1, source_target_pairs={{0,8},{1,9},{2,10},{3,11},{4,0},{5,1},{6,2},{7,3},{8,12},{9,13},{1... | collective-permute-start | bytes 589832 | tf_op jit(solution)/shard_map/ppermute | solution.py:409
  49.4 11.5 %collective-permute-start.8 = (bf16[4,256,128]{2,1,0:T(8,128)(2,1)S(1)}, bf16[4,256,128]{2,1,0:T(8,128)(2,1)S(1)}, u32[]{:S(2)}, u32[]{:S(2)}) collective-permute-start(bf16[4,256,128]{2,1,0:T(8,128)(2,1)S(1)} %collective-permute-done.7.refs_2_), channel_id=1, source_target_pairs={{0,8},{1,9},{2,10},{3,11},{4,0},{5,1},{6,2},{7,3},{8,12},{9,13},{1... | collective-permute-start | bytes 786440 | tf_op jit(solution)/shard_map/ppermute | solution.py:409
  53.7 22.7 %collective-permute-start.5 = (bf16[3,256,128]{2,1,0:T(8,128)(2,1)}, bf16[3,256,128]{2,1,0:T(8,128)(2,1)}, u32[]{:S(2)}, u32[]{:S(2)}) collective-permute-start(bf16[3,256,128]{2,1,0:T(8,128)(2,1)} %collective-permute-done.4.refs_2_), channel_id=1, source_target_pairs={{0,8},{1,9},{2,10},{3,11},{4,0},{5,1},{6,2},{7,3},{8,12},{9,13},{1... | collective-permute-start | bytes 589832 | tf_op jit(solution)/shard_map/ppermute | solution.py:409
  56.8 16.5 %copy-start.1 = (bf16[3,4,16,2,4,256]{5,4,3,2,1,0:T(4,128)(2,1)S(1)}, bf16[3,4,16,2,4,256]{5,4,3,2,1,0:T(4,128)(2,1)}, u32[]{:S(2)}) copy-start(bf16[3,4,16,2,4,256]{5,4,3,2,1,0:T(4,128)(2,1)} %get-tuple-element.18.refs_0_) | copy-start | bytes 2359300
  56.8 1.0 %copy-start.5 = (bf16[1,4,16,2,4,256]{5,4,3,2,1,0:T(4,128)(2,1)S(1)}, bf16[1,4,16,2,4,256]{5,4,3,2,1,0:T(4,128)(2,1)}, u32[]{:S(2)}) copy-start(bf16[1,4,16,2,4,256]{5,4,3,2,1,0:T(4,128)(2,1)} %copy-done.4) | copy-start | bytes 786436
  57.8 0.9 %copy-start.7 = (bf16[1,4,16,2,4,256]{5,4,3,2,1,0:T(4,128)(2,1)S(1)}, bf16[1,4,16,2,4,256]{5,4,3,2,1,0:T(4,128)(2,1)}, u32[]{:S(2)}) copy-start(bf16[1,4,16,2,4,256]{5,4,3,2,1,0:T(4,128)(2,1)} %copy-done.6) | copy-start | bytes 786436
  58.8 0.9 %copy-start.9 = (bf16[1,4,16,2,4,256]{5,4,3,2,1,0:T(4,128)(2,1)S(1)}, bf16[1,4,16,2,4,256]{5,4,3,2,1,0:T(4,128)(2,1)}, u32[]{:S(2)}) copy-start(bf16[1,4,16,2,4,256]{5,4,3,2,1,0:T(4,128)(2,1)} %copy-done.8) | copy-start | bytes 786436
  59.7 0.9 %copy-start.10 = (bf16[1,4,16,2,4,256]{5,4,3,2,1,0:T(4,128)(2,1)S(1)}, bf16[1,4,16,2,4,256]{5,4,3,2,1,0:T(4,128)(2,1)}, u32[]{:S(2)}) copy-start(bf16[1,4,16,2,4,256]{5,4,3,2,1,0:T(4,128)(2,1)} %get-tuple-element.26.refs_0_) | copy-start | bytes 786436
  60.9 13.2 %copy-start.2 = (f32[256,128]{1,0:T(8,128)S(1)}, f32[256,128]{1,0:T(8,128)}, u32[]{:S(2)}) copy-start(f32[256,128]{1,0:T(8,128)} %constant.27.clone.refs_4_) | copy-start | bytes 393220
  61.0 1.0 %copy-start.3 = (f32[256,256]{1,0:T(8,128)S(1)}, f32[256,256]{1,0:T(8,128)}, u32[]{:S(2)}) copy-start(f32[256,256]{1,0:T(8,128)} %constant.32.clone.refs_8_) | copy-start | bytes 786436
  62.0 0.8 copy-start.20
  62.8 0.8 copy-start.22
  63.6 0.8 copy-start.24
  64.5 0.8 copy-start.26
  65.3 8.8 %copy-start.16 = (bf16[3,128,64]{2,1,0:T(8,128)(2,1)S(1)}, bf16[3,128,64]{2,1,0:T(8,128)(2,1)}, u32[]{:S(2)}) copy-start(bf16[3,128,64]{2,1,0:T(8,128)(2,1)} %constant.28.clone.refs_5_) | copy-start | bytes 147460
  65.3 8.8 %copy-start.17 = (bf16[3,128,64]{2,1,0:T(8,128)(2,1)S(1)}, bf16[3,128,64]{2,1,0:T(8,128)(2,1)}, u32[]{:S(2)}) copy-start(bf16[3,128,64]{2,1,0:T(8,128)(2,1)} %constant.29.clone.refs_6_) | copy-start | bytes 147460
  73.3 3.2 %copy-start.11 = (bf16[3,256,128]{2,1,0:T(8,128)(2,1)S(1)}, bf16[3,256,128]{2,1,0:T(8,128)(2,1)}, u32[]{:S(2)}) copy-start(bf16[3,256,128]{2,1,0:T(8,128)(2,1)} %get-tuple-element.24.refs_0_) | copy-start | bytes 589828
  73.3 3.2 %copy-start.13 = (bf16[3,256,128]{2,1,0:T(8,128)(2,1)S(1)}, bf16[3,256,128]{2,1,0:T(8,128)(2,1)}, u32[]{:S(2)}) copy-start(bf16[3,256,128]{2,1,0:T(8,128)(2,1)} %copy-done.12) | copy-start | bytes 589828
  73.3 3.2 %copy-start.14 = (bf16[3,128,64]{2,1,0:T(8,128)(2,1)S(1)}, bf16[3,128,64]{2,1,0:T(8,128)(2,1)}, u32[]{:S(2)}) copy-start(bf16[3,128,64]{2,1,0:T(8,128)(2,1)} %constant.30.clone.refs_5_) | copy-start | bytes 147460
  73.3 3.2 %copy-start.15 = (bf16[3,128,64]{2,1,0:T(8,128)(2,1)S(1)}, bf16[3,128,64]{2,1,0:T(8,128)(2,1)}, u32[]{:S(2)}) copy-start(bf16[3,128,64]{2,1,0:T(8,128)(2,1)} %constant.31.clone.refs_6_) | copy-start | bytes 147460
  74.2 15.0 %copy-start.27 = (bf16[256,64]{1,0:T(8,128)(2,1)S(1)}, bf16[256,64]{1,0:T(8,128)(2,1)}, u32[]{:S(2)}) copy-start(bf16[256,64]{1,0:T(8,128)(2,1)} %constant.35.clone) | copy-start | bytes 98308

commit v3 on v2

--- a/solution.py
+++ b/solution.py
@@ -264,12 +264,19 @@
     )(source)
 
 
+def merged(rows_in):
+    columns = []
+    for i in range(rows_in[0].shape[1]):
+        part = jnp.concatenate([r[0, i] for r in rows_in], axis=2)
+        columns.append(part.reshape(-1, part.shape[-1]))
+    return columns
+
+
 def merge_kernel(*refs):
     rows_in, out = refs[:-1], refs[-1]
     block = rows_in[0].shape[-1]
-    for i in range(rows_in[0].shape[1]):
-        part = jnp.concatenate([r[0, i] for r in rows_in], axis=2)
-        out[0, :, i * block : (i + 1) * block] = part.reshape(-1, block)
+    for i, column in enumerate(merged(rows_in)):
+        out[0, :, i * block : (i + 1) * block] = column
 
 
 def merge(row_parts):
@@ -289,7 +296,13 @@
     )(*row_parts)
 
 
-def predict_kernel(parts, slots, before, matrix, *refs):
+def predict_kernel(members, parts, slots, before, *refs):
+    rows_in, refs = refs[:members], refs[members:]
+    if members == 1:
+        matrix = rows_in[0][0]
+    else:
+        columns = merged(rows_in)
+        matrix = columns[0] if len(columns) == 1 else jnp.concatenate(columns, axis=1)
     spectra_in = refs[: slots * parts]
     mask_ref, fold_a, fold_b = refs[slots * parts : slots * parts + 3]
     out = refs[-1]
@@ -299,7 +312,7 @@
     ]
     spectra = spectra[0] if slots == 1 else jnp.concatenate(spectra, axis=0)
     dests, rows, _ = out.shape
-    total = dot(matrix[0], spectra)
+    total = dot(matrix, spectra)
     total = total.reshape(BAND, 2, rows, -1)
     acc = None
     for c, fold in enumerate((fold_a, fold_b)):
@@ -318,12 +331,17 @@
 
 
 def predict(matrix, spectra_parts, share, shots, first, part, before=None):
-    number, wide, depth = matrix.shape
+    if isinstance(matrix, list):
+        number, _, _, _, rows, depth = matrix[0].shape
+        all_rows = rows * len(matrix)
+    else:
+        number, wide, depth = matrix.shape
+        all_rows = wide // (2 * BAND)
+        matrix = [matrix]
     parts, slots = len(spectra_parts), len(spectra_parts[0])
     _, block, width = spectra_parts[0][0].shape
     cols = width * parts
     per = width // (2 * BAND)
-    all_rows = wide // (2 * BAND)
     lanes = share * 2 * shots
     index = np.arange(cols)
     col_c, col_f = index // BAND % 2, index % BAND
@@ -348,9 +366,14 @@
     flat = [x for spectra in spectra_parts for x in spectra]
     starts = [first * (x.shape[0] > number) for x in flat]
     return pl.pallas_call(
-        functools.partial(predict_kernel, parts, slots, before is not None),
+        functools.partial(predict_kernel, len(matrix), parts, slots, before is not None),
         grid=(number,),
-        in_specs=[pl.BlockSpec((1, wide, depth), lambda q: (q, 0, 0))]
+        in_specs=[
+            pl.BlockSpec(
+                (1,) + x.shape[1:], functools.partial(lambda n, q: (q,) + (0,) * n, x.ndim - 1)
+            )
+            for x in matrix
+        ]
         + [
             pl.BlockSpec((1, block, width), functools.partial(lambda a, q: (a + q, 0, 0), a))
             for a in starts
@@ -362,7 +385,7 @@
         out_shape=jax.ShapeDtypeStruct((number * dests, all_rows, lanes), BF16),
         compiler_params=pltpu.CompilerParams(vmem_limit_bytes=40 << 20),
         name="predict",
-    )(matrix, *flat, *consts, *([] if before is None else [before]))
+    )(*matrix, *flat, *consts, *([] if before is None else [before]))
 
 
 def ring_of(length):
@@ -415,12 +438,11 @@
 
     share = freqs // devices
     first_matrix = merge(first_parts)
-    rest_matrix = merge(rest_parts)
     whole_pieces = [piece for _, piece in pieces[: quads - 1]]
     head_piece, rest_piece = pieces[quads - 1][1], pieces[-1][1]
     early = predict(first_matrix, whole_pieces, share, shot_count, 0, 0)
     early = predict(first_matrix, [head_piece], share, shot_count, 0, quads - 1, early)
-    late = predict(rest_matrix, whole_pieces + [rest_piece], share, shot_count, head, 0)
+    late = predict(rest_parts, whole_pieces + [rest_piece], share, shot_count, head, 0)
     partial_value = jnp.concatenate([early, late], axis=0)
     received = lax.all_to_all(partial_value, "rows", split_axis=0, concat_axis=0, tiled=True)
     choose = np.zeros((lines, members, members, row_count, lines, members, row_count))

time: 90.7 us -> 91.9 us (1.013)
  local copies, waits for them, and re-layouts: 11.9 us -> 12.9 us
    ppermute x9, waiting for transfers between devices: 14.2 us -> 16.7 us  [shards(): piece.append(lax.ppermute(piece[-1], 'rows', step))]
    ppermute x3, waiting for transfers between devices: 7.03 us -> 4.97 us  [exchange(): first = lax.ppermute(first, 'rows', pairs)]
    unnamed x58, local copies, waits for them, and re-layouts: 11.9 us -> 12.9 us
  transfers between devices with their start and end apart: 15 -> 15, of which waited for: 5 -> 6; matrix products, arithmetic and copies ran while one was open for 0% -> 0% of each run, Pallas kernels for 20% -> 20%
where the time goes in v3:
time: 91.9 us; the launch traced here: 91.1 us
  Pallas kernels  27.2 us (30%)
  waiting for transfers between devices  22.5 us (24%)
  starting transfers between devices  18.2 us (20%)
  local copies, waits for them, and re-layouts  12.9 us (14%)
  blocking collectives  9.2 us (10%)
    ppermute x9, waiting for transfers between devices, shards(): piece.append(lax.ppermute(piece[-1], 'rows', step))  16.7 us
    unnamed x58, local copies, waits for them, and re-layouts  12.9 us
    ppermute x9, starting transfers between devices, shards(): piece.append(lax.ppermute(piece[-1], 'rows', step))  12.8 us
    pallas_call x2, Pallas kernels, spectra_of(): pl.pallas_call(functools.partial(spectra_kernel, bands, bins, taps, part,...  11.7 us
    all_to_all x1, blocking collectives, shards(): lax.all_to_all(partial_value, 'rows', split_axis=0, concat_axis=0, tiled=...  9.2 us
    pallas_call x4, Pallas kernels, rows_for(): pl.pallas_call(functools.partial(rows_kernel, block, head, starts), in_sp...  8.35 us
    pallas_call x3, Pallas kernels, predict(): pl.pallas_call(functools.partial(predict_kernel, len(matrix), parts, slot...  6.38 us
    ppermute x3, waiting for transfers between devices, exchange(): first = lax.ppermute(first, 'rows', pairs)  4.97 us
  transfers between devices with their start and end apart: 15, of which 6 were waited for; matrix products, arithmetic and copies ran while one was open for 0% of the time, Pallas kernels for 20%

profile of v3, /device:TPU:0, one launch (start us, length us, event | category | flops | bytes accessed | tf_op | source)
XLA Modules:
  0.0 91.1 jit_solution(2579487865227574521)
XLA Ops:
  0.0 5.9 %spectra.2 = (bf16[4,256,128]{2,1,0:T(8,128)(2,1)}, bf16[128,256]{1,0:T(8,128)(2,1)}, bf16[512,128]{1,0:T(8,128)(2,1)}) custom-call(bf16[8,256,2048]{2,1,0:T(8,128)(2,1)} %refs_0_.3, s32[8,256]{1,0:T(8,128)} %refs_1_.3, bf16[2048,256]{1,0:T(8,128)(2,1)} %constant.24.clone.refs_2_, f32[16,32]{1,0:T(8,128)} %refs_3_.1, f32[32,256]{1,0:T(8,128)} %constant.25.clone.refs_4_, ...), custom_call_target="tpu_custom_call" | custom-call | flops 1073741824 | bytes 4194304 | tf_op jit(solution)/shard_map/spectra/pallas_call | solution.py:174
  5.9 4.1 %collective-permute-start.6 = (bf16[4,256,128]{2,1,0:T(8,128)(2,1)}, bf16[4,256,128]{2,1,0:T(8,128)(2,1)S(1)}, u32[]{:S(2)}, u32[]{:S(2)}) collective-permute-start(bf16[4,256,128]{2,1,0:T(8,128)(2,1)} %get-tuple-element.25.refs_1_.refs_4_), channel_id=1, source_target_pairs={{0,8},{1,9},{2,10},{3,11},{4,0},{5,1},{6,2},{7,3},{8,12},{9,13},{1... | collective-permute-start | bytes 786440 | tf_op jit(solution)/shard_map/ppermute | solution.py:432
  10.0 5.8 %spectra.3 = (bf16[3,256,128]{2,1,0:T(8,128)(2,1)}, bf16[1,256,128]{2,1,0:T(8,128)(2,1)}) custom-call(bf16[8,256,2048]{2,1,0:T(8,128)(2,1)} %refs_0_.3, s32[8,256]{1,0:T(8,128)} %refs_1_.3, bf16[2048,256]{1,0:T(8,128)(2,1)} %constant.24.clone.refs_2_, bf16[128,256]{1,0:T(8,128)(2,1)} %get-tuple-element.22.refs_3_, bf16[512,128]{1,0:T(8,128)(2,1)} %get-tuple-element.23.refs_4_), custom_call_target="tpu_custom_call" | custom-call | flops 1073741824 | bytes 4194304 | tf_op jit(solution)/shard_map/spectra/pallas_call | solution.py:174
  15.8 1.6 %collective-permute-start.12 = (bf16[1,256,128]{2,1,0:T(8,128)(2,1)}, bf16[1,256,128]{2,1,0:T(8,128)(2,1)S(1)}, u32[]{:S(2)}, u32[]{:S(2)}) collective-permute-start(bf16[1,256,128]{2,1,0:T(8,128)(2,1)} %get-tuple-element.30.refs_8_), channel_id=1, source_target_pairs={{0,8},{1,9},{2,10},{3,11},{4,0},{5,1},{6,2},{7,3},{8,12},{9,13},{1... | collective-permute-start | bytes 196616 | tf_op jit(solution)/shard_map/ppermute | solution.py:432
  17.4 0.3 collective-permute-start.3
  17.8 3.3 %collective-permute-done.12.refs_9_ = bf16[1,256,128]{2,1,0:T(8,128)(2,1)S(1)} collective-permute-done((bf16[1,256,128]{2,1,0:T(8,128)(2,1)}, bf16[1,256,128]{2,1,0:T(8,128)(2,1)S(1)}, u32[]{:S(2)}, u32[]{:S(2)}) %collective-permute-start.12) | collective-permute-done | bytes 65568 | tf_op jit(solution)/shard_map/ppermute | solution.py:432
  21.0 2.5 %collective-permute-start.13 = (bf16[1,256,128]{2,1,0:T(8,128)(2,1)S(1)}, bf16[1,256,128]{2,1,0:T(8,128)(2,1)S(1)}, u32[]{:S(2)}, u32[]{:S(2)}) collective-permute-start(bf16[1,256,128]{2,1,0:T(8,128)(2,1)S(1)} %collective-permute-done.12.refs_9_), channel_id=1, source_target_pairs={{0,8},{1,9},{2,10},{3,11},{4,0},{5,1},{6,2},{7,3},{8,12},{9,13},{1... | collective-permute-start | bytes 196616 | tf_op jit(solution)/shard_map/ppermute | solution.py:432
  23.5 2.1 %rows_for.6 = (bf16[3,4,16,2,4,256]{5,4,3,2,1,0:T(4,128)(2,1)}, bf16[1,4,16,2,4,256]{5,4,3,2,1,0:T(4,128)(2,1)}) custom-call(bf16[4,16,2,4,4096]{4,3,2,1,0:T(4,128)(2,1)} %bitcast.5), custom_call_target="tpu_custom_call" | custom-call | tf_op jit(solution)/shard_map/rows_for/pallas_call | solution.py:250
  25.6 1.6 %collective-permute-start.10 = (bf16[1,4,16,2,4,256]{5,4,3,2,1,0:T(4,128)(2,1)}, bf16[1,4,16,2,4,256]{5,4,3,2,1,0:T(4,128)(2,1)S(1)}, u32[]{:S(2)}, u32[]{:S(2)}) collective-permute-start(bf16[1,4,16,2,4,256]{5,4,3,2,1,0:T(4,128)(2,1)} %get-tuple-element.28), channel_id=1, source_target_pairs={{0,2},{1,3},{2,0},{3,1},{4,6},{5,7},{6,4},{7,5},{8,10},{9,11},{10,... | collective-permute-start | bytes 786440 | tf_op jit(solution)/shard_map/ppermute | solution.py:419
  27.2 1.5 %collective-permute-start.14 = (bf16[1,256,128]{2,1,0:T(8,128)(2,1)S(1)}, bf16[1,256,128]{2,1,0:T(8,128)(2,1)S(1)}, u32[]{:S(2)}, u32[]{:S(2)}) collective-permute-start(bf16[1,256,128]{2,1,0:T(8,128)(2,1)S(1)} %collective-permute-done.13.refs_10_), channel_id=1, source_target_pairs={{0,8},{1,9},{2,10},{3,11},{4,0},{5,1},{6,2},{7,3},{8,12},{9,13},{1... | collective-permute-start | bytes 196616 | tf_op jit(solution)/shard_map/ppermute | solution.py:432
  28.7 2.1 %rows_for.7 = (bf16[3,4,16,2,4,256]{5,4,3,2,1,0:T(4,128)(2,1)}, bf16[1,4,16,2,4,256]{5,4,3,2,1,0:T(4,128)(2,1)}) custom-call(bf16[4,16,2,4,4096]{4,3,2,1,0:T(4,128)(2,1)} %bitcast.6), custom_call_target="tpu_custom_call" | custom-call | tf_op jit(solution)/shard_map/rows_for/pallas_call | solution.py:250
  30.9 2.1 %rows_for.5 = (bf16[3,4,16,2,4,256]{5,4,3,2,1,0:T(4,128)(2,1)}, bf16[1,4,16,2,4,256]{5,4,3,2,1,0:T(4,128)(2,1)}) custom-call(bf16[4,16,2,4,4096]{4,3,2,1,0:T(4,128)(2,1)} %bitcast.7), custom_call_target="tpu_custom_call" | custom-call | tf_op jit(solution)/shard_map/rows_for/pallas_call | solution.py:250
  33.0 0.6 copy-done.25
  33.6 1.6 %collective-permute-start = (bf16[3,4,16,2,4,256]{5,4,3,2,1,0:T(4,128)(2,1)}, bf16[3,4,16,2,4,256]{5,4,3,2,1,0:T(4,128)(2,1)S(1)}, u32[]{:S(2)}, u32[]{:S(2)}) collective-permute-start(bf16[3,4,16,2,4,256]{5,4,3,2,1,0:T(4,128)(2,1)} %get-tuple-element.19), channel_id=1, source_target_pairs={{0,1},{1,0},{2,3},{3,2},{4,5},{5,4},{6,7},{7,6},{8,9},{9,8},{10,11... | collective-permute-start | bytes 2359304 | tf_op jit(solution)/shard_map/ppermute | solution.py:418
  35.2 0.7 copy-done.12
  35.9 0.5 collective-permute-start.1
  36.4 0.8 collective-permute-start.2
  37.3 0.7 copy-done.4
  38.0 0.8 collective-permute-start.9
  38.8 0.8 collective-permute-done.11.refs_3_
  39.6 0.7 copy-done.6
  40.3 0.7 copy-done.8
  41.0 0.9 collective-permute-start.4
  41.9 7.5 %collective-permute-done.7.refs_3_.refs_6_ = bf16[4,256,128]{2,1,0:T(8,128)(2,1)S(1)} collective-permute-done((bf16[4,256,128]{2,1,0:T(8,128)(2,1)S(1)}, bf16[4,256,128]{2,1,0:T(8,128)(2,1)S(1)}, u32[]{:S(2)}, u32[]{:S(2)}) %collective-permute-start.7) | collective-permute-done | bytes 262176 | tf_op jit(solution)/shard_map/ppermute | solution.py:432
  49.5 0.9 %collective-permute-start.8 = (bf16[4,256,128]{2,1,0:T(8,128)(2,1)S(1)}, bf16[4,256,128]{2,1,0:T(8,128)(2,1)S(1)}, u32[]{:S(2)}, u32[]{:S(2)}) collective-permute-start(bf16[4,256,128]{2,1,0:T(8,128)(2,1)S(1)} %collective-permute-done.7.refs_3_.refs_6_), channel_id=1, source_target_pairs={{0,8},{1,9},{2,10},{3,11},{4,0},{5,1},{6,2},{7,3},{8,12},{9,13},{1... | collective-permute-start | bytes 786440 | tf_op jit(solution)/shard_map/ppermute | solution.py:432
  50.4 3.4 %collective-permute-done.4.refs_3_ = bf16[3,256,128]{2,1,0:T(8,128)(2,1)} collective-permute-done((bf16[3,256,128]{2,1,0:T(8,128)(2,1)}, bf16[3,256,128]{2,1,0:T(8,128)(2,1)}, u32[]{:S(2)}, u32[]{:S(2)}) %collective-permute-start.4) | collective-permute-done | bytes 196640 | tf_op jit(solution)/shard_map/ppermute | solution.py:432
  53.8 0.9 %collective-permute-start.5 = (bf16[3,256,128]{2,1,0:T(8,128)(2,1)}, bf16[3,256,128]{2,1,0:T(8,128)(2,1)}, u32[]{:S(2)}, u32[]{:S(2)}) collective-permute-start(bf16[3,256,128]{2,1,0:T(8,128)(2,1)} %collective-permute-done.4.refs_3_), channel_id=1, source_target_pairs={{0,8},{1,9},{2,10},{3,11},{4,0},{5,1},{6,2},{7,3},{8,12},{9,13},{1... | collective-permute-start | bytes 589832 | tf_op jit(solution)/shard_map/ppermute | solution.py:432
  54.7 2.1 %rows_for.4 = (bf16[3,4,16,2,4,256]{5,4,3,2,1,0:T(4,128)(2,1)}, bf16[1,4,16,2,4,256]{5,4,3,2,1,0:T(4,128)(2,1)}) custom-call(bf16[4,16,2,4,4096]{4,3,2,1,0:T(4,128)(2,1)} %bitcast.8), custom_call_target="tpu_custom_call" | custom-call | tf_op jit(solution)/shard_map/rows_for/pallas_call | solution.py:250
  56.8 2.5 %collective-permute-done.8.refs_4_.refs_7_ = bf16[4,256,128]{2,1,0:T(8,128)(2,1)S(1)} collective-permute-done((bf16[4,256,128]{2,1,0:T(8,128)(2,1)S(1)}, bf16[4,256,128]{2,1,0:T(8,128)(2,1)S(1)}, u32[]{:S(2)}, u32[]{:S(2)}) %collective-permute-start.8) | collective-permute-done | bytes 262176 | tf_op jit(solution)/shard_map/ppermute | solution.py:432
  59.3 0.9 %copy-done.3 = f32[256,256]{1,0:T(8,128)S(1)} copy-done((f32[256,256]{1,0:T(8,128)S(1)}, f32[256,256]{1,0:T(8,128)}, u32[]{:S(2)}) %copy-start.3) | copy-done | bytes 262168
  60.3 0.9 %copy-done.5 = bf16[1,4,16,2,4,256]{5,4,3,2,1,0:T(4,128)(2,1)S(1)} copy-done((bf16[1,4,16,2,4,256]{5,4,3,2,1,0:T(4,128)(2,1)S(1)}, bf16[1,4,16,2,4,256]{5,4,3,2,1,0:T(4,128)(2,1)}, u32[]{:S(2)}) %copy-start.5) | copy-done | bytes 262168
  61.2 0.9 %copy-done.7 = bf16[1,4,16,2,4,256]{5,4,3,2,1,0:T(4,128)(2,1)S(1)} copy-done((bf16[1,4,16,2,4,256]{5,4,3,2,1,0:T(4,128)(2,1)S(1)}, bf16[1,4,16,2,4,256]{5,4,3,2,1,0:T(4,128)(2,1)}, u32[]{:S(2)}) %copy-start.7) | copy-done | bytes 262168
  62.2 0.9 %copy-done.9 = bf16[1,4,16,2,4,256]{5,4,3,2,1,0:T(4,128)(2,1)S(1)} copy-done((bf16[1,4,16,2,4,256]{5,4,3,2,1,0:T(4,128)(2,1)S(1)}, bf16[1,4,16,2,4,256]{5,4,3,2,1,0:T(4,128)(2,1)}, u32[]{:S(2)}) %copy-start.9) | copy-done | bytes 262168
  63.1 0.9 %copy-done.10 = bf16[1,4,16,2,4,256]{5,4,3,2,1,0:T(4,128)(2,1)S(1)} copy-done((bf16[1,4,16,2,4,256]{5,4,3,2,1,0:T(4,128)(2,1)S(1)}, bf16[1,4,16,2,4,256]{5,4,3,2,1,0:T(4,128)(2,1)}, u32[]{:S(2)}) %copy-start.10) | copy-done | bytes 262168
  64.1 0.8 copy-done.20
  64.9 0.8 copy-done.22
  65.7 0.8 copy-done.24
  66.6 0.8 copy-done.26
  67.4 0.9 predict.5
  68.3 5.0 %collective-permute-done.2.refs_3_ = bf16[3,4,16,2,4,256]{5,4,3,2,1,0:T(4,128)(2,1)S(1)} collective-permute-done((bf16[3,4,16,2,4,256]{5,4,3,2,1,0:T(4,128)(2,1)}, bf16[3,4,16,2,4,256]{5,4,3,2,1,0:T(4,128)(2,1)S(1)}, u32[]{:S(2)}, u32[]{:S(2)}) %collective-permute-start.2) | collective-permute-done | bytes 786464 | tf_op jit(solution)/shard_map/ppermute | solution.py:418
  73.3 1.1 %copy-done.1 = bf16[3,4,16,2,4,256]{5,4,3,2,1,0:T(4,128)(2,1)S(1)} copy-done((bf16[3,4,16,2,4,256]{5,4,3,2,1,0:T(4,128)(2,1)S(1)}, bf16[3,4,16,2,4,256]{5,4,3,2,1,0:T(4,128)(2,1)}, u32[]{:S(2)}) %copy-start.1) | copy-done | bytes 786456
  74.4 0.8 merge.1.refs_0_
  75.3 2.2 %predict.3.refs_8_ = bf16[12,16,64]{2,1,0:T(8,128)(2,1)S(1)} custom-call(bf16[3,512,1024]{2,1,0:T(8,128)(2,1)S(1)} %merge.1.refs_0_, bf16[4,256,128]{2,1,0:T(8,128)(2,1)S(1)} %copy-done, bf16[4,256,128]{2,1,0:T(8,128)(2,1)S(1)} %collective-permute-done.6.refs_2_.refs_5_, bf16[4,256,128]{2,1,0:T(8,128)(2,1)S(1)} %collective-permute-done.7.refs_3_.refs_6_, ...), custom_call_target="tpu_custom_call" | custom-call | tf_op jit(solution)/shard_map/predict/pallas_call | solution.py:368
  77.6 3.3 %predict.4 = bf16[12,16,64]{2,1,0:T(8,128)(2,1)S(1)} custom-call(bf16[3,512,1024]{2,1,0:T(8,128)(2,1)S(1)} %merge.1.refs_0_, bf16[3,256,128]{2,1,0:T(8,128)(2,1)S(1)} %copy-done.11, bf16[3,256,128]{2,1,0:T(8,128)(2,1)S(1)} %copy-done.13, bf16[3,256,128]{2,1,0:T(8,128)(2,1)} %collective-permute-done.4.refs_3_, ...), custom_call_target="tpu_custom_call" | custom-call | tf_op jit(solution)/shard_map/predict/pallas_call | solution.py:368
  80.9 0.1 reshape.15
  81.0 9.2 %all_to_all.5 = bf16[16,2,512]{2,1,0:T(2,128)(2,1)S(1)} all-to-all(bf16[16,2,512]{2,1,0:T(2,128)(2,1)S(1)} %reshape.15), channel_id=1, replica_groups=mesh['parts'=2,'rows'=16] {'rows'}, dimensions={0} | all-to-all | bytes 65536 | tf_op jit(solution)/shard_map/all_to_all | solution.py:447
  90.2 0.1 reshape.16
  90.3 0.8 convolution_convert_fusion
  (53 shorter events, 0.2 us)
Async XLA Ops:
  5.9 30.6 %collective-permute-start.6 = (bf16[4,256,128]{2,1,0:T(8,128)(2,1)}, bf16[4,256,128]{2,1,0:T(8,128)(2,1)S(1)}, u32[]{:S(2)}, u32[]{:S(2)}) collective-permute-start(bf16[4,256,128]{2,1,0:T(8,128)(2,1)} %get-tuple-element.25.refs_1_.refs_4_), channel_id=1, source_target_pairs={{0,8},{1,9},{2,10},{3,11},{4,0},{5,1},{6,2},{7,3},{8,12},{9,13},{1... | collective-permute-start | bytes 786440 | tf_op jit(solution)/shard_map/ppermute | solution.py:432
  15.8 5.2 %collective-permute-start.12 = (bf16[1,256,128]{2,1,0:T(8,128)(2,1)}, bf16[1,256,128]{2,1,0:T(8,128)(2,1)S(1)}, u32[]{:S(2)}, u32[]{:S(2)}) collective-permute-start(bf16[1,256,128]{2,1,0:T(8,128)(2,1)} %get-tuple-element.30.refs_8_), channel_id=1, source_target_pairs={{0,8},{1,9},{2,10},{3,11},{4,0},{5,1},{6,2},{7,3},{8,12},{9,13},{1... | collective-permute-start | bytes 196616 | tf_op jit(solution)/shard_map/ppermute | solution.py:432
  17.4 17.8 %collective-permute-start.3 = (bf16[3,256,128]{2,1,0:T(8,128)(2,1)}, bf16[3,256,128]{2,1,0:T(8,128)(2,1)S(1)}, u32[]{:S(2)}, u32[]{:S(2)}) collective-permute-start(bf16[3,256,128]{2,1,0:T(8,128)(2,1)} %get-tuple-element.24.refs_1_), channel_id=1, source_target_pairs={{0,8},{1,9},{2,10},{3,11},{4,0},{5,1},{6,2},{7,3},{8,12},{9,13},{1... | collective-permute-start | bytes 589832 | tf_op jit(solution)/shard_map/ppermute | solution.py:432
  21.0 9.7 %copy-start.21 = (bf16[1,256,128]{2,1,0:T(8,128)(2,1)}, bf16[1,256,128]{2,1,0:T(8,128)(2,1)S(1)}, u32[]{:S(2)}) copy-start(bf16[1,256,128]{2,1,0:T(8,128)(2,1)S(1)} %collective-permute-done.12.refs_9_) | copy-start | bytes 196612
  21.0 6.1 %collective-permute-start.13 = (bf16[1,256,128]{2,1,0:T(8,128)(2,1)S(1)}, bf16[1,256,128]{2,1,0:T(8,128)(2,1)S(1)}, u32[]{:S(2)}, u32[]{:S(2)}) collective-permute-start(bf16[1,256,128]{2,1,0:T(8,128)(2,1)S(1)} %collective-permute-done.12.refs_9_), channel_id=1, source_target_pairs={{0,8},{1,9},{2,10},{3,11},{4,0},{5,1},{6,2},{7,3},{8,12},{9,13},{1... | collective-permute-start | bytes 196616 | tf_op jit(solution)/shard_map/ppermute | solution.py:432
  25.6 11.7 %collective-permute-start.10 = (bf16[1,4,16,2,4,256]{5,4,3,2,1,0:T(4,128)(2,1)}, bf16[1,4,16,2,4,256]{5,4,3,2,1,0:T(4,128)(2,1)S(1)}, u32[]{:S(2)}, u32[]{:S(2)}) collective-permute-start(bf16[1,4,16,2,4,256]{5,4,3,2,1,0:T(4,128)(2,1)} %get-tuple-element.28), channel_id=1, source_target_pairs={{0,2},{1,3},{2,0},{3,1},{4,6},{5,7},{6,4},{7,5},{8,10},{9,11},{10,... | collective-permute-start | bytes 786440 | tf_op jit(solution)/shard_map/ppermute | solution.py:419
  27.2 5.8 %copy-start.23 = (bf16[1,256,128]{2,1,0:T(8,128)(2,1)}, bf16[1,256,128]{2,1,0:T(8,128)(2,1)S(1)}, u32[]{:S(2)}) copy-start(bf16[1,256,128]{2,1,0:T(8,128)(2,1)S(1)} %collective-permute-done.13.refs_10_) | copy-start | bytes 196612
  27.2 5.8 %collective-permute-start.14 = (bf16[1,256,128]{2,1,0:T(8,128)(2,1)S(1)}, bf16[1,256,128]{2,1,0:T(8,128)(2,1)S(1)}, u32[]{:S(2)}, u32[]{:S(2)}) collective-permute-start(bf16[1,256,128]{2,1,0:T(8,128)(2,1)S(1)} %collective-permute-done.13.refs_10_), channel_id=1, source_target_pairs={{0,8},{1,9},{2,10},{3,11},{4,0},{5,1},{6,2},{7,3},{8,12},{9,13},{1... | collective-permute-start | bytes 196616 | tf_op jit(solution)/shard_map/ppermute | solution.py:432
  30.7 28.6 %copy-start = (bf16[4,256,128]{2,1,0:T(8,128)(2,1)S(1)}, bf16[4,256,128]{2,1,0:T(8,128)(2,1)}, u32[]{:S(2)}) copy-start(bf16[4,256,128]{2,1,0:T(8,128)(2,1)} %get-tuple-element.25.refs_1_.refs_4_) | copy-start | bytes 786436
  30.8 28.5 %copy-start.18 = (bf16[1,256,64]{2,1,0:T(8,128)(2,1)S(1)}, bf16[1,256,64]{2,1,0:T(8,128)(2,1)}, u32[]{:S(2)}) copy-start(bf16[1,256,64]{2,1,0:T(8,128)(2,1)} %constant.33.clone.refs_13_) | copy-start | bytes 98308
  30.8 28.5 %copy-start.19 = (bf16[1,256,64]{2,1,0:T(8,128)(2,1)S(1)}, bf16[1,256,64]{2,1,0:T(8,128)(2,1)}, u32[]{:S(2)}) copy-start(bf16[1,256,64]{2,1,0:T(8,128)(2,1)} %constant.34.clone.refs_14_) | copy-start | bytes 98308
  30.8 8.8 %collective-permute-start.11 = (bf16[1,4,16,2,4,256]{5,4,3,2,1,0:T(4,128)(2,1)}, bf16[1,4,16,2,4,256]{5,4,3,2,1,0:T(4,128)(2,1)S(1)}, u32[]{:S(2)}, u32[]{:S(2)}) collective-permute-start(bf16[1,4,16,2,4,256]{5,4,3,2,1,0:T(4,128)(2,1)} %get-tuple-element.29), channel_id=1, source_target_pairs={{0,3},{1,2},{2,1},{3,0},{4,7},{5,6},{6,5},{7,4},{8,11},{9,10},{10,... | collective-permute-start | bytes 786440 | tf_op jit(solution)/shard_map/ppermute | solution.py:419
  33.0 0.6 copy-start.25
  33.6 34.7 %collective-permute-start = (bf16[3,4,16,2,4,256]{5,4,3,2,1,0:T(4,128)(2,1)}, bf16[3,4,16,2,4,256]{5,4,3,2,1,0:T(4,128)(2,1)S(1)}, u32[]{:S(2)}, u32[]{:S(2)}) collective-permute-start(bf16[3,4,16,2,4,256]{5,4,3,2,1,0:T(4,128)(2,1)} %get-tuple-element.19), channel_id=1, source_target_pairs={{0,1},{1,0},{2,3},{3,2},{4,5},{5,4},{6,7},{7,6},{8,9},{9,8},{10,11... | collective-permute-start | bytes 2359304 | tf_op jit(solution)/shard_map/ppermute | solution.py:418
  35.2 0.7 copy-start.12
  35.9 32.4 %collective-permute-start.1 = (bf16[3,4,16,2,4,256]{5,4,3,2,1,0:T(4,128)(2,1)}, bf16[3,4,16,2,4,256]{5,4,3,2,1,0:T(4,128)(2,1)S(1)}, u32[]{:S(2)}, u32[]{:S(2)}) collective-permute-start(bf16[3,4,16,2,4,256]{5,4,3,2,1,0:T(4,128)(2,1)} %get-tuple-element.20), channel_id=1, source_target_pairs={{0,2},{1,3},{2,0},{3,1},{4,6},{5,7},{6,4},{7,5},{8,10},{9,11},{10,... | collective-permute-start | bytes 2359304 | tf_op jit(solution)/shard_map/ppermute | solution.py:418
  36.4 36.9 %collective-permute-start.2 = (bf16[3,4,16,2,4,256]{5,4,3,2,1,0:T(4,128)(2,1)}, bf16[3,4,16,2,4,256]{5,4,3,2,1,0:T(4,128)(2,1)S(1)}, u32[]{:S(2)}, u32[]{:S(2)}) collective-permute-start(bf16[3,4,16,2,4,256]{5,4,3,2,1,0:T(4,128)(2,1)} %get-tuple-element.21), channel_id=1, source_target_pairs={{0,3},{1,2},{2,1},{3,0},{4,7},{5,6},{6,5},{7,4},{8,11},{9,10},{10,... | collective-permute-start | bytes 2359304 | tf_op jit(solution)/shard_map/ppermute | solution.py:418
  37.3 0.7 copy-start.4
  38.0 2.3 %collective-permute-start.9 = (bf16[1,4,16,2,4,256]{5,4,3,2,1,0:T(4,128)(2,1)}, bf16[1,4,16,2,4,256]{5,4,3,2,1,0:T(4,128)(2,1)S(1)}, u32[]{:S(2)}, u32[]{:S(2)}) collective-permute-start(bf16[1,4,16,2,4,256]{5,4,3,2,1,0:T(4,128)(2,1)} %get-tuple-element.27), channel_id=1, source_target_pairs={{0,1},{1,0},{2,3},{3,2},{4,5},{5,4},{6,7},{7,6},{8,9},{9,8},{10,11... | collective-permute-start | bytes 786440 | tf_op jit(solution)/shard_map/ppermute | solution.py:419
  39.6 0.7 copy-start.6
  40.3 9.2 %collective-permute-start.7 = (bf16[4,256,128]{2,1,0:T(8,128)(2,1)S(1)}, bf16[4,256,128]{2,1,0:T(8,128)(2,1)S(1)}, u32[]{:S(2)}, u32[]{:S(2)}) collective-permute-start(bf16[4,256,128]{2,1,0:T(8,128)(2,1)S(1)} %collective-permute-done.6.refs_2_.refs_5_), channel_id=1, source_target_pairs={{0,8},{1,9},{2,10},{3,11},{4,0},{5,1},{6,2},{7,3},{8,12},{9,13},{1... | collective-permute-start | bytes 786440 | tf_op jit(solution)/shard_map/ppermute | solution.py:432
  40.3 0.7 copy-start.8
  41.0 12.8 %collective-permute-start.4 = (bf16[3,256,128]{2,1,0:T(8,128)(2,1)}, bf16[3,256,128]{2,1,0:T(8,128)(2,1)}, u32[]{:S(2)}, u32[]{:S(2)}) collective-permute-start(bf16[3,256,128]{2,1,0:T(8,128)(2,1)} %copy-done.12), channel_id=1, source_target_pairs={{0,8},{1,9},{2,10},{3,11},{4,0},{5,1},{6,2},{7,3},{8,12},{9,13},{1... | collective-permute-start | bytes 589832 | tf_op jit(solution)/shard_map/ppermute | solution.py:432
  49.5 9.8 %collective-permute-start.8 = (bf16[4,256,128]{2,1,0:T(8,128)(2,1)S(1)}, bf16[4,256,128]{2,1,0:T(8,128)(2,1)S(1)}, u32[]{:S(2)}, u32[]{:S(2)}) collective-permute-start(bf16[4,256,128]{2,1,0:T(8,128)(2,1)S(1)} %collective-permute-done.7.refs_3_.refs_6_), channel_id=1, source_target_pairs={{0,8},{1,9},{2,10},{3,11},{4,0},{5,1},{6,2},{7,3},{8,12},{9,13},{1... | collective-permute-start | bytes 786440 | tf_op jit(solution)/shard_map/ppermute | solution.py:432
  53.8 23.8 %collective-permute-start.5 = (bf16[3,256,128]{2,1,0:T(8,128)(2,1)}, bf16[3,256,128]{2,1,0:T(8,128)(2,1)}, u32[]{:S(2)}, u32[]{:S(2)}) collective-permute-start(bf16[3,256,128]{2,1,0:T(8,128)(2,1)} %collective-permute-done.4.refs_3_), channel_id=1, source_target_pairs={{0,8},{1,9},{2,10},{3,11},{4,0},{5,1},{6,2},{7,3},{8,12},{9,13},{1... | collective-permute-start | bytes 589832 | tf_op jit(solution)/shard_map/ppermute | solution.py:432
  59.3 1.0 %copy-start.3 = (f32[256,256]{1,0:T(8,128)S(1)}, f32[256,256]{1,0:T(8,128)}, u32[]{:S(2)}) copy-start(f32[256,256]{1,0:T(8,128)} %constant.32.clone.refs_12_) | copy-start | bytes 786436
  60.3 0.9 %copy-start.5 = (bf16[1,4,16,2,4,256]{5,4,3,2,1,0:T(4,128)(2,1)S(1)}, bf16[1,4,16,2,4,256]{5,4,3,2,1,0:T(4,128)(2,1)}, u32[]{:S(2)}) copy-start(bf16[1,4,16,2,4,256]{5,4,3,2,1,0:T(4,128)(2,1)} %copy-done.4) | copy-start | bytes 786436
  61.2 0.9 %copy-start.7 = (bf16[1,4,16,2,4,256]{5,4,3,2,1,0:T(4,128)(2,1)S(1)}, bf16[1,4,16,2,4,256]{5,4,3,2,1,0:T(4,128)(2,1)}, u32[]{:S(2)}) copy-start(bf16[1,4,16,2,4,256]{5,4,3,2,1,0:T(4,128)(2,1)} %copy-done.6) | copy-start | bytes 786436
  62.2 0.9 %copy-start.9 = (bf16[1,4,16,2,4,256]{5,4,3,2,1,0:T(4,128)(2,1)S(1)}, bf16[1,4,16,2,4,256]{5,4,3,2,1,0:T(4,128)(2,1)}, u32[]{:S(2)}) copy-start(bf16[1,4,16,2,4,256]{5,4,3,2,1,0:T(4,128)(2,1)} %copy-done.8) | copy-start | bytes 786436
  63.1 0.9 %copy-start.10 = (bf16[1,4,16,2,4,256]{5,4,3,2,1,0:T(4,128)(2,1)S(1)}, bf16[1,4,16,2,4,256]{5,4,3,2,1,0:T(4,128)(2,1)}, u32[]{:S(2)}) copy-start(bf16[1,4,16,2,4,256]{5,4,3,2,1,0:T(4,128)(2,1)} %get-tuple-element.26.refs_0_) | copy-start | bytes 786436
  64.1 0.8 copy-start.20
  64.9 0.8 copy-start.22
  65.7 0.8 copy-start.24
  66.6 0.8 copy-start.26
  67.4 7.9 %copy-start.2 = (f32[256,128]{1,0:T(8,128)S(1)}, f32[256,128]{1,0:T(8,128)}, u32[]{:S(2)}) copy-start(f32[256,128]{1,0:T(8,128)} %constant.27.clone.refs_5_) | copy-start | bytes 393220
  67.4 7.9 %copy-start.16 = (bf16[3,128,64]{2,1,0:T(8,128)(2,1)S(1)}, bf16[3,128,64]{2,1,0:T(8,128)(2,1)}, u32[]{:S(2)}) copy-start(bf16[3,128,64]{2,1,0:T(8,128)(2,1)} %constant.28.clone.refs_6_) | copy-start | bytes 147460
  67.4 7.9 %copy-start.17 = (bf16[3,128,64]{2,1,0:T(8,128)(2,1)S(1)}, bf16[3,128,64]{2,1,0:T(8,128)(2,1)}, u32[]{:S(2)}) copy-start(bf16[3,128,64]{2,1,0:T(8,128)(2,1)} %constant.29.clone.refs_7_) | copy-start | bytes 147460
  73.3 1.1 %copy-start.1 = (bf16[3,4,16,2,4,256]{5,4,3,2,1,0:T(4,128)(2,1)S(1)}, bf16[3,4,16,2,4,256]{5,4,3,2,1,0:T(4,128)(2,1)}, u32[]{:S(2)}) copy-start(bf16[3,4,16,2,4,256]{5,4,3,2,1,0:T(4,128)(2,1)} %get-tuple-element.18.refs_0_) | copy-start | bytes 2359300
  74.4 3.2 %copy-start.11 = (bf16[3,256,128]{2,1,0:T(8,128)(2,1)S(1)}, bf16[3,256,128]{2,1,0:T(8,128)(2,1)}, u32[]{:S(2)}) copy-start(bf16[3,256,128]{2,1,0:T(8,128)(2,1)} %get-tuple-element.24.refs_1_) | copy-start | bytes 589828
  74.4 3.2 %copy-start.13 = (bf16[3,256,128]{2,1,0:T(8,128)(2,1)S(1)}, bf16[3,256,128]{2,1,0:T(8,128)(2,1)}, u32[]{:S(2)}) copy-start(bf16[3,256,128]{2,1,0:T(8,128)(2,1)} %copy-done.12) | copy-start | bytes 589828
  74.4 3.2 %copy-start.14 = (bf16[3,128,64]{2,1,0:T(8,128)(2,1)S(1)}, bf16[3,128,64]{2,1,0:T(8,128)(2,1)}, u32[]{:S(2)}) copy-start(bf16[3,128,64]{2,1,0:T(8,128)(2,1)} %constant.30.clone.refs_6_) | copy-start | bytes 147460
  74.4 3.2 %copy-start.15 = (bf16[3,128,64]{2,1,0:T(8,128)(2,1)S(1)}, bf16[3,128,64]{2,1,0:T(8,128)(2,1)}, u32[]{:S(2)}) copy-start(bf16[3,128,64]{2,1,0:T(8,128)(2,1)} %constant.31.clone.refs_7_) | copy-start | bytes 147460
  75.3 15.0 %copy-start.27 = (bf16[256,64]{1,0:T(8,128)(2,1)S(1)}, bf16[256,64]{1,0:T(8,128)(2,1)}, u32[]{:S(2)}) copy-start(bf16[256,64]{1,0:T(8,128)(2,1)} %constant.35.clone) | copy-start | bytes 98308

commit v4 on v3

--- a/solution.py
+++ b/solution.py
@@ -233,7 +233,7 @@
         copy.wait()
 
 
-def rows_for(data_matrix, starts, block, head):
+def rows_for(data_matrix, starts, block, head, limit=None):
     freqs, parts, rows, _ = data_matrix.shape
     bands = freqs // BAND
     slots = starts.shape[1]
@@ -260,6 +260,7 @@
             pltpu.SemaphoreType.DMA((slots,)),
             pltpu.SemaphoreType.DMA((slots, 2)),
         ],
+        compiler_params=pltpu.CompilerParams(vmem_limit_bytes=limit),
         name="rows_for",
     )(source)
 
@@ -412,7 +413,7 @@
     first_parts, rest_parts = [None] * members, [None] * members
 
     def exchange(m):
-        first, rest = rows_for(data_matrix, blocks[:, m], block, head)
+        first, rest = rows_for(data_matrix, blocks[:, m], block, head, (40 << 20) if m < 2 else None)
         pairs = [(i, i ^ m) for i in range(devices)]
         if m:
             first = lax.ppermute(first, "rows", pairs)

time: 91.9 us -> 89.1 us (0.970)
  waiting for transfers between devices: 22.5 us -> 33.6 us
  local copies, waits for them, and re-layouts: 12.9 us -> 2.47 us
  Pallas kernels: 27.2 us -> 24.2 us
    unnamed x58 -> x32, local copies, waits for them, and re-layouts: 12.9 us -> 2.47 us
    ppermute x3, waiting for transfers between devices: 4.97 us -> 13.7 us  [exchange(): first = lax.ppermute(first, 'rows', pairs)]
    pallas_call x4, Pallas kernels: 8.35 us -> 6.34 us  [rows_for(): pl.pallas_call(functools.partial(rows_kernel, block, head, starts), in_sp...]
    ppermute x9, waiting for transfers between devices: 16.7 us -> 18.3 us  [shards(): piece.append(lax.ppermute(piece[-1], 'rows', step))]
    pallas_call x3, Pallas kernels: 6.38 us -> 5.37 us  [predict(): pl.pallas_call(functools.partial(predict_kernel, len(matrix), parts, slot...]
  transfers between devices with their start and end apart: 15 -> 15, of which waited for: 6 -> 6; matrix products, arithmetic and copies ran while one was open for 0% -> 0% of each run, Pallas kernels for 20% -> 18%
where the time goes in v4:
time: 89.1 us; the launch traced here: 88.9 us
  waiting for transfers between devices  33.6 us (38%)
  Pallas kernels  24.2 us (27%)
  starting transfers between devices  18.4 us (21%)
  blocking collectives  9.2 us (10%)
  local copies, waits for them, and re-layouts  2.47 us (3%)
    ppermute x9, waiting for transfers between devices, shards(): piece.append(lax.ppermute(piece[-1], 'rows', step))  18.3 us
    ppermute x3, waiting for transfers between devices, exchange(): first = lax.ppermute(first, 'rows', pairs)  13.7 us
    ppermute x9, starting transfers between devices, shards(): piece.append(lax.ppermute(piece[-1], 'rows', step))  12.9 us
    pallas_call x2, Pallas kernels, spectra_of(): pl.pallas_call(functools.partial(spectra_kernel, bands, bins, taps, part,...  11.6 us
    all_to_all x1, blocking collectives, shards(): lax.all_to_all(partial_value, 'rows', split_axis=0, concat_axis=0, tiled=...  9.2 us
    pallas_call x4, Pallas kernels, rows_for(): pl.pallas_call(functools.partial(rows_kernel, block, head, starts), in_sp...  6.34 us
    pallas_call x3, Pallas kernels, predict(): pl.pallas_call(functools.partial(predict_kernel, len(matrix), parts, slot...  5.37 us
    ppermute x3, starting transfers between devices, exchange(): first = lax.ppermute(first, 'rows', pairs)  3.13 us
  transfers between devices with their start and end apart: 15, of which 6 were waited for; matrix products, arithmetic and copies ran while one was open for 0% of the time, Pallas kernels for 18%

profile of v4, /device:TPU:0, one launch (start us, length us, event | category | flops | bytes accessed | tf_op | source)
XLA Modules:
  0.0 88.9 jit_solution(12997381144757588199)
XLA Ops:
  0.0 5.8 %spectra.2 = (bf16[4,256,128]{2,1,0:T(8,128)(2,1)}, bf16[128,256]{1,0:T(8,128)(2,1)}, bf16[512,128]{1,0:T(8,128)(2,1)}) custom-call(bf16[8,256,2048]{2,1,0:T(8,128)(2,1)} %refs_0_.3, s32[8,256]{1,0:T(8,128)} %refs_1_.3, bf16[2048,256]{1,0:T(8,128)(2,1)} %constant.24.clone.refs_2_, f32[16,32]{1,0:T(8,128)} %refs_3_.1, f32[32,256]{1,0:T(8,128)} %constant.25.clone.refs_4_, ...), custom_call_target="tpu_custom_call" | custom-call | flops 1073741824 | bytes 4194304 | tf_op jit(solution)/shard_map/spectra/pallas_call | solution.py:174
  5.9 4.1 %collective-permute-start.6 = (bf16[4,256,128]{2,1,0:T(8,128)(2,1)}, bf16[4,256,128]{2,1,0:T(8,128)(2,1)S(1)}, u32[]{:S(2)}, u32[]{:S(2)}) collective-permute-start(bf16[4,256,128]{2,1,0:T(8,128)(2,1)} %get-tuple-element.25.refs_1_.refs_4_), channel_id=1, source_target_pairs={{0,8},{1,9},{2,10},{3,11},{4,0},{5,1},{6,2},{7,3},{8,12},{9,13},{1... | collective-permute-start | bytes 786440 | tf_op jit(solution)/shard_map/ppermute | solution.py:433
  10.0 5.8 %spectra.3 = (bf16[3,256,128]{2,1,0:T(8,128)(2,1)}, bf16[1,256,128]{2,1,0:T(8,128)(2,1)}) custom-call(bf16[8,256,2048]{2,1,0:T(8,128)(2,1)} %refs_0_.3, s32[8,256]{1,0:T(8,128)} %refs_1_.3, bf16[2048,256]{1,0:T(8,128)(2,1)} %constant.24.clone.refs_2_, bf16[128,256]{1,0:T(8,128)(2,1)} %get-tuple-element.22.refs_3_, bf16[512,128]{1,0:T(8,128)(2,1)} %get-tuple-element.23.refs_4_), custom_call_target="tpu_custom_call" | custom-call | flops 1073741824 | bytes 4194304 | tf_op jit(solution)/shard_map/spectra/pallas_call | solution.py:174
  15.8 1.6 %collective-permute-start.12 = (bf16[1,256,128]{2,1,0:T(8,128)(2,1)}, bf16[1,256,128]{2,1,0:T(8,128)(2,1)S(1)}, u32[]{:S(2)}, u32[]{:S(2)}) collective-permute-start(bf16[1,256,128]{2,1,0:T(8,128)(2,1)} %get-tuple-element.30.refs_8_), channel_id=1, source_target_pairs={{0,8},{1,9},{2,10},{3,11},{4,0},{5,1},{6,2},{7,3},{8,12},{9,13},{1... | collective-permute-start | bytes 196616 | tf_op jit(solution)/shard_map/ppermute | solution.py:433
  17.4 0.3 collective-permute-start.3
  17.7 3.3 %collective-permute-done.12.refs_9_ = bf16[1,256,128]{2,1,0:T(8,128)(2,1)S(1)} collective-permute-done((bf16[1,256,128]{2,1,0:T(8,128)(2,1)}, bf16[1,256,128]{2,1,0:T(8,128)(2,1)S(1)}, u32[]{:S(2)}, u32[]{:S(2)}) %collective-permute-start.12) | collective-permute-done | bytes 65568 | tf_op jit(solution)/shard_map/ppermute | solution.py:433
  21.0 2.5 %collective-permute-start.13 = (bf16[1,256,128]{2,1,0:T(8,128)(2,1)S(1)}, bf16[1,256,128]{2,1,0:T(8,128)(2,1)S(1)}, u32[]{:S(2)}, u32[]{:S(2)}) collective-permute-start(bf16[1,256,128]{2,1,0:T(8,128)(2,1)S(1)} %collective-permute-done.12.refs_9_), channel_id=1, source_target_pairs={{0,8},{1,9},{2,10},{3,11},{4,0},{5,1},{6,2},{7,3},{8,12},{9,13},{1... | collective-permute-start | bytes 196616 | tf_op jit(solution)/shard_map/ppermute | solution.py:433
  23.5 2.1 %rows_for.6 = (bf16[3,4,16,2,4,256]{5,4,3,2,1,0:T(4,128)(2,1)}, bf16[1,4,16,2,4,256]{5,4,3,2,1,0:T(4,128)(2,1)}) custom-call(bf16[4,16,2,4,4096]{4,3,2,1,0:T(4,128)(2,1)} %bitcast.5), custom_call_target="tpu_custom_call" | custom-call | tf_op jit(solution)/shard_map/rows_for/pallas_call | solution.py:250
  25.6 1.6 %collective-permute-start.10 = (bf16[1,4,16,2,4,256]{5,4,3,2,1,0:T(4,128)(2,1)}, bf16[1,4,16,2,4,256]{5,4,3,2,1,0:T(4,128)(2,1)S(1)}, u32[]{:S(2)}, u32[]{:S(2)}) collective-permute-start(bf16[1,4,16,2,4,256]{5,4,3,2,1,0:T(4,128)(2,1)} %get-tuple-element.28), channel_id=1, source_target_pairs={{0,2},{1,3},{2,0},{3,1},{4,6},{5,7},{6,4},{7,5},{8,10},{9,11},{10,... | collective-permute-start | bytes 786440 | tf_op jit(solution)/shard_map/ppermute | solution.py:420
  27.1 0.0 collective-permute-done.13.refs_10_
  27.1 1.5 %collective-permute-start.14 = (bf16[1,256,128]{2,1,0:T(8,128)(2,1)S(1)}, bf16[1,256,128]{2,1,0:T(8,128)(2,1)S(1)}, u32[]{:S(2)}, u32[]{:S(2)}) collective-permute-start(bf16[1,256,128]{2,1,0:T(8,128)(2,1)S(1)} %collective-permute-done.13.refs_10_), channel_id=1, source_target_pairs={{0,8},{1,9},{2,10},{3,11},{4,0},{5,1},{6,2},{7,3},{8,12},{9,13},{1... | collective-permute-start | bytes 196616 | tf_op jit(solution)/shard_map/ppermute | solution.py:433
  28.6 2.1 %rows_for.7 = (bf16[3,4,16,2,4,256]{5,4,3,2,1,0:T(4,128)(2,1)}, bf16[1,4,16,2,4,256]{5,4,3,2,1,0:T(4,128)(2,1)}) custom-call(bf16[4,16,2,4,4096]{4,3,2,1,0:T(4,128)(2,1)} %bitcast.6), custom_call_target="tpu_custom_call" | custom-call | tf_op jit(solution)/shard_map/rows_for/pallas_call | solution.py:250
  30.7 0.1 collective-permute-start.11
  30.8 0.0 copy-start
  30.8 2.2 %copy-done = bf16[64,2,4,4096]{3,2,1,0:T(4,128)(2,1)S(1)} copy-done((bf16[64,2,4,4096]{3,2,1,0:T(4,128)(2,1)S(1)}, bf16[64,2,4,4096]{3,2,1,0:T(4,128)(2,1)}, u32[]{:S(2)}) %copy-start) | copy-done | bytes 4194328
  33.0 0.0 copy-start.10
  33.0 1.1 %rows_for.5 = (bf16[3,4,16,2,4,256]{5,4,3,2,1,0:T(4,128)(2,1)S(1)}, bf16[1,4,16,2,4,256]{5,4,3,2,1,0:T(4,128)(2,1)S(1)}) custom-call(bf16[4,16,2,4,4096]{4,3,2,1,0:T(4,128)(2,1)S(1)} %bitcast.7), custom_call_target="tpu_custom_call" | custom-call | tf_op jit(solution)/shard_map/rows_for/pallas_call | solution.py:250
  34.2 1.7 %collective-permute-start = (bf16[3,4,16,2,4,256]{5,4,3,2,1,0:T(4,128)(2,1)S(1)}, bf16[3,4,16,2,4,256]{5,4,3,2,1,0:T(4,128)(2,1)S(1)}, u32[]{:S(2)}, u32[]{:S(2)}) collective-permute-start(bf16[3,4,16,2,4,256]{5,4,3,2,1,0:T(4,128)(2,1)S(1)} %get-tuple-element.19), channel_id=1, source_target_pairs={{0,1},{1,0},{2,3},{3,2},{4,5},{5,4},{6,7},{7,6},{8,9},{9,8},{10,11... | collective-permute-start | bytes 2359304 | tf_op jit(solution)/shard_map/ppermute | solution.py:419
  35.8 0.0 collective-permute-done.3.refs_2_
  35.8 0.5 collective-permute-start.1
  36.4 0.0 collective-permute-done.6.refs_2_.refs_5_
  36.4 0.9 %collective-permute-start.2 = (bf16[3,4,16,2,4,256]{5,4,3,2,1,0:T(4,128)(2,1)S(1)}, bf16[3,4,16,2,4,256]{5,4,3,2,1,0:T(4,128)(2,1)S(1)}, u32[]{:S(2)}, u32[]{:S(2)}) collective-permute-start(bf16[3,4,16,2,4,256]{5,4,3,2,1,0:T(4,128)(2,1)S(1)} %copy-done.14), channel_id=1, source_target_pairs={{0,3},{1,2},{2,1},{3,0},{4,7},{5,6},{6,5},{7,4},{8,11},{9,10},{10,... | collective-permute-start | bytes 2359304 | tf_op jit(solution)/shard_map/ppermute | solution.py:419
  37.3 0.7 collective-permute-start.9
  38.0 1.5 %collective-permute-done.11.refs_3_ = bf16[1,4,16,2,4,256]{5,4,3,2,1,0:T(4,128)(2,1)S(1)} collective-permute-done((bf16[1,4,16,2,4,256]{5,4,3,2,1,0:T(4,128)(2,1)}, bf16[1,4,16,2,4,256]{5,4,3,2,1,0:T(4,128)(2,1)S(1)}, u32[]{:S(2)}, u32[]{:S(2)}) %collective-permute-start.11) | collective-permute-done | bytes 262176 | tf_op jit(solution)/shard_map/ppermute | solution.py:420
  39.5 0.0 collective-permute-start.7
  39.5 0.0 collective-permute-done.9.refs_1_
  39.5 1.0 %collective-permute-start.4 = (bf16[3,256,128]{2,1,0:T(8,128)(2,1)S(1)}, bf16[3,256,128]{2,1,0:T(8,128)(2,1)S(1)}, u32[]{:S(2)}, u32[]{:S(2)}) collective-permute-start(bf16[3,256,128]{2,1,0:T(8,128)(2,1)S(1)} %collective-permute-done.3.refs_2_), channel_id=1, source_target_pairs={{0,8},{1,9},{2,10},{3,11},{4,0},{5,1},{6,2},{7,3},{8,12},{9,13},{1... | collective-permute-start | bytes 589832 | tf_op jit(solution)/shard_map/ppermute | solution.py:433
  40.6 8.1 %collective-permute-done.7.refs_3_.refs_6_ = bf16[4,256,128]{2,1,0:T(8,128)(2,1)S(1)} collective-permute-done((bf16[4,256,128]{2,1,0:T(8,128)(2,1)S(1)}, bf16[4,256,128]{2,1,0:T(8,128)(2,1)S(1)}, u32[]{:S(2)}, u32[]{:S(2)}) %collective-permute-start.7) | collective-permute-done | bytes 262176 | tf_op jit(solution)/shard_map/ppermute | solution.py:433
  48.7 0.9 %collective-permute-start.8 = (bf16[4,256,128]{2,1,0:T(8,128)(2,1)S(1)}, bf16[4,256,128]{2,1,0:T(8,128)(2,1)S(1)}, u32[]{:S(2)}, u32[]{:S(2)}) collective-permute-start(bf16[4,256,128]{2,1,0:T(8,128)(2,1)S(1)} %collective-permute-done.7.refs_3_.refs_6_), channel_id=1, source_target_pairs={{0,8},{1,9},{2,10},{3,11},{4,0},{5,1},{6,2},{7,3},{8,12},{9,13},{1... | collective-permute-start | bytes 786440 | tf_op jit(solution)/shard_map/ppermute | solution.py:433
  49.6 3.3 %collective-permute-done.4.refs_3_ = bf16[3,256,128]{2,1,0:T(8,128)(2,1)S(1)} collective-permute-done((bf16[3,256,128]{2,1,0:T(8,128)(2,1)S(1)}, bf16[3,256,128]{2,1,0:T(8,128)(2,1)S(1)}, u32[]{:S(2)}, u32[]{:S(2)}) %collective-permute-start.4) | collective-permute-done | bytes 196640 | tf_op jit(solution)/shard_map/ppermute | solution.py:433
  52.9 0.9 %collective-permute-start.5 = (bf16[3,256,128]{2,1,0:T(8,128)(2,1)S(1)}, bf16[3,256,128]{2,1,0:T(8,128)(2,1)S(1)}, u32[]{:S(2)}, u32[]{:S(2)}) collective-permute-start(bf16[3,256,128]{2,1,0:T(8,128)(2,1)S(1)} %collective-permute-done.4.refs_3_), channel_id=1, source_target_pairs={{0,8},{1,9},{2,10},{3,11},{4,0},{5,1},{6,2},{7,3},{8,12},{9,13},{1... | collective-permute-start | bytes 589832 | tf_op jit(solution)/shard_map/ppermute | solution.py:433
  53.8 1.1 %rows_for.4 = (bf16[3,4,16,2,4,256]{5,4,3,2,1,0:T(4,128)(2,1)S(1)}, bf16[1,4,16,2,4,256]{5,4,3,2,1,0:T(4,128)(2,1)S(1)}) custom-call(bf16[4,16,2,4,4096]{4,3,2,1,0:T(4,128)(2,1)S(1)} %bitcast.8), custom_call_target="tpu_custom_call" | custom-call | tf_op jit(solution)/shard_map/rows_for/pallas_call | solution.py:250
  54.9 3.6 %collective-permute-done.8.refs_4_.refs_7_ = bf16[4,256,128]{2,1,0:T(8,128)(2,1)S(1)} collective-permute-done((bf16[4,256,128]{2,1,0:T(8,128)(2,1)S(1)}, bf16[4,256,128]{2,1,0:T(8,128)(2,1)S(1)}, u32[]{:S(2)}, u32[]{:S(2)}) %collective-permute-start.8) | collective-permute-done | bytes 262176 | tf_op jit(solution)/shard_map/ppermute | solution.py:433
  58.6 0.0 copy-start.2
  58.6 0.0 copy-start.7
  58.6 0.0 copy-start.8
  58.6 0.9 predict.5
  59.5 0.0 collective-permute-done.refs_1_
  59.5 0.0 collective-permute-done.1.refs_2_
  59.5 13.7 %collective-permute-done.2.refs_3_ = bf16[3,4,16,2,4,256]{5,4,3,2,1,0:T(4,128)(2,1)S(1)} collective-permute-done((bf16[3,4,16,2,4,256]{5,4,3,2,1,0:T(4,128)(2,1)S(1)}, bf16[3,4,16,2,4,256]{5,4,3,2,1,0:T(4,128)(2,1)S(1)}, u32[]{:S(2)}, u32[]{:S(2)}) %collective-permute-start.2) | collective-permute-done | bytes 786464 | tf_op jit(solution)/shard_map/ppermute | solution.py:419
  73.2 0.8 merge.1.refs_0_
  74.1 0.0 copy-start.12
  74.1 2.2 %predict.3.refs_8_ = bf16[12,16,64]{2,1,0:T(8,128)(2,1)S(1)} custom-call(bf16[3,512,1024]{2,1,0:T(8,128)(2,1)S(1)} %merge.1.refs_0_, bf16[4,256,128]{2,1,0:T(8,128)(2,1)S(1)} %copy-done.1, bf16[4,256,128]{2,1,0:T(8,128)(2,1)S(1)} %collective-permute-done.6.refs_2_.refs_5_, bf16[4,256,128]{2,1,0:T(8,128)(2,1)S(1)} %collective-permute-done.7.refs_3_.refs_6_, ...), custom_call_target="tpu_custom_call" | custom-call | tf_op jit(solution)/shard_map/predict/pallas_call | solution.py:369
  76.4 2.2 %predict.4 = bf16[12,16,64]{2,1,0:T(8,128)(2,1)S(1)} custom-call(bf16[3,512,1024]{2,1,0:T(8,128)(2,1)S(1)} %merge.1.refs_0_, bf16[3,256,128]{2,1,0:T(8,128)(2,1)S(1)} %copy-done.4, bf16[3,256,128]{2,1,0:T(8,128)(2,1)S(1)} %collective-permute-done.3.refs_2_, bf16[3,256,128]{2,1,0:T(8,128)(2,1)S(1)} %collective-permute-done.4.refs_3_, ...), custom_call_target="tpu_custom_call" | custom-call | tf_op jit(solution)/shard_map/predict/pallas_call | solution.py:369
  78.7 0.1 reshape.15
  78.8 9.2 %all_to_all.5 = bf16[16,2,512]{2,1,0:T(2,128)(2,1)S(1)} all-to-all(bf16[16,2,512]{2,1,0:T(2,128)(2,1)S(1)} %reshape.15), channel_id=1, replica_groups=mesh['parts'=2,'rows'=16] {'rows'}, dimensions={0} | all-to-all | bytes 65536 | tf_op jit(solution)/shard_map/all_to_all | solution.py:448
  88.0 0.1 reshape.16
  88.1 0.8 convolution_convert_fusion
  (27 shorter events, 0.1 us)
Async XLA Ops:
  5.9 30.5 %collective-permute-start.6 = (bf16[4,256,128]{2,1,0:T(8,128)(2,1)}, bf16[4,256,128]{2,1,0:T(8,128)(2,1)S(1)}, u32[]{:S(2)}, u32[]{:S(2)}) collective-permute-start(bf16[4,256,128]{2,1,0:T(8,128)(2,1)} %get-tuple-element.25.refs_1_.refs_4_), channel_id=1, source_target_pairs={{0,8},{1,9},{2,10},{3,11},{4,0},{5,1},{6,2},{7,3},{8,12},{9,13},{1... | collective-permute-start | bytes 786440 | tf_op jit(solution)/shard_map/ppermute | solution.py:433
  15.8 5.2 %collective-permute-start.12 = (bf16[1,256,128]{2,1,0:T(8,128)(2,1)}, bf16[1,256,128]{2,1,0:T(8,128)(2,1)S(1)}, u32[]{:S(2)}, u32[]{:S(2)}) collective-permute-start(bf16[1,256,128]{2,1,0:T(8,128)(2,1)} %get-tuple-element.30.refs_8_), channel_id=1, source_target_pairs={{0,8},{1,9},{2,10},{3,11},{4,0},{5,1},{6,2},{7,3},{8,12},{9,13},{1... | collective-permute-start | bytes 196616 | tf_op jit(solution)/shard_map/ppermute | solution.py:433
  17.4 18.4 %collective-permute-start.3 = (bf16[3,256,128]{2,1,0:T(8,128)(2,1)}, bf16[3,256,128]{2,1,0:T(8,128)(2,1)S(1)}, u32[]{:S(2)}, u32[]{:S(2)}) collective-permute-start(bf16[3,256,128]{2,1,0:T(8,128)(2,1)} %get-tuple-element.24.refs_1_), channel_id=1, source_target_pairs={{0,8},{1,9},{2,10},{3,11},{4,0},{5,1},{6,2},{7,3},{8,12},{9,13},{1... | collective-permute-start | bytes 589832 | tf_op jit(solution)/shard_map/ppermute | solution.py:433
  21.0 6.1 %collective-permute-start.13 = (bf16[1,256,128]{2,1,0:T(8,128)(2,1)S(1)}, bf16[1,256,128]{2,1,0:T(8,128)(2,1)S(1)}, u32[]{:S(2)}, u32[]{:S(2)}) collective-permute-start(bf16[1,256,128]{2,1,0:T(8,128)(2,1)S(1)} %collective-permute-done.12.refs_9_), channel_id=1, source_target_pairs={{0,8},{1,9},{2,10},{3,11},{4,0},{5,1},{6,2},{7,3},{8,12},{9,13},{1... | collective-permute-start | bytes 196616 | tf_op jit(solution)/shard_map/ppermute | solution.py:433
  25.5 10.3 %copy-start.13 = (bf16[3,4,16,2,4,256]{5,4,3,2,1,0:T(4,128)(2,1)S(1)}, bf16[3,4,16,2,4,256]{5,4,3,2,1,0:T(4,128)(2,1)}, u32[]{:S(2)}) copy-start(bf16[3,4,16,2,4,256]{5,4,3,2,1,0:T(4,128)(2,1)} %get-tuple-element.20) | copy-start | bytes 2359300
  25.6 11.7 %collective-permute-start.10 = (bf16[1,4,16,2,4,256]{5,4,3,2,1,0:T(4,128)(2,1)}, bf16[1,4,16,2,4,256]{5,4,3,2,1,0:T(4,128)(2,1)S(1)}, u32[]{:S(2)}, u32[]{:S(2)}) collective-permute-start(bf16[1,4,16,2,4,256]{5,4,3,2,1,0:T(4,128)(2,1)} %get-tuple-element.28), channel_id=1, source_target_pairs={{0,2},{1,3},{2,0},{3,1},{4,6},{5,7},{6,4},{7,5},{8,10},{9,11},{10,... | collective-permute-start | bytes 786440 | tf_op jit(solution)/shard_map/ppermute | solution.py:420
  27.1 7.0 %collective-permute-start.14 = (bf16[1,256,128]{2,1,0:T(8,128)(2,1)S(1)}, bf16[1,256,128]{2,1,0:T(8,128)(2,1)S(1)}, u32[]{:S(2)}, u32[]{:S(2)}) collective-permute-start(bf16[1,256,128]{2,1,0:T(8,128)(2,1)S(1)} %collective-permute-done.13.refs_10_), channel_id=1, source_target_pairs={{0,8},{1,9},{2,10},{3,11},{4,0},{5,1},{6,2},{7,3},{8,12},{9,13},{1... | collective-permute-start | bytes 196616 | tf_op jit(solution)/shard_map/ppermute | solution.py:433
  30.7 8.8 %collective-permute-start.11 = (bf16[1,4,16,2,4,256]{5,4,3,2,1,0:T(4,128)(2,1)}, bf16[1,4,16,2,4,256]{5,4,3,2,1,0:T(4,128)(2,1)S(1)}, u32[]{:S(2)}, u32[]{:S(2)}) collective-permute-start(bf16[1,4,16,2,4,256]{5,4,3,2,1,0:T(4,128)(2,1)} %get-tuple-element.29), channel_id=1, source_target_pairs={{0,3},{1,2},{2,1},{3,0},{4,7},{5,6},{6,5},{7,4},{8,11},{9,10},{10,... | collective-permute-start | bytes 786440 | tf_op jit(solution)/shard_map/ppermute | solution.py:420
  30.8 2.2 %copy-start = (bf16[64,2,4,4096]{3,2,1,0:T(4,128)(2,1)S(1)}, bf16[64,2,4,4096]{3,2,1,0:T(4,128)(2,1)}, u32[]{:S(2)}) copy-start(bf16[64,2,4,4096]{3,2,1,0:T(4,128)(2,1)} %param.20) | copy-start | bytes 12582916
  33.0 3.4 %copy-start.14 = (bf16[3,4,16,2,4,256]{5,4,3,2,1,0:T(4,128)(2,1)S(1)}, bf16[3,4,16,2,4,256]{5,4,3,2,1,0:T(4,128)(2,1)}, u32[]{:S(2)}) copy-start(bf16[3,4,16,2,4,256]{5,4,3,2,1,0:T(4,128)(2,1)} %get-tuple-element.21) | copy-start | bytes 2359300
  33.0 25.5 %copy-start.1 = (bf16[4,256,128]{2,1,0:T(8,128)(2,1)S(1)}, bf16[4,256,128]{2,1,0:T(8,128)(2,1)}, u32[]{:S(2)}) copy-start(bf16[4,256,128]{2,1,0:T(8,128)(2,1)} %get-tuple-element.25.refs_1_.refs_4_) | copy-start | bytes 786436
  33.0 25.5 %copy-start.3 = (f32[256,256]{1,0:T(8,128)S(1)}, f32[256,256]{1,0:T(8,128)}, u32[]{:S(2)}) copy-start(f32[256,256]{1,0:T(8,128)} %constant.32.clone.refs_12_) | copy-start | bytes 786436
  33.0 25.5 %copy-start.9 = (bf16[1,256,64]{2,1,0:T(8,128)(2,1)S(1)}, bf16[1,256,64]{2,1,0:T(8,128)(2,1)}, u32[]{:S(2)}) copy-start(bf16[1,256,64]{2,1,0:T(8,128)(2,1)} %constant.33.clone.refs_13_) | copy-start | bytes 98308
  33.0 25.5 %copy-start.10 = (bf16[1,256,64]{2,1,0:T(8,128)(2,1)S(1)}, bf16[1,256,64]{2,1,0:T(8,128)(2,1)}, u32[]{:S(2)}) copy-start(bf16[1,256,64]{2,1,0:T(8,128)(2,1)} %constant.34.clone.refs_14_) | copy-start | bytes 98308
  33.0 25.5 %copy-start.11 = (bf16[1,256,128]{2,1,0:T(8,128)(2,1)S(1)}, bf16[1,256,128]{2,1,0:T(8,128)(2,1)}, u32[]{:S(2)}) copy-start(bf16[1,256,128]{2,1,0:T(8,128)(2,1)} %get-tuple-element.30.refs_8_) | copy-start | bytes 196612
  34.2 25.3 %collective-permute-start = (bf16[3,4,16,2,4,256]{5,4,3,2,1,0:T(4,128)(2,1)S(1)}, bf16[3,4,16,2,4,256]{5,4,3,2,1,0:T(4,128)(2,1)S(1)}, u32[]{:S(2)}, u32[]{:S(2)}) collective-permute-start(bf16[3,4,16,2,4,256]{5,4,3,2,1,0:T(4,128)(2,1)S(1)} %get-tuple-element.19), channel_id=1, source_target_pairs={{0,1},{1,0},{2,3},{3,2},{4,5},{5,4},{6,7},{7,6},{8,9},{9,8},{10,11... | collective-permute-start | bytes 2359304 | tf_op jit(solution)/shard_map/ppermute | solution.py:419
  35.8 23.6 %collective-permute-start.1 = (bf16[3,4,16,2,4,256]{5,4,3,2,1,0:T(4,128)(2,1)S(1)}, bf16[3,4,16,2,4,256]{5,4,3,2,1,0:T(4,128)(2,1)S(1)}, u32[]{:S(2)}, u32[]{:S(2)}) collective-permute-start(bf16[3,4,16,2,4,256]{5,4,3,2,1,0:T(4,128)(2,1)S(1)} %copy-done.13), channel_id=1, source_target_pairs={{0,2},{1,3},{2,0},{3,1},{4,6},{5,7},{6,4},{7,5},{8,10},{9,11},{10,... | collective-permute-start | bytes 2359304 | tf_op jit(solution)/shard_map/ppermute | solution.py:419
  36.4 36.9 %collective-permute-start.2 = (bf16[3,4,16,2,4,256]{5,4,3,2,1,0:T(4,128)(2,1)S(1)}, bf16[3,4,16,2,4,256]{5,4,3,2,1,0:T(4,128)(2,1)S(1)}, u32[]{:S(2)}, u32[]{:S(2)}) collective-permute-start(bf16[3,4,16,2,4,256]{5,4,3,2,1,0:T(4,128)(2,1)S(1)} %copy-done.14), channel_id=1, source_target_pairs={{0,3},{1,2},{2,1},{3,0},{4,7},{5,6},{6,5},{7,4},{8,11},{9,10},{10,... | collective-permute-start | bytes 2359304 | tf_op jit(solution)/shard_map/ppermute | solution.py:419
  37.3 2.2 %collective-permute-start.9 = (bf16[1,4,16,2,4,256]{5,4,3,2,1,0:T(4,128)(2,1)S(1)}, bf16[1,4,16,2,4,256]{5,4,3,2,1,0:T(4,128)(2,1)S(1)}, u32[]{:S(2)}, u32[]{:S(2)}) collective-permute-start(bf16[1,4,16,2,4,256]{5,4,3,2,1,0:T(4,128)(2,1)S(1)} %get-tuple-element.27), channel_id=1, source_target_pairs={{0,1},{1,0},{2,3},{3,2},{4,5},{5,4},{6,7},{7,6},{8,9},{9,8},{10,11... | collective-permute-start | bytes 786440 | tf_op jit(solution)/shard_map/ppermute | solution.py:420
  39.5 9.2 %collective-permute-start.7 = (bf16[4,256,128]{2,1,0:T(8,128)(2,1)S(1)}, bf16[4,256,128]{2,1,0:T(8,128)(2,1)S(1)}, u32[]{:S(2)}, u32[]{:S(2)}) collective-permute-start(bf16[4,256,128]{2,1,0:T(8,128)(2,1)S(1)} %collective-permute-done.6.refs_2_.refs_5_), channel_id=1, source_target_pairs={{0,8},{1,9},{2,10},{3,11},{4,0},{5,1},{6,2},{7,3},{8,12},{9,13},{1... | collective-permute-start | bytes 786440 | tf_op jit(solution)/shard_map/ppermute | solution.py:433
  39.5 13.4 %collective-permute-start.4 = (bf16[3,256,128]{2,1,0:T(8,128)(2,1)S(1)}, bf16[3,256,128]{2,1,0:T(8,128)(2,1)S(1)}, u32[]{:S(2)}, u32[]{:S(2)}) collective-permute-start(bf16[3,256,128]{2,1,0:T(8,128)(2,1)S(1)} %collective-permute-done.3.refs_2_), channel_id=1, source_target_pairs={{0,8},{1,9},{2,10},{3,11},{4,0},{5,1},{6,2},{7,3},{8,12},{9,13},{1... | collective-permute-start | bytes 589832 | tf_op jit(solution)/shard_map/ppermute | solution.py:433
  48.7 9.8 %collective-permute-start.8 = (bf16[4,256,128]{2,1,0:T(8,128)(2,1)S(1)}, bf16[4,256,128]{2,1,0:T(8,128)(2,1)S(1)}, u32[]{:S(2)}, u32[]{:S(2)}) collective-permute-start(bf16[4,256,128]{2,1,0:T(8,128)(2,1)S(1)} %collective-permute-done.7.refs_3_.refs_6_), channel_id=1, source_target_pairs={{0,8},{1,9},{2,10},{3,11},{4,0},{5,1},{6,2},{7,3},{8,12},{9,13},{1... | collective-permute-start | bytes 786440 | tf_op jit(solution)/shard_map/ppermute | solution.py:433
  52.9 23.4 %collective-permute-start.5 = (bf16[3,256,128]{2,1,0:T(8,128)(2,1)S(1)}, bf16[3,256,128]{2,1,0:T(8,128)(2,1)S(1)}, u32[]{:S(2)}, u32[]{:S(2)}) collective-permute-start(bf16[3,256,128]{2,1,0:T(8,128)(2,1)S(1)} %collective-permute-done.4.refs_3_), channel_id=1, source_target_pairs={{0,8},{1,9},{2,10},{3,11},{4,0},{5,1},{6,2},{7,3},{8,12},{9,13},{1... | collective-permute-start | bytes 589832 | tf_op jit(solution)/shard_map/ppermute | solution.py:433
  58.6 15.5 %copy-start.2 = (f32[256,128]{1,0:T(8,128)S(1)}, f32[256,128]{1,0:T(8,128)}, u32[]{:S(2)}) copy-start(f32[256,128]{1,0:T(8,128)} %constant.27.clone.refs_5_) | copy-start | bytes 393220
  58.6 15.5 %copy-start.7 = (bf16[3,128,64]{2,1,0:T(8,128)(2,1)S(1)}, bf16[3,128,64]{2,1,0:T(8,128)(2,1)}, u32[]{:S(2)}) copy-start(bf16[3,128,64]{2,1,0:T(8,128)(2,1)} %constant.28.clone.refs_6_) | copy-start | bytes 147460
  58.6 15.5 %copy-start.8 = (bf16[3,128,64]{2,1,0:T(8,128)(2,1)S(1)}, bf16[3,128,64]{2,1,0:T(8,128)(2,1)}, u32[]{:S(2)}) copy-start(bf16[3,128,64]{2,1,0:T(8,128)(2,1)} %constant.29.clone.refs_7_) | copy-start | bytes 147460
  73.2 3.1 %copy-start.4 = (bf16[3,256,128]{2,1,0:T(8,128)(2,1)S(1)}, bf16[3,256,128]{2,1,0:T(8,128)(2,1)}, u32[]{:S(2)}) copy-start(bf16[3,256,128]{2,1,0:T(8,128)(2,1)} %get-tuple-element.24.refs_1_) | copy-start | bytes 589828
  73.2 3.1 %copy-start.5 = (bf16[3,128,64]{2,1,0:T(8,128)(2,1)S(1)}, bf16[3,128,64]{2,1,0:T(8,128)(2,1)}, u32[]{:S(2)}) copy-start(bf16[3,128,64]{2,1,0:T(8,128)(2,1)} %constant.30.clone.refs_6_) | copy-start | bytes 147460
  73.2 3.1 %copy-start.6 = (bf16[3,128,64]{2,1,0:T(8,128)(2,1)S(1)}, bf16[3,128,64]{2,1,0:T(8,128)(2,1)}, u32[]{:S(2)}) copy-start(bf16[3,128,64]{2,1,0:T(8,128)(2,1)} %constant.31.clone.refs_7_) | copy-start | bytes 147460
  74.1 14.0 %copy-start.12 = (bf16[256,64]{1,0:T(8,128)(2,1)S(1)}, bf16[256,64]{1,0:T(8,128)(2,1)}, u32[]{:S(2)}) copy-start(bf16[256,64]{1,0:T(8,128)(2,1)} %constant.35.clone) | copy-start | bytes 98308

commit v5 on v3

--- a/solution.py
+++ b/solution.py
@@ -204,32 +204,23 @@
     return results
 
 
-def rows_kernel(block, head, starts, source, first, rest, buffer, in_sems, out_sems):
-    slots = buffer.shape[1]
-    bands = buffer.shape[0]
-    ins = []
+def rows_kernel(block, head, starts, source, first, rest, sems):
+    slots = first.shape[1]
+    bands = head + rest.shape[0]
     device = lax.axis_index("rows")
+    copies = []
     for i in range(slots):
         start = jnp.int32(0)
         for d, row in enumerate(starts):
             start = jnp.where(device == d, jnp.int32(int(row[i]) * block), start)
-        column = pl.multiple_of(start, block)
-        ins.append(
-            pltpu.make_async_copy(
-                source.at[:, :, :, :, pl.ds(column, block)], buffer.at[:, i], in_sems.at[i]
-            )
-        )
-        ins[-1].start()
-    outs = []
-    for i in range(slots):
-        ins[i].wait()
+        column = pl.ds(pl.multiple_of(start, block), block)
         for k, (low, high, target) in enumerate(((0, head, first), (head, bands, rest))):
             copy = pltpu.make_async_copy(
-                buffer.at[low:high, i], target.at[:, i], out_sems.at[i, k]
+                source.at[low:high, :, :, :, column], target.at[:, i], sems.at[i, k]
             )
             copy.start()
-            outs.append(copy)
-    for copy in outs:
+            copies.append(copy)
+    for copy in copies:
         copy.wait()
 
 
@@ -250,16 +241,13 @@
     return pl.pallas_call(
         functools.partial(rows_kernel, block, head, starts),
         in_specs=[pl.BlockSpec(memory_space=pltpu.HBM)],
-        out_specs=[pl.BlockSpec(memory_space=pltpu.HBM)] * 2,
+        out_specs=[pl.BlockSpec(memory_space=pl.ANY)] * 2,
         out_shape=[
             jax.ShapeDtypeStruct((head,) + shape, kind),
             jax.ShapeDtypeStruct((bands - head,) + shape, kind),
         ],
-        scratch_shapes=[
-            pltpu.VMEM((bands,) + shape, kind),
-            pltpu.SemaphoreType.DMA((slots,)),
-            pltpu.SemaphoreType.DMA((slots, 2)),
-        ],
+        scratch_shapes=[pltpu.SemaphoreType.DMA((slots, 2))],
+        compiler_params=pltpu.CompilerParams(vmem_limit_bytes=51 << 20),
         name="rows_for",
     )(source)
 

time: 91.9 us -> 88.3 us (0.961)
  waiting for transfers between devices: 22.5 us -> 35.4 us
  local copies, waits for them, and re-layouts: 12.9 us -> 0.28 us
  Pallas kernels: 27.2 us -> 23.4 us
    unnamed x58 -> x26, local copies, waits for them, and re-layouts: 12.9 us -> 0.28 us
    ppermute x3, waiting for transfers between devices: 4.97 us -> 13.7 us  [exchange(): first = lax.ppermute(first, 'rows', pairs)]
    pallas_call x4, Pallas kernels: 8.35 us -> 5.56 us  [rows_for(): pl.pallas_call(functools.partial(rows_kernel, block, head, starts), in_sp...]
    ppermute x3, waiting for transfers between devices: 0.83 us -> 3.3 us  [exchange(): rest = lax.ppermute(rest, 'rows', pairs)]
    ppermute x9, waiting for transfers between devices: 16.7 us -> 18.4 us  [shards(): piece.append(lax.ppermute(piece[-1], 'rows', step))]
    pallas_call x3, Pallas kernels: 6.38 us -> 5.37 us  [predict(): pl.pallas_call(functools.partial(predict_kernel, len(matrix), parts, slot...]
  transfers between devices with their start and end apart: 15 -> 15, of which waited for: 6 -> 6; matrix products, arithmetic and copies ran while one was open for 0% -> 0% of each run, Pallas kernels for 20% -> 17%
where the time goes in v5:
time: 88.3 us; the launch traced here: 88 us
  waiting for transfers between devices  35.4 us (40%)
  Pallas kernels  23.4 us (27%)
  starting transfers between devices  18.7 us (21%)
  blocking collectives  9.2 us (10%)
    ppermute x9, waiting for transfers between devices, shards(): piece.append(lax.ppermute(piece[-1], 'rows', step))  18.4 us
    ppermute x3, waiting for transfers between devices, exchange(): first = lax.ppermute(first, 'rows', pairs)  13.7 us
    ppermute x9, starting transfers between devices, shards(): piece.append(lax.ppermute(piece[-1], 'rows', step))  13.3 us
    pallas_call x2, Pallas kernels, spectra_of(): pl.pallas_call(functools.partial(spectra_kernel, bands, bins, taps, part,...  11.6 us
    all_to_all x1, blocking collectives, shards(): lax.all_to_all(partial_value, 'rows', split_axis=0, concat_axis=0, tiled=...  9.2 us
    pallas_call x4, Pallas kernels, rows_for(): pl.pallas_call(functools.partial(rows_kernel, block, head, starts), in_sp...  5.56 us
    pallas_call x3, Pallas kernels, predict(): pl.pallas_call(functools.partial(predict_kernel, len(matrix), parts, slot...  5.37 us
    ppermute x3, waiting for transfers between devices, exchange(): rest = lax.ppermute(rest, 'rows', pairs)  3.3 us
  transfers between devices with their start and end apart: 15, of which 6 were waited for; matrix products, arithmetic and copies ran while one was open for 0% of the time, Pallas kernels for 17%

profile of v5, /device:TPU:0, one launch (start us, length us, event | category | flops | bytes accessed | tf_op | source)
XLA Modules:
  0.0 88.0 jit_solution(7221265790649257635)
XLA Ops:
  0.0 5.9 %spectra.2 = (bf16[4,256,128]{2,1,0:T(8,128)(2,1)}, bf16[128,256]{1,0:T(8,128)(2,1)}, bf16[512,128]{1,0:T(8,128)(2,1)}) custom-call(bf16[8,256,2048]{2,1,0:T(8,128)(2,1)} %refs_0_.3, s32[8,256]{1,0:T(8,128)} %refs_1_.3, bf16[2048,256]{1,0:T(8,128)(2,1)} %constant.24.clone.refs_2_, f32[16,32]{1,0:T(8,128)} %refs_3_.1, f32[32,256]{1,0:T(8,128)} %constant.25.clone.refs_4_, ...), custom_call_target="tpu_custom_call" | custom-call | flops 1073741824 | bytes 4194304 | tf_op jit(solution)/shard_map/spectra/pallas_call | solution.py:174
  5.9 4.1 %collective-permute-start.6 = (bf16[4,256,128]{2,1,0:T(8,128)(2,1)}, bf16[4,256,128]{2,1,0:T(8,128)(2,1)S(1)}, u32[]{:S(2)}, u32[]{:S(2)}) collective-permute-start(bf16[4,256,128]{2,1,0:T(8,128)(2,1)} %get-tuple-element.25.refs_1_.refs_4_), channel_id=1, source_target_pairs={{0,8},{1,9},{2,10},{3,11},{4,0},{5,1},{6,2},{7,3},{8,12},{9,13},{1... | collective-permute-start | bytes 786440 | tf_op jit(solution)/shard_map/ppermute | solution.py:420
  10.0 5.8 %spectra.3 = (bf16[3,256,128]{2,1,0:T(8,128)(2,1)}, bf16[1,256,128]{2,1,0:T(8,128)(2,1)}) custom-call(bf16[8,256,2048]{2,1,0:T(8,128)(2,1)} %refs_0_.3, s32[8,256]{1,0:T(8,128)} %refs_1_.3, bf16[2048,256]{1,0:T(8,128)(2,1)} %constant.24.clone.refs_2_, bf16[128,256]{1,0:T(8,128)(2,1)} %get-tuple-element.22.refs_3_, bf16[512,128]{1,0:T(8,128)(2,1)} %get-tuple-element.23.refs_4_), custom_call_target="tpu_custom_call" | custom-call | flops 1073741824 | bytes 4194304 | tf_op jit(solution)/shard_map/spectra/pallas_call | solution.py:174
  15.8 1.6 %collective-permute-start.12 = (bf16[1,256,128]{2,1,0:T(8,128)(2,1)}, bf16[1,256,128]{2,1,0:T(8,128)(2,1)S(1)}, u32[]{:S(2)}, u32[]{:S(2)}) collective-permute-start(bf16[1,256,128]{2,1,0:T(8,128)(2,1)} %get-tuple-element.30.refs_8_), channel_id=1, source_target_pairs={{0,8},{1,9},{2,10},{3,11},{4,0},{5,1},{6,2},{7,3},{8,12},{9,13},{1... | collective-permute-start | bytes 196616 | tf_op jit(solution)/shard_map/ppermute | solution.py:420
  17.4 0.3 collective-permute-start.3
  17.7 3.3 %collective-permute-done.12.refs_9_ = bf16[1,256,128]{2,1,0:T(8,128)(2,1)S(1)} collective-permute-done((bf16[1,256,128]{2,1,0:T(8,128)(2,1)}, bf16[1,256,128]{2,1,0:T(8,128)(2,1)S(1)}, u32[]{:S(2)}, u32[]{:S(2)}) %collective-permute-start.12) | collective-permute-done | bytes 65568 | tf_op jit(solution)/shard_map/ppermute | solution.py:420
  21.0 2.5 %collective-permute-start.13 = (bf16[1,256,128]{2,1,0:T(8,128)(2,1)S(1)}, bf16[1,256,128]{2,1,0:T(8,128)(2,1)S(1)}, u32[]{:S(2)}, u32[]{:S(2)}) collective-permute-start(bf16[1,256,128]{2,1,0:T(8,128)(2,1)S(1)} %collective-permute-done.12.refs_9_), channel_id=1, source_target_pairs={{0,8},{1,9},{2,10},{3,11},{4,0},{5,1},{6,2},{7,3},{8,12},{9,13},{1... | collective-permute-start | bytes 196616 | tf_op jit(solution)/shard_map/ppermute | solution.py:420
  23.5 1.4 %rows_for.6 = (bf16[3,4,16,2,4,256]{5,4,3,2,1,0:T(4,128)(2,1)S(1)}, bf16[1,4,16,2,4,256]{5,4,3,2,1,0:T(4,128)(2,1)S(1)}) custom-call(bf16[4,16,2,4,4096]{4,3,2,1,0:T(4,128)(2,1)} %bitcast.5), custom_call_target="tpu_custom_call" | custom-call | tf_op jit(solution)/shard_map/rows_for/pallas_call | solution.py:241
  24.9 1.6 %collective-permute-start.10 = (bf16[1,4,16,2,4,256]{5,4,3,2,1,0:T(4,128)(2,1)S(1)}, bf16[1,4,16,2,4,256]{5,4,3,2,1,0:T(4,128)(2,1)S(1)}, u32[]{:S(2)}, u32[]{:S(2)}) collective-permute-start(bf16[1,4,16,2,4,256]{5,4,3,2,1,0:T(4,128)(2,1)S(1)} %get-tuple-element.28), channel_id=1, source_target_pairs={{0,2},{1,3},{2,0},{3,1},{4,6},{5,7},{6,4},{7,5},{8,10},{9,11},{10,... | collective-permute-start | bytes 786440 | tf_op jit(solution)/shard_map/ppermute | solution.py:407
  26.4 0.0 collective-permute-done.13.refs_10_
  26.4 2.2 %collective-permute-start.14 = (bf16[1,256,128]{2,1,0:T(8,128)(2,1)S(1)}, bf16[1,256,128]{2,1,0:T(8,128)(2,1)S(1)}, u32[]{:S(2)}, u32[]{:S(2)}) collective-permute-start(bf16[1,256,128]{2,1,0:T(8,128)(2,1)S(1)} %collective-permute-done.13.refs_10_), channel_id=1, source_target_pairs={{0,8},{1,9},{2,10},{3,11},{4,0},{5,1},{6,2},{7,3},{8,12},{9,13},{1... | collective-permute-start | bytes 196616 | tf_op jit(solution)/shard_map/ppermute | solution.py:420
  28.6 1.4 %rows_for.7 = (bf16[3,4,16,2,4,256]{5,4,3,2,1,0:T(4,128)(2,1)S(1)}, bf16[1,4,16,2,4,256]{5,4,3,2,1,0:T(4,128)(2,1)S(1)}) custom-call(bf16[4,16,2,4,4096]{4,3,2,1,0:T(4,128)(2,1)} %bitcast.6), custom_call_target="tpu_custom_call" | custom-call | tf_op jit(solution)/shard_map/rows_for/pallas_call | solution.py:241
  30.0 0.0 copy-start.2
  30.0 0.0 copy-start.8
  30.1 0.0 copy-start.9
  30.1 0.1 collective-permute-start.11
  30.2 1.4 %rows_for.5 = (bf16[3,4,16,2,4,256]{5,4,3,2,1,0:T(4,128)(2,1)S(1)}, bf16[1,4,16,2,4,256]{5,4,3,2,1,0:T(4,128)(2,1)S(1)}) custom-call(bf16[4,16,2,4,4096]{4,3,2,1,0:T(4,128)(2,1)} %bitcast.7), custom_call_target="tpu_custom_call" | custom-call | tf_op jit(solution)/shard_map/rows_for/pallas_call | solution.py:241
  31.6 0.0 collective-permute-done.14.refs_11_
  31.6 1.6 %collective-permute-start = (bf16[3,4,16,2,4,256]{5,4,3,2,1,0:T(4,128)(2,1)S(1)}, bf16[3,4,16,2,4,256]{5,4,3,2,1,0:T(4,128)(2,1)S(1)}, u32[]{:S(2)}, u32[]{:S(2)}) collective-permute-start(bf16[3,4,16,2,4,256]{5,4,3,2,1,0:T(4,128)(2,1)S(1)} %get-tuple-element.19), channel_id=1, source_target_pairs={{0,1},{1,0},{2,3},{3,2},{4,5},{5,4},{6,7},{7,6},{8,9},{9,8},{10,11... | collective-permute-start | bytes 2359304 | tf_op jit(solution)/shard_map/ppermute | solution.py:406
  33.2 0.0 collective-permute-done.3.refs_2_
  33.2 0.5 collective-permute-start.1
  33.7 0.0 collective-permute-done.6.refs_2_.refs_5_
  33.7 0.9 %collective-permute-start.2 = (bf16[3,4,16,2,4,256]{5,4,3,2,1,0:T(4,128)(2,1)S(1)}, bf16[3,4,16,2,4,256]{5,4,3,2,1,0:T(4,128)(2,1)S(1)}, u32[]{:S(2)}, u32[]{:S(2)}) collective-permute-start(bf16[3,4,16,2,4,256]{5,4,3,2,1,0:T(4,128)(2,1)S(1)} %get-tuple-element.21), channel_id=1, source_target_pairs={{0,3},{1,2},{2,1},{3,0},{4,7},{5,6},{6,5},{7,4},{8,11},{9,10},{10,... | collective-permute-start | bytes 2359304 | tf_op jit(solution)/shard_map/ppermute | solution.py:406
  34.7 0.0 collective-permute-done.10.refs_2_
  34.7 0.7 collective-permute-start.9
  35.4 3.3 %collective-permute-done.11.refs_3_ = bf16[1,4,16,2,4,256]{5,4,3,2,1,0:T(4,128)(2,1)S(1)} collective-permute-done((bf16[1,4,16,2,4,256]{5,4,3,2,1,0:T(4,128)(2,1)S(1)}, bf16[1,4,16,2,4,256]{5,4,3,2,1,0:T(4,128)(2,1)S(1)}, u32[]{:S(2)}, u32[]{:S(2)}) %collective-permute-start.11) | collective-permute-done | bytes 262176 | tf_op jit(solution)/shard_map/ppermute | solution.py:407
  38.7 0.0 collective-permute-start.7
  38.7 0.0 collective-permute-done.9.refs_1_
  38.7 0.7 collective-permute-start.4
  39.4 8.5 %collective-permute-done.7.refs_3_.refs_6_ = bf16[4,256,128]{2,1,0:T(8,128)(2,1)S(1)} collective-permute-done((bf16[4,256,128]{2,1,0:T(8,128)(2,1)S(1)}, bf16[4,256,128]{2,1,0:T(8,128)(2,1)S(1)}, u32[]{:S(2)}, u32[]{:S(2)}) %collective-permute-start.7) | collective-permute-done | bytes 262176 | tf_op jit(solution)/shard_map/ppermute | solution.py:420
  47.9 0.9 %collective-permute-start.8 = (bf16[4,256,128]{2,1,0:T(8,128)(2,1)S(1)}, bf16[4,256,128]{2,1,0:T(8,128)(2,1)S(1)}, u32[]{:S(2)}, u32[]{:S(2)}) collective-permute-start(bf16[4,256,128]{2,1,0:T(8,128)(2,1)S(1)} %collective-permute-done.7.refs_3_.refs_6_), channel_id=1, source_target_pairs={{0,8},{1,9},{2,10},{3,11},{4,0},{5,1},{6,2},{7,3},{8,12},{9,13},{1... | collective-permute-start | bytes 786440 | tf_op jit(solution)/shard_map/ppermute | solution.py:420
  48.8 3.3 %collective-permute-done.4.refs_3_ = bf16[3,256,128]{2,1,0:T(8,128)(2,1)S(1)} collective-permute-done((bf16[3,256,128]{2,1,0:T(8,128)(2,1)S(1)}, bf16[3,256,128]{2,1,0:T(8,128)(2,1)S(1)}, u32[]{:S(2)}, u32[]{:S(2)}) %collective-permute-start.4) | collective-permute-done | bytes 196640 | tf_op jit(solution)/shard_map/ppermute | solution.py:420
  52.1 0.9 %collective-permute-start.5 = (bf16[3,256,128]{2,1,0:T(8,128)(2,1)S(1)}, bf16[3,256,128]{2,1,0:T(8,128)(2,1)S(1)}, u32[]{:S(2)}, u32[]{:S(2)}) collective-permute-start(bf16[3,256,128]{2,1,0:T(8,128)(2,1)S(1)} %collective-permute-done.4.refs_3_), channel_id=1, source_target_pairs={{0,8},{1,9},{2,10},{3,11},{4,0},{5,1},{6,2},{7,3},{8,12},{9,13},{1... | collective-permute-start | bytes 589832 | tf_op jit(solution)/shard_map/ppermute | solution.py:420
  53.0 1.4 %rows_for.4 = (bf16[3,4,16,2,4,256]{5,4,3,2,1,0:T(4,128)(2,1)S(1)}, bf16[1,4,16,2,4,256]{5,4,3,2,1,0:T(4,128)(2,1)S(1)}) custom-call(bf16[4,16,2,4,4096]{4,3,2,1,0:T(4,128)(2,1)} %bitcast.8), custom_call_target="tpu_custom_call" | custom-call | tf_op jit(solution)/shard_map/rows_for/pallas_call | solution.py:241
  54.3 3.3 %collective-permute-done.8.refs_4_.refs_7_ = bf16[4,256,128]{2,1,0:T(8,128)(2,1)S(1)} collective-permute-done((bf16[4,256,128]{2,1,0:T(8,128)(2,1)S(1)}, bf16[4,256,128]{2,1,0:T(8,128)(2,1)S(1)}, u32[]{:S(2)}, u32[]{:S(2)}) %collective-permute-start.8) | collective-permute-done | bytes 262176 | tf_op jit(solution)/shard_map/ppermute | solution.py:420
  57.7 0.0 copy-start.1
  57.7 0.0 copy-start.6
  57.7 0.0 copy-start.7
  57.8 0.9 %predict.5 = bf16[4,16,64]{2,1,0:T(8,128)(2,1)S(1)} custom-call(bf16[1,4,16,2,4,256]{5,4,3,2,1,0:T(4,128)(2,1)S(1)} %get-tuple-element.26.refs_0_, bf16[1,4,16,2,4,256]{5,4,3,2,1,0:T(4,128)(2,1)S(1)} %collective-permute-done.9.refs_1_, bf16[1,4,16,2,4,256]{5,4,3,2,1,0:T(4,128)(2,1)S(1)} %collective-permute-done.10.refs_2_, ...), custom_call_target="tpu_custom_call" | custom-call | tf_op jit(solution)/shard_map/predict/pallas_call | solution.py:356
  58.7 13.7 %collective-permute-done.2.refs_3_ = bf16[3,4,16,2,4,256]{5,4,3,2,1,0:T(4,128)(2,1)S(1)} collective-permute-done((bf16[3,4,16,2,4,256]{5,4,3,2,1,0:T(4,128)(2,1)S(1)}, bf16[3,4,16,2,4,256]{5,4,3,2,1,0:T(4,128)(2,1)S(1)}, u32[]{:S(2)}, u32[]{:S(2)}) %collective-permute-start.2) | collective-permute-done | bytes 786464 | tf_op jit(solution)/shard_map/ppermute | solution.py:406
  72.4 0.8 merge.1.refs_0_
  73.2 0.0 copy-start.11
  73.2 2.2 %predict.3.refs_8_ = bf16[12,16,64]{2,1,0:T(8,128)(2,1)S(1)} custom-call(bf16[3,512,1024]{2,1,0:T(8,128)(2,1)S(1)} %merge.1.refs_0_, bf16[4,256,128]{2,1,0:T(8,128)(2,1)S(1)} %copy-done, bf16[4,256,128]{2,1,0:T(8,128)(2,1)S(1)} %collective-permute-done.6.refs_2_.refs_5_, bf16[4,256,128]{2,1,0:T(8,128)(2,1)S(1)} %collective-permute-done.7.refs_3_.refs_6_, ...), custom_call_target="tpu_custom_call" | custom-call | tf_op jit(solution)/shard_map/predict/pallas_call | solution.py:356
  75.5 2.2 %predict.4 = bf16[12,16,64]{2,1,0:T(8,128)(2,1)S(1)} custom-call(bf16[3,512,1024]{2,1,0:T(8,128)(2,1)S(1)} %merge.1.refs_0_, bf16[3,256,128]{2,1,0:T(8,128)(2,1)S(1)} %copy-done.3, bf16[3,256,128]{2,1,0:T(8,128)(2,1)S(1)} %collective-permute-done.3.refs_2_, bf16[3,256,128]{2,1,0:T(8,128)(2,1)S(1)} %collective-permute-done.4.refs_3_, ...), custom_call_target="tpu_custom_call" | custom-call | tf_op jit(solution)/shard_map/predict/pallas_call | solution.py:356
  77.8 0.1 reshape.15
  77.9 9.2 %all_to_all.5 = bf16[16,2,512]{2,1,0:T(2,128)(2,1)S(1)} all-to-all(bf16[16,2,512]{2,1,0:T(2,128)(2,1)S(1)} %reshape.15), channel_id=1, replica_groups=mesh['parts'=2,'rows'=16] {'rows'}, dimensions={0} | all-to-all | bytes 65536 | tf_op jit(solution)/shard_map/all_to_all | solution.py:435
  87.1 0.1 reshape.16
  87.3 0.8 convolution_convert_fusion
  (21 shorter events, 0.1 us)
Async XLA Ops:
  5.9 27.9 %collective-permute-start.6 = (bf16[4,256,128]{2,1,0:T(8,128)(2,1)}, bf16[4,256,128]{2,1,0:T(8,128)(2,1)S(1)}, u32[]{:S(2)}, u32[]{:S(2)}) collective-permute-start(bf16[4,256,128]{2,1,0:T(8,128)(2,1)} %get-tuple-element.25.refs_1_.refs_4_), channel_id=1, source_target_pairs={{0,8},{1,9},{2,10},{3,11},{4,0},{5,1},{6,2},{7,3},{8,12},{9,13},{1... | collective-permute-start | bytes 786440 | tf_op jit(solution)/shard_map/ppermute | solution.py:420
  15.8 5.2 %collective-permute-start.12 = (bf16[1,256,128]{2,1,0:T(8,128)(2,1)}, bf16[1,256,128]{2,1,0:T(8,128)(2,1)S(1)}, u32[]{:S(2)}, u32[]{:S(2)}) collective-permute-start(bf16[1,256,128]{2,1,0:T(8,128)(2,1)} %get-tuple-element.30.refs_8_), channel_id=1, source_target_pairs={{0,8},{1,9},{2,10},{3,11},{4,0},{5,1},{6,2},{7,3},{8,12},{9,13},{1... | collective-permute-start | bytes 196616 | tf_op jit(solution)/shard_map/ppermute | solution.py:420
  17.4 15.8 %collective-permute-start.3 = (bf16[3,256,128]{2,1,0:T(8,128)(2,1)}, bf16[3,256,128]{2,1,0:T(8,128)(2,1)S(1)}, u32[]{:S(2)}, u32[]{:S(2)}) collective-permute-start(bf16[3,256,128]{2,1,0:T(8,128)(2,1)} %get-tuple-element.24.refs_1_), channel_id=1, source_target_pairs={{0,8},{1,9},{2,10},{3,11},{4,0},{5,1},{6,2},{7,3},{8,12},{9,13},{1... | collective-permute-start | bytes 589832 | tf_op jit(solution)/shard_map/ppermute | solution.py:420
  21.0 5.4 %collective-permute-start.13 = (bf16[1,256,128]{2,1,0:T(8,128)(2,1)S(1)}, bf16[1,256,128]{2,1,0:T(8,128)(2,1)S(1)}, u32[]{:S(2)}, u32[]{:S(2)}) collective-permute-start(bf16[1,256,128]{2,1,0:T(8,128)(2,1)S(1)} %collective-permute-done.12.refs_9_), channel_id=1, source_target_pairs={{0,8},{1,9},{2,10},{3,11},{4,0},{5,1},{6,2},{7,3},{8,12},{9,13},{1... | collective-permute-start | bytes 196616 | tf_op jit(solution)/shard_map/ppermute | solution.py:420
  24.9 9.8 %collective-permute-start.10 = (bf16[1,4,16,2,4,256]{5,4,3,2,1,0:T(4,128)(2,1)S(1)}, bf16[1,4,16,2,4,256]{5,4,3,2,1,0:T(4,128)(2,1)S(1)}, u32[]{:S(2)}, u32[]{:S(2)}) collective-permute-start(bf16[1,4,16,2,4,256]{5,4,3,2,1,0:T(4,128)(2,1)S(1)} %get-tuple-element.28), channel_id=1, source_target_pairs={{0,2},{1,3},{2,0},{3,1},{4,6},{5,7},{6,4},{7,5},{8,10},{9,11},{10,... | collective-permute-start | bytes 786440 | tf_op jit(solution)/shard_map/ppermute | solution.py:407
  26.4 5.2 %collective-permute-start.14 = (bf16[1,256,128]{2,1,0:T(8,128)(2,1)S(1)}, bf16[1,256,128]{2,1,0:T(8,128)(2,1)S(1)}, u32[]{:S(2)}, u32[]{:S(2)}) collective-permute-start(bf16[1,256,128]{2,1,0:T(8,128)(2,1)S(1)} %collective-permute-done.13.refs_10_), channel_id=1, source_target_pairs={{0,8},{1,9},{2,10},{3,11},{4,0},{5,1},{6,2},{7,3},{8,12},{9,13},{1... | collective-permute-start | bytes 196616 | tf_op jit(solution)/shard_map/ppermute | solution.py:420
  30.0 27.7 %copy-start = (bf16[4,256,128]{2,1,0:T(8,128)(2,1)S(1)}, bf16[4,256,128]{2,1,0:T(8,128)(2,1)}, u32[]{:S(2)}) copy-start(bf16[4,256,128]{2,1,0:T(8,128)(2,1)} %get-tuple-element.25.refs_1_.refs_4_) | copy-start | bytes 786436
  30.0 27.7 %copy-start.2 = (f32[256,256]{1,0:T(8,128)S(1)}, f32[256,256]{1,0:T(8,128)}, u32[]{:S(2)}) copy-start(f32[256,256]{1,0:T(8,128)} %constant.32.clone.refs_12_) | copy-start | bytes 786436
  30.0 27.7 %copy-start.8 = (bf16[1,256,64]{2,1,0:T(8,128)(2,1)S(1)}, bf16[1,256,64]{2,1,0:T(8,128)(2,1)}, u32[]{:S(2)}) copy-start(bf16[1,256,64]{2,1,0:T(8,128)(2,1)} %constant.33.clone.refs_13_) | copy-start | bytes 98308
  30.1 27.6 %copy-start.9 = (bf16[1,256,64]{2,1,0:T(8,128)(2,1)S(1)}, bf16[1,256,64]{2,1,0:T(8,128)(2,1)}, u32[]{:S(2)}) copy-start(bf16[1,256,64]{2,1,0:T(8,128)(2,1)} %constant.34.clone.refs_14_) | copy-start | bytes 98308
  30.1 27.6 %copy-start.10 = (bf16[1,256,128]{2,1,0:T(8,128)(2,1)S(1)}, bf16[1,256,128]{2,1,0:T(8,128)(2,1)}, u32[]{:S(2)}) copy-start(bf16[1,256,128]{2,1,0:T(8,128)(2,1)} %get-tuple-element.30.refs_8_) | copy-start | bytes 196612
  30.1 8.6 %collective-permute-start.11 = (bf16[1,4,16,2,4,256]{5,4,3,2,1,0:T(4,128)(2,1)S(1)}, bf16[1,4,16,2,4,256]{5,4,3,2,1,0:T(4,128)(2,1)S(1)}, u32[]{:S(2)}, u32[]{:S(2)}) collective-permute-start(bf16[1,4,16,2,4,256]{5,4,3,2,1,0:T(4,128)(2,1)S(1)} %get-tuple-element.29), channel_id=1, source_target_pairs={{0,3},{1,2},{2,1},{3,0},{4,7},{5,6},{6,5},{7,4},{8,11},{9,10},{10,... | collective-permute-start | bytes 786440 | tf_op jit(solution)/shard_map/ppermute | solution.py:407
  31.6 27.0 %collective-permute-start = (bf16[3,4,16,2,4,256]{5,4,3,2,1,0:T(4,128)(2,1)S(1)}, bf16[3,4,16,2,4,256]{5,4,3,2,1,0:T(4,128)(2,1)S(1)}, u32[]{:S(2)}, u32[]{:S(2)}) collective-permute-start(bf16[3,4,16,2,4,256]{5,4,3,2,1,0:T(4,128)(2,1)S(1)} %get-tuple-element.19), channel_id=1, source_target_pairs={{0,1},{1,0},{2,3},{3,2},{4,5},{5,4},{6,7},{7,6},{8,9},{9,8},{10,11... | collective-permute-start | bytes 2359304 | tf_op jit(solution)/shard_map/ppermute | solution.py:406
  33.2 25.4 %collective-permute-start.1 = (bf16[3,4,16,2,4,256]{5,4,3,2,1,0:T(4,128)(2,1)S(1)}, bf16[3,4,16,2,4,256]{5,4,3,2,1,0:T(4,128)(2,1)S(1)}, u32[]{:S(2)}, u32[]{:S(2)}) collective-permute-start(bf16[3,4,16,2,4,256]{5,4,3,2,1,0:T(4,128)(2,1)S(1)} %get-tuple-element.20), channel_id=1, source_target_pairs={{0,2},{1,3},{2,0},{3,1},{4,6},{5,7},{6,4},{7,5},{8,10},{9,11},{10,... | collective-permute-start | bytes 2359304 | tf_op jit(solution)/shard_map/ppermute | solution.py:406
  33.7 38.6 %collective-permute-start.2 = (bf16[3,4,16,2,4,256]{5,4,3,2,1,0:T(4,128)(2,1)S(1)}, bf16[3,4,16,2,4,256]{5,4,3,2,1,0:T(4,128)(2,1)S(1)}, u32[]{:S(2)}, u32[]{:S(2)}) collective-permute-start(bf16[3,4,16,2,4,256]{5,4,3,2,1,0:T(4,128)(2,1)S(1)} %get-tuple-element.21), channel_id=1, source_target_pairs={{0,3},{1,2},{2,1},{3,0},{4,7},{5,6},{6,5},{7,4},{8,11},{9,10},{10,... | collective-permute-start | bytes 2359304 | tf_op jit(solution)/shard_map/ppermute | solution.py:406
  34.7 4.0 %collective-permute-start.9 = (bf16[1,4,16,2,4,256]{5,4,3,2,1,0:T(4,128)(2,1)S(1)}, bf16[1,4,16,2,4,256]{5,4,3,2,1,0:T(4,128)(2,1)S(1)}, u32[]{:S(2)}, u32[]{:S(2)}) collective-permute-start(bf16[1,4,16,2,4,256]{5,4,3,2,1,0:T(4,128)(2,1)S(1)} %get-tuple-element.27), channel_id=1, source_target_pairs={{0,1},{1,0},{2,3},{3,2},{4,5},{5,4},{6,7},{7,6},{8,9},{9,8},{10,11... | collective-permute-start | bytes 786440 | tf_op jit(solution)/shard_map/ppermute | solution.py:407
  38.7 9.2 %collective-permute-start.7 = (bf16[4,256,128]{2,1,0:T(8,128)(2,1)S(1)}, bf16[4,256,128]{2,1,0:T(8,128)(2,1)S(1)}, u32[]{:S(2)}, u32[]{:S(2)}) collective-permute-start(bf16[4,256,128]{2,1,0:T(8,128)(2,1)S(1)} %collective-permute-done.6.refs_2_.refs_5_), channel_id=1, source_target_pairs={{0,8},{1,9},{2,10},{3,11},{4,0},{5,1},{6,2},{7,3},{8,12},{9,13},{1... | collective-permute-start | bytes 786440 | tf_op jit(solution)/shard_map/ppermute | solution.py:420
  38.7 13.4 %collective-permute-start.4 = (bf16[3,256,128]{2,1,0:T(8,128)(2,1)S(1)}, bf16[3,256,128]{2,1,0:T(8,128)(2,1)S(1)}, u32[]{:S(2)}, u32[]{:S(2)}) collective-permute-start(bf16[3,256,128]{2,1,0:T(8,128)(2,1)S(1)} %collective-permute-done.3.refs_2_), channel_id=1, source_target_pairs={{0,8},{1,9},{2,10},{3,11},{4,0},{5,1},{6,2},{7,3},{8,12},{9,13},{1... | collective-permute-start | bytes 589832 | tf_op jit(solution)/shard_map/ppermute | solution.py:420
  47.9 9.8 %collective-permute-start.8 = (bf16[4,256,128]{2,1,0:T(8,128)(2,1)S(1)}, bf16[4,256,128]{2,1,0:T(8,128)(2,1)S(1)}, u32[]{:S(2)}, u32[]{:S(2)}) collective-permute-start(bf16[4,256,128]{2,1,0:T(8,128)(2,1)S(1)} %collective-permute-done.7.refs_3_.refs_6_), channel_id=1, source_target_pairs={{0,8},{1,9},{2,10},{3,11},{4,0},{5,1},{6,2},{7,3},{8,12},{9,13},{1... | collective-permute-start | bytes 786440 | tf_op jit(solution)/shard_map/ppermute | solution.py:420
  52.1 23.4 %collective-permute-start.5 = (bf16[3,256,128]{2,1,0:T(8,128)(2,1)S(1)}, bf16[3,256,128]{2,1,0:T(8,128)(2,1)S(1)}, u32[]{:S(2)}, u32[]{:S(2)}) collective-permute-start(bf16[3,256,128]{2,1,0:T(8,128)(2,1)S(1)} %collective-permute-done.4.refs_3_), channel_id=1, source_target_pairs={{0,8},{1,9},{2,10},{3,11},{4,0},{5,1},{6,2},{7,3},{8,12},{9,13},{1... | collective-permute-start | bytes 589832 | tf_op jit(solution)/shard_map/ppermute | solution.py:420
  57.7 15.5 %copy-start.1 = (f32[256,128]{1,0:T(8,128)S(1)}, f32[256,128]{1,0:T(8,128)}, u32[]{:S(2)}) copy-start(f32[256,128]{1,0:T(8,128)} %constant.27.clone.refs_5_) | copy-start | bytes 393220
  57.7 15.5 %copy-start.6 = (bf16[3,128,64]{2,1,0:T(8,128)(2,1)S(1)}, bf16[3,128,64]{2,1,0:T(8,128)(2,1)}, u32[]{:S(2)}) copy-start(bf16[3,128,64]{2,1,0:T(8,128)(2,1)} %constant.28.clone.refs_6_) | copy-start | bytes 147460
  57.7 15.5 %copy-start.7 = (bf16[3,128,64]{2,1,0:T(8,128)(2,1)S(1)}, bf16[3,128,64]{2,1,0:T(8,128)(2,1)}, u32[]{:S(2)}) copy-start(bf16[3,128,64]{2,1,0:T(8,128)(2,1)} %constant.29.clone.refs_7_) | copy-start | bytes 147460
  72.4 3.1 %copy-start.3 = (bf16[3,256,128]{2,1,0:T(8,128)(2,1)S(1)}, bf16[3,256,128]{2,1,0:T(8,128)(2,1)}, u32[]{:S(2)}) copy-start(bf16[3,256,128]{2,1,0:T(8,128)(2,1)} %get-tuple-element.24.refs_1_) | copy-start | bytes 589828
  72.4 3.1 %copy-start.4 = (bf16[3,128,64]{2,1,0:T(8,128)(2,1)S(1)}, bf16[3,128,64]{2,1,0:T(8,128)(2,1)}, u32[]{:S(2)}) copy-start(bf16[3,128,64]{2,1,0:T(8,128)(2,1)} %constant.30.clone.refs_6_) | copy-start | bytes 147460
  72.4 3.1 %copy-start.5 = (bf16[3,128,64]{2,1,0:T(8,128)(2,1)S(1)}, bf16[3,128,64]{2,1,0:T(8,128)(2,1)}, u32[]{:S(2)}) copy-start(bf16[3,128,64]{2,1,0:T(8,128)(2,1)} %constant.31.clone.refs_7_) | copy-start | bytes 147460
  73.2 14.0 %copy-start.11 = (bf16[256,64]{1,0:T(8,128)(2,1)S(1)}, bf16[256,64]{1,0:T(8,128)(2,1)}, u32[]{:S(2)}) copy-start(bf16[256,64]{1,0:T(8,128)(2,1)} %constant.35.clone) | copy-start | bytes 98308

commit v6 on v5

--- a/solution.py
+++ b/solution.py
@@ -285,9 +285,15 @@
 
 
 def predict_kernel(members, parts, slots, before, *refs):
+    for q in range(refs[0].shape[0]):
+        predict_band(members, parts, slots, before, q, *refs)
+
+
+def predict_band(members, parts, slots, before, q, *refs):
+    number = refs[0].shape[0]
     rows_in, refs = refs[:members], refs[members:]
     if members == 1:
-        matrix = rows_in[0][0]
+        matrix = rows_in[0][q]
     else:
         columns = merged(rows_in)
         matrix = columns[0] if len(columns) == 1 else jnp.concatenate(columns, axis=1)
@@ -295,11 +301,13 @@
     mask_ref, fold_a, fold_b = refs[slots * parts : slots * parts + 3]
     out = refs[-1]
     spectra = [
-        jnp.concatenate([spectra_in[p * slots + i][0] for p in range(parts)], axis=1)
+        jnp.concatenate([spectra_in[p * slots + i][q] for p in range(parts)], axis=1)
         for i in range(slots)
     ]
     spectra = spectra[0] if slots == 1 else jnp.concatenate(spectra, axis=0)
     dests, rows, _ = out.shape
+    dests //= number
+    span = pl.ds(q * dests, dests)
     total = dot(matrix, spectra)
     total = total.reshape(BAND, 2, rows, -1)
     acc = None
@@ -307,15 +315,15 @@
         value = total[:, c].reshape(BAND * rows, -1)
         value = jnp.where(mask_ref[...] != 0, value, 0.0)
         for piece in split(value, 2):
-            term = dot(piece, fold[0])
+            term = dot(piece, fold[q])
             acc = term if acc is None else acc + term
     acc = acc.reshape(dests, BAND // dests, rows, -1)
     value = acc[:, 0]
     for i in range(1, BAND // dests):
         value = value + acc[:, i]
     if before:
-        value = value + refs[-2][...].astype(F32)
-    out[...] = value.astype(out.dtype)
+        value = value + refs[-2][span].astype(F32)
+    out[span] = value.astype(out.dtype)
 
 
 def predict(matrix, spectra_parts, share, shots, first, part, before=None):
@@ -350,24 +358,21 @@
         jnp.asarray(fold_b.reshape(number, cols, lanes), BF16),
     ]
     dests = BAND // share
-    out_spec = pl.BlockSpec((dests, all_rows, lanes), lambda q: (q, 0, 0))
+    out_spec = pl.BlockSpec((number * dests, all_rows, lanes), lambda q: (0, 0, 0))
     flat = [x for spectra in spectra_parts for x in spectra]
-    starts = [first * (x.shape[0] > number) for x in flat]
+    starts = [first * (x.shape[0] > number) // number for x in flat]
     return pl.pallas_call(
         functools.partial(predict_kernel, len(matrix), parts, slots, before is not None),
-        grid=(number,),
+        grid=(1,),
         in_specs=[
-            pl.BlockSpec(
-                (1,) + x.shape[1:], functools.partial(lambda n, q: (q,) + (0,) * n, x.ndim - 1)
-            )
-            for x in matrix
+            pl.BlockSpec(x.shape, functools.partial(lambda n, q: (0,) * n, x.ndim)) for x in matrix
         ]
         + [
-            pl.BlockSpec((1, block, width), functools.partial(lambda a, q: (a + q, 0, 0), a))
+            pl.BlockSpec((number, block, width), functools.partial(lambda a, q: (a, 0, 0), a))
             for a in starts
         ]
         + [pl.BlockSpec(mask.shape, lambda q: (0, 0))]
-        + [pl.BlockSpec((1, cols, lanes), lambda q: (q, 0, 0))] * 2
+        + [pl.BlockSpec((number, cols, lanes), lambda q: (0, 0, 0))] * 2
         + ([] if before is None else [out_spec]),
         out_specs=out_spec,
         out_shape=jax.ShapeDtypeStruct((number * dests, all_rows, lanes), BF16),

time: 88.3 us -> 87.9 us (level)
  no operation moved by 1% of the time
where the time goes in v6:
time: 87.9 us; the launch traced here: 87.6 us
  waiting for transfers between devices  35.4 us (40%)
  Pallas kernels  22.9 us (26%)
  starting transfers between devices  18.7 us (21%)
  blocking collectives  9.2 us (10%)
    ppermute x9, waiting for transfers between devices, shards(): piece.append(lax.ppermute(piece[-1], 'rows', step))  18.4 us
    ppermute x3, waiting for transfers between devices, exchange(): first = lax.ppermute(first, 'rows', pairs)  13.7 us
    ppermute x9, starting transfers between devices, shards(): piece.append(lax.ppermute(piece[-1], 'rows', step))  13.3 us
    pallas_call x2, Pallas kernels, spectra_of(): pl.pallas_call(functools.partial(spectra_kernel, bands, bins, taps, part,...  11.6 us
    all_to_all x1, blocking collectives, shards(): lax.all_to_all(partial_value, 'rows', split_axis=0, concat_axis=0, tiled=...  9.2 us
    pallas_call x4, Pallas kernels, rows_for(): pl.pallas_call(functools.partial(rows_kernel, block, head, starts), in_sp...  5.56 us
    pallas_call x3, Pallas kernels, predict(): pl.pallas_call(functools.partial(predict_kernel, len(matrix), parts, slot...  4.94 us
    ppermute x3, waiting for transfers between devices, exchange(): rest = lax.ppermute(rest, 'rows', pairs)  3.3 us
  transfers between devices with their start and end apart: 15, of which 6 were waited for; matrix products, arithmetic and copies ran while one was open for 0% of the time, Pallas kernels for 17%

profile of v6, /device:TPU:0, one launch (start us, length us, event | category | flops | bytes accessed | tf_op | source)
XLA Modules:
  0.0 87.6 jit_solution(4209910098944076286)
XLA Ops:
  0.0 5.9 %spectra.2 = (bf16[4,256,128]{2,1,0:T(8,128)(2,1)}, bf16[128,256]{1,0:T(8,128)(2,1)}, bf16[512,128]{1,0:T(8,128)(2,1)}) custom-call(bf16[8,256,2048]{2,1,0:T(8,128)(2,1)} %refs_0_.3, s32[8,256]{1,0:T(8,128)} %refs_1_.3, bf16[2048,256]{1,0:T(8,128)(2,1)} %constant.24.clone.refs_2_, f32[16,32]{1,0:T(8,128)} %refs_3_.1, f32[32,256]{1,0:T(8,128)} %constant.25.clone.refs_4_, ...), custom_call_target="tpu_custom_call" | custom-call | flops 1073741824 | bytes 4194304 | tf_op jit(solution)/shard_map/spectra/pallas_call | solution.py:174
  5.9 4.1 %collective-permute-start.6 = (bf16[4,256,128]{2,1,0:T(8,128)(2,1)}, bf16[4,256,128]{2,1,0:T(8,128)(2,1)S(1)}, u32[]{:S(2)}, u32[]{:S(2)}) collective-permute-start(bf16[4,256,128]{2,1,0:T(8,128)(2,1)} %get-tuple-element.25.refs_1_.refs_4_), channel_id=1, source_target_pairs={{0,8},{1,9},{2,10},{3,11},{4,0},{5,1},{6,2},{7,3},{8,12},{9,13},{1... | collective-permute-start | bytes 786440 | tf_op jit(solution)/shard_map/ppermute | solution.py:425
  10.0 5.8 %spectra.3 = (bf16[3,256,128]{2,1,0:T(8,128)(2,1)}, bf16[1,256,128]{2,1,0:T(8,128)(2,1)}) custom-call(bf16[8,256,2048]{2,1,0:T(8,128)(2,1)} %refs_0_.3, s32[8,256]{1,0:T(8,128)} %refs_1_.3, bf16[2048,256]{1,0:T(8,128)(2,1)} %constant.24.clone.refs_2_, bf16[128,256]{1,0:T(8,128)(2,1)} %get-tuple-element.22.refs_3_, bf16[512,128]{1,0:T(8,128)(2,1)} %get-tuple-element.23.refs_4_), custom_call_target="tpu_custom_call" | custom-call | flops 1073741824 | bytes 4194304 | tf_op jit(solution)/shard_map/spectra/pallas_call | solution.py:174
  15.8 1.6 %collective-permute-start.12 = (bf16[1,256,128]{2,1,0:T(8,128)(2,1)}, bf16[1,256,128]{2,1,0:T(8,128)(2,1)S(1)}, u32[]{:S(2)}, u32[]{:S(2)}) collective-permute-start(bf16[1,256,128]{2,1,0:T(8,128)(2,1)} %get-tuple-element.30.refs_8_), channel_id=1, source_target_pairs={{0,8},{1,9},{2,10},{3,11},{4,0},{5,1},{6,2},{7,3},{8,12},{9,13},{1... | collective-permute-start | bytes 196616 | tf_op jit(solution)/shard_map/ppermute | solution.py:425
  17.4 0.3 collective-permute-start.3
  17.7 3.3 %collective-permute-done.12.refs_9_ = bf16[1,256,128]{2,1,0:T(8,128)(2,1)S(1)} collective-permute-done((bf16[1,256,128]{2,1,0:T(8,128)(2,1)}, bf16[1,256,128]{2,1,0:T(8,128)(2,1)S(1)}, u32[]{:S(2)}, u32[]{:S(2)}) %collective-permute-start.12) | collective-permute-done | bytes 65568 | tf_op jit(solution)/shard_map/ppermute | solution.py:425
  21.0 2.5 %collective-permute-start.13 = (bf16[1,256,128]{2,1,0:T(8,128)(2,1)S(1)}, bf16[1,256,128]{2,1,0:T(8,128)(2,1)S(1)}, u32[]{:S(2)}, u32[]{:S(2)}) collective-permute-start(bf16[1,256,128]{2,1,0:T(8,128)(2,1)S(1)} %collective-permute-done.12.refs_9_), channel_id=1, source_target_pairs={{0,8},{1,9},{2,10},{3,11},{4,0},{5,1},{6,2},{7,3},{8,12},{9,13},{1... | collective-permute-start | bytes 196616 | tf_op jit(solution)/shard_map/ppermute | solution.py:425
  23.5 1.4 %rows_for.6 = (bf16[3,4,16,2,4,256]{5,4,3,2,1,0:T(4,128)(2,1)S(1)}, bf16[1,4,16,2,4,256]{5,4,3,2,1,0:T(4,128)(2,1)S(1)}) custom-call(bf16[4,16,2,4,4096]{4,3,2,1,0:T(4,128)(2,1)} %bitcast.5), custom_call_target="tpu_custom_call" | custom-call | tf_op jit(solution)/shard_map/rows_for/pallas_call | solution.py:241
  24.9 1.6 %collective-permute-start.10 = (bf16[1,4,16,2,4,256]{5,4,3,2,1,0:T(4,128)(2,1)S(1)}, bf16[1,4,16,2,4,256]{5,4,3,2,1,0:T(4,128)(2,1)S(1)}, u32[]{:S(2)}, u32[]{:S(2)}) collective-permute-start(bf16[1,4,16,2,4,256]{5,4,3,2,1,0:T(4,128)(2,1)S(1)} %get-tuple-element.28), channel_id=1, source_target_pairs={{0,2},{1,3},{2,0},{3,1},{4,6},{5,7},{6,4},{7,5},{8,10},{9,11},{10,... | collective-permute-start | bytes 786440 | tf_op jit(solution)/shard_map/ppermute | solution.py:412
  26.4 0.0 collective-permute-done.13.refs_10_
  26.4 2.2 %collective-permute-start.14 = (bf16[1,256,128]{2,1,0:T(8,128)(2,1)S(1)}, bf16[1,256,128]{2,1,0:T(8,128)(2,1)S(1)}, u32[]{:S(2)}, u32[]{:S(2)}) collective-permute-start(bf16[1,256,128]{2,1,0:T(8,128)(2,1)S(1)} %collective-permute-done.13.refs_10_), channel_id=1, source_target_pairs={{0,8},{1,9},{2,10},{3,11},{4,0},{5,1},{6,2},{7,3},{8,12},{9,13},{1... | collective-permute-start | bytes 196616 | tf_op jit(solution)/shard_map/ppermute | solution.py:425
  28.6 1.4 %rows_for.7 = (bf16[3,4,16,2,4,256]{5,4,3,2,1,0:T(4,128)(2,1)S(1)}, bf16[1,4,16,2,4,256]{5,4,3,2,1,0:T(4,128)(2,1)S(1)}) custom-call(bf16[4,16,2,4,4096]{4,3,2,1,0:T(4,128)(2,1)} %bitcast.6), custom_call_target="tpu_custom_call" | custom-call | tf_op jit(solution)/shard_map/rows_for/pallas_call | solution.py:241
  30.0 0.0 copy-start.2
  30.0 0.0 copy-start.8
  30.1 0.0 copy-start.9
  30.1 0.1 collective-permute-start.11
  30.2 1.4 %rows_for.5 = (bf16[3,4,16,2,4,256]{5,4,3,2,1,0:T(4,128)(2,1)S(1)}, bf16[1,4,16,2,4,256]{5,4,3,2,1,0:T(4,128)(2,1)S(1)}) custom-call(bf16[4,16,2,4,4096]{4,3,2,1,0:T(4,128)(2,1)} %bitcast.7), custom_call_target="tpu_custom_call" | custom-call | tf_op jit(solution)/shard_map/rows_for/pallas_call | solution.py:241
  31.6 0.0 collective-permute-done.14.refs_11_
  31.6 1.6 %collective-permute-start = (bf16[3,4,16,2,4,256]{5,4,3,2,1,0:T(4,128)(2,1)S(1)}, bf16[3,4,16,2,4,256]{5,4,3,2,1,0:T(4,128)(2,1)S(1)}, u32[]{:S(2)}, u32[]{:S(2)}) collective-permute-start(bf16[3,4,16,2,4,256]{5,4,3,2,1,0:T(4,128)(2,1)S(1)} %get-tuple-element.19), channel_id=1, source_target_pairs={{0,1},{1,0},{2,3},{3,2},{4,5},{5,4},{6,7},{7,6},{8,9},{9,8},{10,11... | collective-permute-start | bytes 2359304 | tf_op jit(solution)/shard_map/ppermute | solution.py:411
  33.2 0.0 collective-permute-done.3.refs_2_
  33.2 0.5 collective-permute-start.1
  33.7 0.0 collective-permute-done.6.refs_2_.refs_5_
  33.7 0.9 %collective-permute-start.2 = (bf16[3,4,16,2,4,256]{5,4,3,2,1,0:T(4,128)(2,1)S(1)}, bf16[3,4,16,2,4,256]{5,4,3,2,1,0:T(4,128)(2,1)S(1)}, u32[]{:S(2)}, u32[]{:S(2)}) collective-permute-start(bf16[3,4,16,2,4,256]{5,4,3,2,1,0:T(4,128)(2,1)S(1)} %get-tuple-element.21), channel_id=1, source_target_pairs={{0,3},{1,2},{2,1},{3,0},{4,7},{5,6},{6,5},{7,4},{8,11},{9,10},{10,... | collective-permute-start | bytes 2359304 | tf_op jit(solution)/shard_map/ppermute | solution.py:411
  34.7 0.0 collective-permute-done.10.refs_2_
  34.7 0.7 collective-permute-start.9
  35.4 3.3 %collective-permute-done.11.refs_3_ = bf16[1,4,16,2,4,256]{5,4,3,2,1,0:T(4,128)(2,1)S(1)} collective-permute-done((bf16[1,4,16,2,4,256]{5,4,3,2,1,0:T(4,128)(2,1)S(1)}, bf16[1,4,16,2,4,256]{5,4,3,2,1,0:T(4,128)(2,1)S(1)}, u32[]{:S(2)}, u32[]{:S(2)}) %collective-permute-start.11) | collective-permute-done | bytes 262176 | tf_op jit(solution)/shard_map/ppermute | solution.py:412
  38.7 0.0 collective-permute-start.7
  38.7 0.0 collective-permute-done.9.refs_1_
  38.7 0.7 collective-permute-start.4
  39.4 8.5 %collective-permute-done.7.refs_3_.refs_6_ = bf16[4,256,128]{2,1,0:T(8,128)(2,1)S(1)} collective-permute-done((bf16[4,256,128]{2,1,0:T(8,128)(2,1)S(1)}, bf16[4,256,128]{2,1,0:T(8,128)(2,1)S(1)}, u32[]{:S(2)}, u32[]{:S(2)}) %collective-permute-start.7) | collective-permute-done | bytes 262176 | tf_op jit(solution)/shard_map/ppermute | solution.py:425
  47.9 0.9 %collective-permute-start.8 = (bf16[4,256,128]{2,1,0:T(8,128)(2,1)S(1)}, bf16[4,256,128]{2,1,0:T(8,128)(2,1)S(1)}, u32[]{:S(2)}, u32[]{:S(2)}) collective-permute-start(bf16[4,256,128]{2,1,0:T(8,128)(2,1)S(1)} %collective-permute-done.7.refs_3_.refs_6_), channel_id=1, source_target_pairs={{0,8},{1,9},{2,10},{3,11},{4,0},{5,1},{6,2},{7,3},{8,12},{9,13},{1... | collective-permute-start | bytes 786440 | tf_op jit(solution)/shard_map/ppermute | solution.py:425
  48.8 3.3 %collective-permute-done.4.refs_3_ = bf16[3,256,128]{2,1,0:T(8,128)(2,1)S(1)} collective-permute-done((bf16[3,256,128]{2,1,0:T(8,128)(2,1)S(1)}, bf16[3,256,128]{2,1,0:T(8,128)(2,1)S(1)}, u32[]{:S(2)}, u32[]{:S(2)}) %collective-permute-start.4) | collective-permute-done | bytes 196640 | tf_op jit(solution)/shard_map/ppermute | solution.py:425
  52.1 0.9 %collective-permute-start.5 = (bf16[3,256,128]{2,1,0:T(8,128)(2,1)S(1)}, bf16[3,256,128]{2,1,0:T(8,128)(2,1)S(1)}, u32[]{:S(2)}, u32[]{:S(2)}) collective-permute-start(bf16[3,256,128]{2,1,0:T(8,128)(2,1)S(1)} %collective-permute-done.4.refs_3_), channel_id=1, source_target_pairs={{0,8},{1,9},{2,10},{3,11},{4,0},{5,1},{6,2},{7,3},{8,12},{9,13},{1... | collective-permute-start | bytes 589832 | tf_op jit(solution)/shard_map/ppermute | solution.py:425
  53.0 1.4 %rows_for.4 = (bf16[3,4,16,2,4,256]{5,4,3,2,1,0:T(4,128)(2,1)S(1)}, bf16[1,4,16,2,4,256]{5,4,3,2,1,0:T(4,128)(2,1)S(1)}) custom-call(bf16[4,16,2,4,4096]{4,3,2,1,0:T(4,128)(2,1)} %bitcast.8), custom_call_target="tpu_custom_call" | custom-call | tf_op jit(solution)/shard_map/rows_for/pallas_call | solution.py:241
  54.3 3.3 %collective-permute-done.8.refs_4_.refs_7_ = bf16[4,256,128]{2,1,0:T(8,128)(2,1)S(1)} collective-permute-done((bf16[4,256,128]{2,1,0:T(8,128)(2,1)S(1)}, bf16[4,256,128]{2,1,0:T(8,128)(2,1)S(1)}, u32[]{:S(2)}, u32[]{:S(2)}) %collective-permute-start.8) | collective-permute-done | bytes 262176 | tf_op jit(solution)/shard_map/ppermute | solution.py:425
  57.7 0.0 copy-start.1
  57.7 0.0 copy-start.6
  57.7 0.0 copy-start.7
  57.8 0.9 %predict.5 = bf16[4,16,64]{2,1,0:T(8,128)(2,1)S(1)} custom-call(bf16[1,4,16,2,4,256]{5,4,3,2,1,0:T(4,128)(2,1)S(1)} %get-tuple-element.26.refs_0_, bf16[1,4,16,2,4,256]{5,4,3,2,1,0:T(4,128)(2,1)S(1)} %collective-permute-done.9.refs_1_, bf16[1,4,16,2,4,256]{5,4,3,2,1,0:T(4,128)(2,1)S(1)} %collective-permute-done.10.refs_2_, ...), custom_call_target="tpu_custom_call" | custom-call | tf_op jit(solution)/shard_map/predict/pallas_call | solution.py:364
  58.7 13.7 %collective-permute-done.2.refs_3_ = bf16[3,4,16,2,4,256]{5,4,3,2,1,0:T(4,128)(2,1)S(1)} collective-permute-done((bf16[3,4,16,2,4,256]{5,4,3,2,1,0:T(4,128)(2,1)S(1)}, bf16[3,4,16,2,4,256]{5,4,3,2,1,0:T(4,128)(2,1)S(1)}, u32[]{:S(2)}, u32[]{:S(2)}) %collective-permute-start.2) | collective-permute-done | bytes 786464 | tf_op jit(solution)/shard_map/ppermute | solution.py:411
  72.4 0.8 merge.1.refs_0_
  73.2 0.0 copy-start.11
  73.2 2.0 %predict.3.refs_8_ = bf16[12,16,64]{2,1,0:T(8,128)(2,1)S(1)} custom-call(bf16[3,512,1024]{2,1,0:T(8,128)(2,1)S(1)} %merge.1.refs_0_, bf16[4,256,128]{2,1,0:T(8,128)(2,1)S(1)} %copy-done, bf16[4,256,128]{2,1,0:T(8,128)(2,1)S(1)} %collective-permute-done.6.refs_2_.refs_5_, bf16[4,256,128]{2,1,0:T(8,128)(2,1)S(1)} %collective-permute-done.7.refs_3_.refs_6_, ...), custom_call_target="tpu_custom_call" | custom-call | tf_op jit(solution)/shard_map/predict/pallas_call | solution.py:364
  75.3 2.0 %predict.4 = bf16[12,16,64]{2,1,0:T(8,128)(2,1)S(1)} custom-call(bf16[3,512,1024]{2,1,0:T(8,128)(2,1)S(1)} %merge.1.refs_0_, bf16[3,256,128]{2,1,0:T(8,128)(2,1)S(1)} %copy-done.3, bf16[3,256,128]{2,1,0:T(8,128)(2,1)S(1)} %collective-permute-done.3.refs_2_, bf16[3,256,128]{2,1,0:T(8,128)(2,1)S(1)} %collective-permute-done.4.refs_3_, ...), custom_call_target="tpu_custom_call" | custom-call | tf_op jit(solution)/shard_map/predict/pallas_call | solution.py:364
  77.4 0.1 reshape.15
  77.5 9.2 %all_to_all.5 = bf16[16,2,512]{2,1,0:T(2,128)(2,1)S(1)} all-to-all(bf16[16,2,512]{2,1,0:T(2,128)(2,1)S(1)} %reshape.15), channel_id=1, replica_groups=mesh['parts'=2,'rows'=16] {'rows'}, dimensions={0} | all-to-all | bytes 65536 | tf_op jit(solution)/shard_map/all_to_all | solution.py:440
  86.7 0.1 reshape.16
  86.8 0.8 convolution_convert_fusion
  (21 shorter events, 0.1 us)
Async XLA Ops:
  5.9 27.9 %collective-permute-start.6 = (bf16[4,256,128]{2,1,0:T(8,128)(2,1)}, bf16[4,256,128]{2,1,0:T(8,128)(2,1)S(1)}, u32[]{:S(2)}, u32[]{:S(2)}) collective-permute-start(bf16[4,256,128]{2,1,0:T(8,128)(2,1)} %get-tuple-element.25.refs_1_.refs_4_), channel_id=1, source_target_pairs={{0,8},{1,9},{2,10},{3,11},{4,0},{5,1},{6,2},{7,3},{8,12},{9,13},{1... | collective-permute-start | bytes 786440 | tf_op jit(solution)/shard_map/ppermute | solution.py:425
  15.8 5.2 %collective-permute-start.12 = (bf16[1,256,128]{2,1,0:T(8,128)(2,1)}, bf16[1,256,128]{2,1,0:T(8,128)(2,1)S(1)}, u32[]{:S(2)}, u32[]{:S(2)}) collective-permute-start(bf16[1,256,128]{2,1,0:T(8,128)(2,1)} %get-tuple-element.30.refs_8_), channel_id=1, source_target_pairs={{0,8},{1,9},{2,10},{3,11},{4,0},{5,1},{6,2},{7,3},{8,12},{9,13},{1... | collective-permute-start | bytes 196616 | tf_op jit(solution)/shard_map/ppermute | solution.py:425
  17.4 15.8 %collective-permute-start.3 = (bf16[3,256,128]{2,1,0:T(8,128)(2,1)}, bf16[3,256,128]{2,1,0:T(8,128)(2,1)S(1)}, u32[]{:S(2)}, u32[]{:S(2)}) collective-permute-start(bf16[3,256,128]{2,1,0:T(8,128)(2,1)} %get-tuple-element.24.refs_1_), channel_id=1, source_target_pairs={{0,8},{1,9},{2,10},{3,11},{4,0},{5,1},{6,2},{7,3},{8,12},{9,13},{1... | collective-permute-start | bytes 589832 | tf_op jit(solution)/shard_map/ppermute | solution.py:425
  21.0 5.4 %collective-permute-start.13 = (bf16[1,256,128]{2,1,0:T(8,128)(2,1)S(1)}, bf16[1,256,128]{2,1,0:T(8,128)(2,1)S(1)}, u32[]{:S(2)}, u32[]{:S(2)}) collective-permute-start(bf16[1,256,128]{2,1,0:T(8,128)(2,1)S(1)} %collective-permute-done.12.refs_9_), channel_id=1, source_target_pairs={{0,8},{1,9},{2,10},{3,11},{4,0},{5,1},{6,2},{7,3},{8,12},{9,13},{1... | collective-permute-start | bytes 196616 | tf_op jit(solution)/shard_map/ppermute | solution.py:425
  24.9 9.8 %collective-permute-start.10 = (bf16[1,4,16,2,4,256]{5,4,3,2,1,0:T(4,128)(2,1)S(1)}, bf16[1,4,16,2,4,256]{5,4,3,2,1,0:T(4,128)(2,1)S(1)}, u32[]{:S(2)}, u32[]{:S(2)}) collective-permute-start(bf16[1,4,16,2,4,256]{5,4,3,2,1,0:T(4,128)(2,1)S(1)} %get-tuple-element.28), channel_id=1, source_target_pairs={{0,2},{1,3},{2,0},{3,1},{4,6},{5,7},{6,4},{7,5},{8,10},{9,11},{10,... | collective-permute-start | bytes 786440 | tf_op jit(solution)/shard_map/ppermute | solution.py:412
  26.4 5.2 %collective-permute-start.14 = (bf16[1,256,128]{2,1,0:T(8,128)(2,1)S(1)}, bf16[1,256,128]{2,1,0:T(8,128)(2,1)S(1)}, u32[]{:S(2)}, u32[]{:S(2)}) collective-permute-start(bf16[1,256,128]{2,1,0:T(8,128)(2,1)S(1)} %collective-permute-done.13.refs_10_), channel_id=1, source_target_pairs={{0,8},{1,9},{2,10},{3,11},{4,0},{5,1},{6,2},{7,3},{8,12},{9,13},{1... | collective-permute-start | bytes 196616 | tf_op jit(solution)/shard_map/ppermute | solution.py:425
  30.0 27.7 %copy-start = (bf16[4,256,128]{2,1,0:T(8,128)(2,1)S(1)}, bf16[4,256,128]{2,1,0:T(8,128)(2,1)}, u32[]{:S(2)}) copy-start(bf16[4,256,128]{2,1,0:T(8,128)(2,1)} %get-tuple-element.25.refs_1_.refs_4_) | copy-start | bytes 786436
  30.0 27.7 %copy-start.2 = (f32[256,256]{1,0:T(8,128)S(1)}, f32[256,256]{1,0:T(8,128)}, u32[]{:S(2)}) copy-start(f32[256,256]{1,0:T(8,128)} %constant.32.clone.refs_12_) | copy-start | bytes 786436
  30.0 27.7 %copy-start.8 = (bf16[1,256,64]{2,1,0:T(8,128)(2,1)S(1)}, bf16[1,256,64]{2,1,0:T(8,128)(2,1)}, u32[]{:S(2)}) copy-start(bf16[1,256,64]{2,1,0:T(8,128)(2,1)} %constant.33.clone.refs_13_) | copy-start | bytes 98308
  30.1 27.6 %copy-start.9 = (bf16[1,256,64]{2,1,0:T(8,128)(2,1)S(1)}, bf16[1,256,64]{2,1,0:T(8,128)(2,1)}, u32[]{:S(2)}) copy-start(bf16[1,256,64]{2,1,0:T(8,128)(2,1)} %constant.34.clone.refs_14_) | copy-start | bytes 98308
  30.1 27.6 %copy-start.10 = (bf16[1,256,128]{2,1,0:T(8,128)(2,1)S(1)}, bf16[1,256,128]{2,1,0:T(8,128)(2,1)}, u32[]{:S(2)}) copy-start(bf16[1,256,128]{2,1,0:T(8,128)(2,1)} %get-tuple-element.30.refs_8_) | copy-start | bytes 196612
  30.1 8.6 %collective-permute-start.11 = (bf16[1,4,16,2,4,256]{5,4,3,2,1,0:T(4,128)(2,1)S(1)}, bf16[1,4,16,2,4,256]{5,4,3,2,1,0:T(4,128)(2,1)S(1)}, u32[]{:S(2)}, u32[]{:S(2)}) collective-permute-start(bf16[1,4,16,2,4,256]{5,4,3,2,1,0:T(4,128)(2,1)S(1)} %get-tuple-element.29), channel_id=1, source_target_pairs={{0,3},{1,2},{2,1},{3,0},{4,7},{5,6},{6,5},{7,4},{8,11},{9,10},{10,... | collective-permute-start | bytes 786440 | tf_op jit(solution)/shard_map/ppermute | solution.py:412
  31.6 27.0 %collective-permute-start = (bf16[3,4,16,2,4,256]{5,4,3,2,1,0:T(4,128)(2,1)S(1)}, bf16[3,4,16,2,4,256]{5,4,3,2,1,0:T(4,128)(2,1)S(1)}, u32[]{:S(2)}, u32[]{:S(2)}) collective-permute-start(bf16[3,4,16,2,4,256]{5,4,3,2,1,0:T(4,128)(2,1)S(1)} %get-tuple-element.19), channel_id=1, source_target_pairs={{0,1},{1,0},{2,3},{3,2},{4,5},{5,4},{6,7},{7,6},{8,9},{9,8},{10,11... | collective-permute-start | bytes 2359304 | tf_op jit(solution)/shard_map/ppermute | solution.py:411
  33.2 25.4 %collective-permute-start.1 = (bf16[3,4,16,2,4,256]{5,4,3,2,1,0:T(4,128)(2,1)S(1)}, bf16[3,4,16,2,4,256]{5,4,3,2,1,0:T(4,128)(2,1)S(1)}, u32[]{:S(2)}, u32[]{:S(2)}) collective-permute-start(bf16[3,4,16,2,4,256]{5,4,3,2,1,0:T(4,128)(2,1)S(1)} %get-tuple-element.20), channel_id=1, source_target_pairs={{0,2},{1,3},{2,0},{3,1},{4,6},{5,7},{6,4},{7,5},{8,10},{9,11},{10,... | collective-permute-start | bytes 2359304 | tf_op jit(solution)/shard_map/ppermute | solution.py:411
  33.7 38.6 %collective-permute-start.2 = (bf16[3,4,16,2,4,256]{5,4,3,2,1,0:T(4,128)(2,1)S(1)}, bf16[3,4,16,2,4,256]{5,4,3,2,1,0:T(4,128)(2,1)S(1)}, u32[]{:S(2)}, u32[]{:S(2)}) collective-permute-start(bf16[3,4,16,2,4,256]{5,4,3,2,1,0:T(4,128)(2,1)S(1)} %get-tuple-element.21), channel_id=1, source_target_pairs={{0,3},{1,2},{2,1},{3,0},{4,7},{5,6},{6,5},{7,4},{8,11},{9,10},{10,... | collective-permute-start | bytes 2359304 | tf_op jit(solution)/shard_map/ppermute | solution.py:411
  34.7 4.0 %collective-permute-start.9 = (bf16[1,4,16,2,4,256]{5,4,3,2,1,0:T(4,128)(2,1)S(1)}, bf16[1,4,16,2,4,256]{5,4,3,2,1,0:T(4,128)(2,1)S(1)}, u32[]{:S(2)}, u32[]{:S(2)}) collective-permute-start(bf16[1,4,16,2,4,256]{5,4,3,2,1,0:T(4,128)(2,1)S(1)} %get-tuple-element.27), channel_id=1, source_target_pairs={{0,1},{1,0},{2,3},{3,2},{4,5},{5,4},{6,7},{7,6},{8,9},{9,8},{10,11... | collective-permute-start | bytes 786440 | tf_op jit(solution)/shard_map/ppermute | solution.py:412
  38.7 9.2 %collective-permute-start.7 = (bf16[4,256,128]{2,1,0:T(8,128)(2,1)S(1)}, bf16[4,256,128]{2,1,0:T(8,128)(2,1)S(1)}, u32[]{:S(2)}, u32[]{:S(2)}) collective-permute-start(bf16[4,256,128]{2,1,0:T(8,128)(2,1)S(1)} %collective-permute-done.6.refs_2_.refs_5_), channel_id=1, source_target_pairs={{0,8},{1,9},{2,10},{3,11},{4,0},{5,1},{6,2},{7,3},{8,12},{9,13},{1... | collective-permute-start | bytes 786440 | tf_op jit(solution)/shard_map/ppermute | solution.py:425
  38.7 13.4 %collective-permute-start.4 = (bf16[3,256,128]{2,1,0:T(8,128)(2,1)S(1)}, bf16[3,256,128]{2,1,0:T(8,128)(2,1)S(1)}, u32[]{:S(2)}, u32[]{:S(2)}) collective-permute-start(bf16[3,256,128]{2,1,0:T(8,128)(2,1)S(1)} %collective-permute-done.3.refs_2_), channel_id=1, source_target_pairs={{0,8},{1,9},{2,10},{3,11},{4,0},{5,1},{6,2},{7,3},{8,12},{9,13},{1... | collective-permute-start | bytes 589832 | tf_op jit(solution)/shard_map/ppermute | solution.py:425
  47.9 9.8 %collective-permute-start.8 = (bf16[4,256,128]{2,1,0:T(8,128)(2,1)S(1)}, bf16[4,256,128]{2,1,0:T(8,128)(2,1)S(1)}, u32[]{:S(2)}, u32[]{:S(2)}) collective-permute-start(bf16[4,256,128]{2,1,0:T(8,128)(2,1)S(1)} %collective-permute-done.7.refs_3_.refs_6_), channel_id=1, source_target_pairs={{0,8},{1,9},{2,10},{3,11},{4,0},{5,1},{6,2},{7,3},{8,12},{9,13},{1... | collective-permute-start | bytes 786440 | tf_op jit(solution)/shard_map/ppermute | solution.py:425
  52.1 23.2 %collective-permute-start.5 = (bf16[3,256,128]{2,1,0:T(8,128)(2,1)S(1)}, bf16[3,256,128]{2,1,0:T(8,128)(2,1)S(1)}, u32[]{:S(2)}, u32[]{:S(2)}) collective-permute-start(bf16[3,256,128]{2,1,0:T(8,128)(2,1)S(1)} %collective-permute-done.4.refs_3_), channel_id=1, source_target_pairs={{0,8},{1,9},{2,10},{3,11},{4,0},{5,1},{6,2},{7,3},{8,12},{9,13},{1... | collective-permute-start | bytes 589832 | tf_op jit(solution)/shard_map/ppermute | solution.py:425
  57.7 15.5 %copy-start.1 = (f32[256,128]{1,0:T(8,128)S(1)}, f32[256,128]{1,0:T(8,128)}, u32[]{:S(2)}) copy-start(f32[256,128]{1,0:T(8,128)} %constant.27.clone.refs_5_) | copy-start | bytes 393220
  57.7 15.5 %copy-start.6 = (bf16[3,128,64]{2,1,0:T(8,128)(2,1)S(1)}, bf16[3,128,64]{2,1,0:T(8,128)(2,1)}, u32[]{:S(2)}) copy-start(bf16[3,128,64]{2,1,0:T(8,128)(2,1)} %constant.28.clone.refs_6_) | copy-start | bytes 147460
  57.7 15.5 %copy-start.7 = (bf16[3,128,64]{2,1,0:T(8,128)(2,1)S(1)}, bf16[3,128,64]{2,1,0:T(8,128)(2,1)}, u32[]{:S(2)}) copy-start(bf16[3,128,64]{2,1,0:T(8,128)(2,1)} %constant.29.clone.refs_7_) | copy-start | bytes 147460
  72.4 2.9 %copy-start.3 = (bf16[3,256,128]{2,1,0:T(8,128)(2,1)S(1)}, bf16[3,256,128]{2,1,0:T(8,128)(2,1)}, u32[]{:S(2)}) copy-start(bf16[3,256,128]{2,1,0:T(8,128)(2,1)} %get-tuple-element.24.refs_1_) | copy-start | bytes 589828
  72.4 2.9 %copy-start.4 = (bf16[3,128,64]{2,1,0:T(8,128)(2,1)S(1)}, bf16[3,128,64]{2,1,0:T(8,128)(2,1)}, u32[]{:S(2)}) copy-start(bf16[3,128,64]{2,1,0:T(8,128)(2,1)} %constant.30.clone.refs_6_) | copy-start | bytes 147460
  72.4 2.9 %copy-start.5 = (bf16[3,128,64]{2,1,0:T(8,128)(2,1)S(1)}, bf16[3,128,64]{2,1,0:T(8,128)(2,1)}, u32[]{:S(2)}) copy-start(bf16[3,128,64]{2,1,0:T(8,128)(2,1)} %constant.31.clone.refs_7_) | copy-start | bytes 147460
  73.2 13.6 %copy-start.11 = (bf16[256,64]{1,0:T(8,128)(2,1)S(1)}, bf16[256,64]{1,0:T(8,128)(2,1)}, u32[]{:S(2)}) copy-start(bf16[256,64]{1,0:T(8,128)(2,1)} %constant.35.clone) | copy-start | bytes 98308

commit v7 on v6

--- a/solution.py
+++ b/solution.py
@@ -157,7 +157,7 @@
     bins, taps = filters.shape
     bands = freqs // BAND
     width = 2 * freqs
-    group = 2
+    group = 4
     main, resp, tail = transform_tables(freqs, length, taps)
     per = width // (2 * BAND)
     made = [
@@ -292,7 +292,7 @@
 def predict_band(members, parts, slots, before, q, *refs):
     number = refs[0].shape[0]
     rows_in, refs = refs[:members], refs[members:]
-    if members == 1:
+    if len(rows_in[0].shape) == 3:
         matrix = rows_in[0][q]
     else:
         columns = merged(rows_in)
@@ -435,7 +435,13 @@
     head_piece, rest_piece = pieces[quads - 1][1], pieces[-1][1]
     early = predict(first_matrix, whole_pieces, share, shot_count, 0, 0)
     early = predict(first_matrix, [head_piece], share, shot_count, 0, quads - 1, early)
-    late = predict(rest_parts, whole_pieces + [rest_piece], share, shot_count, head, 0)
+    absent = members // 2
+    others = [x for m, x in enumerate(rest_parts) if m != absent or members == 1]
+    late = predict(others, whole_pieces + [rest_piece], share, shot_count, head, 0)
+    if len(others) < members:
+        last = predict([rest_parts[absent]], whole_pieces + [rest_piece], share, shot_count, head, 0)
+        at = absent * row_count
+        late = jnp.concatenate([late[:, :at], last, late[:, at:]], axis=1)
     partial_value = jnp.concatenate([early, late], axis=0)
     received = lax.all_to_all(partial_value, "rows", split_axis=0, concat_axis=0, tiled=True)
     choose = np.zeros((lines, members, members, row_count, lines, members, row_count))

time: 87.9 us -> 90.4 us (1.028)
  starting transfers between devices: 18.7 us -> 24.5 us
  waiting for transfers between devices: 35.4 us -> 31.3 us
    ppermute x3, waiting for transfers between devices: 13.7 us -> 0.01 us  [exchange(): first = lax.ppermute(first, 'rows', pairs)]
    ppermute x3, waiting for transfers between devices: 3.3 us -> 16.9 us  [exchange(): rest = lax.ppermute(rest, 'rows', pairs)]
    ppermute x9, starting transfers between devices: 13.3 us -> 20.5 us  [shards(): piece.append(lax.ppermute(piece[-1], 'rows', step))]
    ppermute x9, waiting for transfers between devices: 18.4 us -> 14.5 us  [shards(): piece.append(lax.ppermute(piece[-1], 'rows', step))]
    ppermute x3, starting transfers between devices: 3.05 us -> 1.86 us  [exchange(): first = lax.ppermute(first, 'rows', pairs)]
    pallas_call x3 -> x4, Pallas kernels: 4.94 us -> 5.22 us  [predict(): pl.pallas_call(functools.partial(predict_kernel, len(matrix), parts, slot...]
where the time goes in v7:
time: 90.4 us; the launch traced here: 90.1 us
  waiting for transfers between devices  31.3 us (35%)
  starting transfers between devices  24.5 us (27%)
  Pallas kernels  23.5 us (26%)
  blocking collectives  9.33 us (10%)
    ppermute x9, starting transfers between devices, shards(): piece.append(lax.ppermute(piece[-1], 'rows', step))  20.5 us
    ppermute x3, waiting for transfers between devices, exchange(): rest = lax.ppermute(rest, 'rows', pairs)  16.9 us
    ppermute x9, waiting for transfers between devices, shards(): piece.append(lax.ppermute(piece[-1], 'rows', step))  14.5 us
    pallas_call x2, Pallas kernels, spectra_of(): pl.pallas_call(functools.partial(spectra_kernel, bands, bins, taps, part,...  11.8 us
    all_to_all x1, blocking collectives, shards(): lax.all_to_all(partial_value, 'rows', split_axis=0, concat_axis=0, tiled=...  9.33 us
    pallas_call x4, Pallas kernels, rows_for(): pl.pallas_call(functools.partial(rows_kernel, block, head, starts), in_sp...  5.61 us
    pallas_call x4, Pallas kernels, predict(): pl.pallas_call(functools.partial(predict_kernel, len(matrix), parts, slot...  5.22 us
    ppermute x3, starting transfers between devices, exchange(): rest = lax.ppermute(rest, 'rows', pairs)  2.13 us
  transfers between devices with their start and end apart: 15, of which 6 were waited for; matrix products, arithmetic and copies ran while one was open for 0% of the time, Pallas kernels for 17%

profile of v7, /device:TPU:0, one launch (start us, length us, event | category | flops | bytes accessed | tf_op | source)
XLA Modules:
  0.0 90.1 jit_solution(822521154999112200)
XLA Ops:
  0.0 5.9 %spectra.2 = (bf16[4,256,128]{2,1,0:T(8,128)(2,1)}, bf16[128,256]{1,0:T(8,128)(2,1)}, bf16[512,128]{1,0:T(8,128)(2,1)}) custom-call(bf16[8,256,2048]{2,1,0:T(8,128)(2,1)} %refs_0_.3, s32[8,256]{1,0:T(8,128)} %refs_1_.3, bf16[2048,256]{1,0:T(8,128)(2,1)} %constant.26.clone.refs_2_, f32[16,32]{1,0:T(8,128)} %refs_3_.1, f32[32,256]{1,0:T(8,128)} %constant.27.clone.refs_4_, ...), custom_call_target="tpu_custom_call" | custom-call | flops 1073741824 | bytes 4194304 | tf_op jit(solution)/shard_map/spectra/pallas_call | solution.py:174
  5.9 4.1 %collective-permute-start.6 = (bf16[4,256,128]{2,1,0:T(8,128)(2,1)}, bf16[4,256,128]{2,1,0:T(8,128)(2,1)S(1)}, u32[]{:S(2)}, u32[]{:S(2)}) collective-permute-start(bf16[4,256,128]{2,1,0:T(8,128)(2,1)} %get-tuple-element.25.refs_1_.refs_3_), channel_id=1, source_target_pairs={{0,8},{1,9},{2,10},{3,11},{4,0},{5,1},{6,2},{7,3},{8,12},{9,13},{1... | collective-permute-start | bytes 786440 | tf_op jit(solution)/shard_map/ppermute | solution.py:425
  10.1 5.9 %spectra.3 = (bf16[3,256,128]{2,1,0:T(8,128)(2,1)}, bf16[1,256,128]{2,1,0:T(8,128)(2,1)}) custom-call(bf16[8,256,2048]{2,1,0:T(8,128)(2,1)} %refs_0_.3, s32[8,256]{1,0:T(8,128)} %refs_1_.3, bf16[2048,256]{1,0:T(8,128)(2,1)} %constant.26.clone.refs_2_, bf16[128,256]{1,0:T(8,128)(2,1)} %get-tuple-element.22.refs_3_, bf16[512,128]{1,0:T(8,128)(2,1)} %get-tuple-element.23.refs_4_), custom_call_target="tpu_custom_call" | custom-call | flops 1073741824 | bytes 4194304 | tf_op jit(solution)/shard_map/spectra/pallas_call | solution.py:174
  15.9 1.6 %collective-permute-start.11 = (bf16[1,256,128]{2,1,0:T(8,128)(2,1)}, bf16[1,256,128]{2,1,0:T(8,128)(2,1)S(1)}, u32[]{:S(2)}, u32[]{:S(2)}) collective-permute-start(bf16[1,256,128]{2,1,0:T(8,128)(2,1)} %get-tuple-element.29.refs_7_.refs_5_), channel_id=1, source_target_pairs={{0,8},{1,9},{2,10},{3,11},{4,0},{5,1},{6,2},{7,3},{8,12},{9,13},{1... | collective-permute-start | bytes 196616 | tf_op jit(solution)/shard_map/ppermute | solution.py:425
  17.6 0.3 collective-permute-start.3
  17.9 1.4 %rows_for.7 = (bf16[3,4,16,2,4,256]{5,4,3,2,1,0:T(4,128)(2,1)S(1)}, bf16[1,4,16,2,4,256]{5,4,3,2,1,0:T(4,128)(2,1)S(1)}) custom-call(bf16[4,16,2,4,4096]{4,3,2,1,0:T(4,128)(2,1)} %bitcast.5), custom_call_target="tpu_custom_call" | custom-call | tf_op jit(solution)/shard_map/rows_for/pallas_call | solution.py:241
  19.3 0.2 collective-permute-start.10
  19.5 1.7 %collective-permute-done.11.refs_8_.refs_6_ = bf16[1,256,128]{2,1,0:T(8,128)(2,1)S(1)} collective-permute-done((bf16[1,256,128]{2,1,0:T(8,128)(2,1)}, bf16[1,256,128]{2,1,0:T(8,128)(2,1)S(1)}, u32[]{:S(2)}, u32[]{:S(2)}) %collective-permute-start.11) | collective-permute-done | bytes 65568 | tf_op jit(solution)/shard_map/ppermute | solution.py:425
  21.2 2.5 %collective-permute-start.12 = (bf16[1,256,128]{2,1,0:T(8,128)(2,1)S(1)}, bf16[1,256,128]{2,1,0:T(8,128)(2,1)S(1)}, u32[]{:S(2)}, u32[]{:S(2)}) collective-permute-start(bf16[1,256,128]{2,1,0:T(8,128)(2,1)S(1)} %collective-permute-done.11.refs_8_.refs_6_), channel_id=1, source_target_pairs={{0,8},{1,9},{2,10},{3,11},{4,0},{5,1},{6,2},{7,3},{8,12},{9,13},{1... | collective-permute-start | bytes 196616 | tf_op jit(solution)/shard_map/ppermute | solution.py:425
  23.6 2.3 %collective-permute-done.12.refs_9_.refs_7_ = bf16[1,256,128]{2,1,0:T(8,128)(2,1)S(1)} collective-permute-done((bf16[1,256,128]{2,1,0:T(8,128)(2,1)S(1)}, bf16[1,256,128]{2,1,0:T(8,128)(2,1)S(1)}, u32[]{:S(2)}, u32[]{:S(2)}) %collective-permute-start.12) | collective-permute-done | bytes 65568 | tf_op jit(solution)/shard_map/ppermute | solution.py:425
  26.0 2.8 %collective-permute-start.13 = (bf16[1,256,128]{2,1,0:T(8,128)(2,1)S(1)}, bf16[1,256,128]{2,1,0:T(8,128)(2,1)S(1)}, u32[]{:S(2)}, u32[]{:S(2)}) collective-permute-start(bf16[1,256,128]{2,1,0:T(8,128)(2,1)S(1)} %collective-permute-done.12.refs_9_.refs_7_), channel_id=1, source_target_pairs={{0,8},{1,9},{2,10},{3,11},{4,0},{5,1},{6,2},{7,3},{8,12},{9,13},{1... | collective-permute-start | bytes 196616 | tf_op jit(solution)/shard_map/ppermute | solution.py:425
  28.8 1.4 %rows_for.5 = (bf16[3,4,16,2,4,256]{5,4,3,2,1,0:T(4,128)(2,1)S(1)}, bf16[1,4,16,2,4,256]{5,4,3,2,1,0:T(4,128)(2,1)S(1)}) custom-call(bf16[4,16,2,4,4096]{4,3,2,1,0:T(4,128)(2,1)} %bitcast.6), custom_call_target="tpu_custom_call" | custom-call | tf_op jit(solution)/shard_map/rows_for/pallas_call | solution.py:241
  30.2 0.0 copy-start.2
  30.2 0.0 copy-start.3
  30.2 0.0 copy-start.6
  30.2 0.1 collective-permute-start
  30.3 1.5 %rows_for.6 = (bf16[3,4,16,2,4,256]{5,4,3,2,1,0:T(4,128)(2,1)S(1)}, bf16[1,4,16,2,4,256]{5,4,3,2,1,0:T(4,128)(2,1)S(1)}) custom-call(bf16[4,16,2,4,4096]{4,3,2,1,0:T(4,128)(2,1)} %bitcast.7), custom_call_target="tpu_custom_call" | custom-call | tf_op jit(solution)/shard_map/rows_for/pallas_call | solution.py:241
  31.8 0.0 copy-start.11
  31.8 1.6 %collective-permute-start.1 = (bf16[3,4,16,2,4,256]{5,4,3,2,1,0:T(4,128)(2,1)S(1)}, bf16[3,4,16,2,4,256]{5,4,3,2,1,0:T(4,128)(2,1)S(1)}, u32[]{:S(2)}, u32[]{:S(2)}) collective-permute-start(bf16[3,4,16,2,4,256]{5,4,3,2,1,0:T(4,128)(2,1)S(1)} %get-tuple-element.20), channel_id=1, source_target_pairs={{0,2},{1,3},{2,0},{3,1},{4,6},{5,7},{6,4},{7,5},{8,10},{9,11},{10,... | collective-permute-start | bytes 2359304 | tf_op jit(solution)/shard_map/ppermute | solution.py:411
  33.4 0.2 collective-permute-start.2
  33.6 0.4 collective-permute-start.9
  34.1 2.1 %collective-permute-start.7 = (bf16[4,256,128]{2,1,0:T(8,128)(2,1)S(1)}, bf16[4,256,128]{2,1,0:T(8,128)(2,1)S(1)}, u32[]{:S(2)}, u32[]{:S(2)}) collective-permute-start(bf16[4,256,128]{2,1,0:T(8,128)(2,1)S(1)} %collective-permute-done.6.refs_2_.refs_4_), channel_id=1, source_target_pairs={{0,8},{1,9},{2,10},{3,11},{4,0},{5,1},{6,2},{7,3},{8,12},{9,13},{1... | collective-permute-start | bytes 786440 | tf_op jit(solution)/shard_map/ppermute | solution.py:425
  36.1 1.2 %collective-permute-start.4 = (bf16[3,256,128]{2,1,0:T(8,128)(2,1)S(1)}, bf16[3,256,128]{2,1,0:T(8,128)(2,1)S(1)}, u32[]{:S(2)}, u32[]{:S(2)}) collective-permute-start(bf16[3,256,128]{2,1,0:T(8,128)(2,1)S(1)} %collective-permute-done.3.refs_2_), channel_id=1, source_target_pairs={{0,8},{1,9},{2,10},{3,11},{4,0},{5,1},{6,2},{7,3},{8,12},{9,13},{1... | collective-permute-start | bytes 589832 | tf_op jit(solution)/shard_map/ppermute | solution.py:425
  37.3 6.0 %collective-permute-done.7.refs_3_.refs_5_ = bf16[4,256,128]{2,1,0:T(8,128)(2,1)S(1)} collective-permute-done((bf16[4,256,128]{2,1,0:T(8,128)(2,1)S(1)}, bf16[4,256,128]{2,1,0:T(8,128)(2,1)S(1)}, u32[]{:S(2)}, u32[]{:S(2)}) %collective-permute-start.7) | collective-permute-done | bytes 262176 | tf_op jit(solution)/shard_map/ppermute | solution.py:425
  43.2 3.0 %collective-permute-start.8 = (bf16[4,256,128]{2,1,0:T(8,128)(2,1)S(1)}, bf16[4,256,128]{2,1,0:T(8,128)(2,1)S(1)}, u32[]{:S(2)}, u32[]{:S(2)}) collective-permute-start(bf16[4,256,128]{2,1,0:T(8,128)(2,1)S(1)} %collective-permute-done.7.refs_3_.refs_5_), channel_id=1, source_target_pairs={{0,8},{1,9},{2,10},{3,11},{4,0},{5,1},{6,2},{7,3},{8,12},{9,13},{1... | collective-permute-start | bytes 786440 | tf_op jit(solution)/shard_map/ppermute | solution.py:425
  46.2 1.3 %collective-permute-done.4.refs_3_ = bf16[3,256,128]{2,1,0:T(8,128)(2,1)S(1)} collective-permute-done((bf16[3,256,128]{2,1,0:T(8,128)(2,1)S(1)}, bf16[3,256,128]{2,1,0:T(8,128)(2,1)S(1)}, u32[]{:S(2)}, u32[]{:S(2)}) %collective-permute-start.4) | collective-permute-done | bytes 196640 | tf_op jit(solution)/shard_map/ppermute | solution.py:425
  47.5 1.5 %collective-permute-start.14 = (bf16[1,4,16,2,4,256]{5,4,3,2,1,0:T(4,128)(2,1)S(1)}, bf16[1,4,16,2,4,256]{5,4,3,2,1,0:T(4,128)(2,1)S(1)}, u32[]{:S(2)}, u32[]{:S(2)}) collective-permute-start(bf16[1,4,16,2,4,256]{5,4,3,2,1,0:T(4,128)(2,1)S(1)} %get-tuple-element.30), channel_id=1, source_target_pairs={{0,2},{1,3},{2,0},{3,1},{4,6},{5,7},{6,4},{7,5},{8,10},{9,11},{10,... | collective-permute-start | bytes 786440 | tf_op jit(solution)/shard_map/ppermute | solution.py:412
  49.0 3.2 %collective-permute-done.8.refs_4_.refs_6_ = bf16[4,256,128]{2,1,0:T(8,128)(2,1)S(1)} collective-permute-done((bf16[4,256,128]{2,1,0:T(8,128)(2,1)S(1)}, bf16[4,256,128]{2,1,0:T(8,128)(2,1)S(1)}, u32[]{:S(2)}, u32[]{:S(2)}) %collective-permute-start.8) | collective-permute-done | bytes 262176 | tf_op jit(solution)/shard_map/ppermute | solution.py:425
  52.2 2.9 %collective-permute-start.5 = (bf16[3,256,128]{2,1,0:T(8,128)(2,1)S(1)}, bf16[3,256,128]{2,1,0:T(8,128)(2,1)S(1)}, u32[]{:S(2)}, u32[]{:S(2)}) collective-permute-start(bf16[3,256,128]{2,1,0:T(8,128)(2,1)S(1)} %collective-permute-done.4.refs_3_), channel_id=1, source_target_pairs={{0,8},{1,9},{2,10},{3,11},{4,0},{5,1},{6,2},{7,3},{8,12},{9,13},{1... | collective-permute-start | bytes 589832 | tf_op jit(solution)/shard_map/ppermute | solution.py:425
  55.1 1.4 %rows_for.4 = (bf16[3,4,16,2,4,256]{5,4,3,2,1,0:T(4,128)(2,1)S(1)}, bf16[1,4,16,2,4,256]{5,4,3,2,1,0:T(4,128)(2,1)S(1)}) custom-call(bf16[4,16,2,4,4096]{4,3,2,1,0:T(4,128)(2,1)} %bitcast.8), custom_call_target="tpu_custom_call" | custom-call | tf_op jit(solution)/shard_map/rows_for/pallas_call | solution.py:241
  56.6 0.7 predict.6
  57.3 0.0 copy-start.12
  57.3 0.0 copy-start.1
  57.3 0.0 copy-start.9
  57.3 0.0 copy-start.10
  57.4 16.9 %collective-permute-done.14.refs_0_ = bf16[1,4,16,2,4,256]{5,4,3,2,1,0:T(4,128)(2,1)S(1)} collective-permute-done((bf16[1,4,16,2,4,256]{5,4,3,2,1,0:T(4,128)(2,1)S(1)}, bf16[1,4,16,2,4,256]{5,4,3,2,1,0:T(4,128)(2,1)S(1)}, u32[]{:S(2)}, u32[]{:S(2)}) %collective-permute-start.14) | collective-permute-done | bytes 262176 | tf_op jit(solution)/shard_map/ppermute | solution.py:412
  74.2 0.4 predict.7
  74.7 0.0 copy-start.7
  74.7 0.0 copy-start.8
  74.7 0.8 merge.1.refs_0_
  75.6 0.0 copy-start.13
  75.6 2.0 %predict.4.refs_8_ = bf16[12,16,64]{2,1,0:T(8,128)(2,1)S(1)} custom-call(bf16[3,512,1024]{2,1,0:T(8,128)(2,1)S(1)} %merge.1.refs_0_, bf16[4,256,128]{2,1,0:T(8,128)(2,1)S(1)} %copy-done, bf16[4,256,128]{2,1,0:T(8,128)(2,1)S(1)} %collective-permute-done.6.refs_2_.refs_4_, bf16[4,256,128]{2,1,0:T(8,128)(2,1)S(1)} %collective-permute-done.7.refs_3_.refs_5_, ...), custom_call_target="tpu_custom_call" | custom-call | tf_op jit(solution)/shard_map/predict/pallas_call | solution.py:364
  77.7 0.0 slice-start
  77.7 2.0 %predict.5 = bf16[12,16,64]{2,1,0:T(8,128)(2,1)S(1)} custom-call(bf16[3,512,1024]{2,1,0:T(8,128)(2,1)S(1)} %merge.1.refs_0_, bf16[3,256,128]{2,1,0:T(8,128)(2,1)S(1)} %copy-done.5, bf16[3,256,128]{2,1,0:T(8,128)(2,1)S(1)} %collective-permute-done.3.refs_2_, bf16[3,256,128]{2,1,0:T(8,128)(2,1)S(1)} %collective-permute-done.4.refs_3_, ...), custom_call_target="tpu_custom_call" | custom-call | tf_op jit(solution)/shard_map/predict/pallas_call | solution.py:364
  79.8 0.1 reshape.15
  79.9 9.3 %all_to_all.5 = bf16[16,2,512]{2,1,0:T(2,128)(2,1)S(1)} all-to-all(bf16[16,2,512]{2,1,0:T(2,128)(2,1)S(1)} %reshape.15), channel_id=1, replica_groups=mesh['parts'=2,'rows'=16] {'rows'}, dimensions={0} | all-to-all | bytes 65536 | tf_op jit(solution)/shard_map/all_to_all | solution.py:446
  89.2 0.1 reshape.16
  89.3 0.8 convolution_convert_fusion
  (29 shorter events, 0.1 us)
Async XLA Ops:
  5.9 27.7 %collective-permute-start.6 = (bf16[4,256,128]{2,1,0:T(8,128)(2,1)}, bf16[4,256,128]{2,1,0:T(8,128)(2,1)S(1)}, u32[]{:S(2)}, u32[]{:S(2)}) collective-permute-start(bf16[4,256,128]{2,1,0:T(8,128)(2,1)} %get-tuple-element.25.refs_1_.refs_3_), channel_id=1, source_target_pairs={{0,8},{1,9},{2,10},{3,11},{4,0},{5,1},{6,2},{7,3},{8,12},{9,13},{1... | collective-permute-start | bytes 786440 | tf_op jit(solution)/shard_map/ppermute | solution.py:425
  15.9 5.2 %collective-permute-start.11 = (bf16[1,256,128]{2,1,0:T(8,128)(2,1)}, bf16[1,256,128]{2,1,0:T(8,128)(2,1)S(1)}, u32[]{:S(2)}, u32[]{:S(2)}) collective-permute-start(bf16[1,256,128]{2,1,0:T(8,128)(2,1)} %get-tuple-element.29.refs_7_.refs_5_), channel_id=1, source_target_pairs={{0,8},{1,9},{2,10},{3,11},{4,0},{5,1},{6,2},{7,3},{8,12},{9,13},{1... | collective-permute-start | bytes 196616 | tf_op jit(solution)/shard_map/ppermute | solution.py:425
  17.6 15.9 %collective-permute-start.3 = (bf16[3,256,128]{2,1,0:T(8,128)(2,1)}, bf16[3,256,128]{2,1,0:T(8,128)(2,1)S(1)}, u32[]{:S(2)}, u32[]{:S(2)}) collective-permute-start(bf16[3,256,128]{2,1,0:T(8,128)(2,1)} %get-tuple-element.24.refs_1_), channel_id=1, source_target_pairs={{0,8},{1,9},{2,10},{3,11},{4,0},{5,1},{6,2},{7,3},{8,12},{9,13},{1... | collective-permute-start | bytes 589832 | tf_op jit(solution)/shard_map/ppermute | solution.py:425
  19.3 14.8 %collective-permute-start.10 = (bf16[1,4,16,2,4,256]{5,4,3,2,1,0:T(4,128)(2,1)S(1)}, bf16[1,4,16,2,4,256]{5,4,3,2,1,0:T(4,128)(2,1)S(1)}, u32[]{:S(2)}, u32[]{:S(2)}) collective-permute-start(bf16[1,4,16,2,4,256]{5,4,3,2,1,0:T(4,128)(2,1)S(1)} %get-tuple-element.28), channel_id=1, source_target_pairs={{0,3},{1,2},{2,1},{3,0},{4,7},{5,6},{6,5},{7,4},{8,11},{9,10},{10,... | collective-permute-start | bytes 786440 | tf_op jit(solution)/shard_map/ppermute | solution.py:412
  21.2 4.8 %collective-permute-start.12 = (bf16[1,256,128]{2,1,0:T(8,128)(2,1)S(1)}, bf16[1,256,128]{2,1,0:T(8,128)(2,1)S(1)}, u32[]{:S(2)}, u32[]{:S(2)}) collective-permute-start(bf16[1,256,128]{2,1,0:T(8,128)(2,1)S(1)} %collective-permute-done.11.refs_8_.refs_6_), channel_id=1, source_target_pairs={{0,8},{1,9},{2,10},{3,11},{4,0},{5,1},{6,2},{7,3},{8,12},{9,13},{1... | collective-permute-start | bytes 196616 | tf_op jit(solution)/shard_map/ppermute | solution.py:425
  26.0 5.9 %collective-permute-start.13 = (bf16[1,256,128]{2,1,0:T(8,128)(2,1)S(1)}, bf16[1,256,128]{2,1,0:T(8,128)(2,1)S(1)}, u32[]{:S(2)}, u32[]{:S(2)}) collective-permute-start(bf16[1,256,128]{2,1,0:T(8,128)(2,1)S(1)} %collective-permute-done.12.refs_9_.refs_7_), channel_id=1, source_target_pairs={{0,8},{1,9},{2,10},{3,11},{4,0},{5,1},{6,2},{7,3},{8,12},{9,13},{1... | collective-permute-start | bytes 196616 | tf_op jit(solution)/shard_map/ppermute | solution.py:425
  30.2 26.3 %copy-start = (bf16[4,256,128]{2,1,0:T(8,128)(2,1)S(1)}, bf16[4,256,128]{2,1,0:T(8,128)(2,1)}, u32[]{:S(2)}) copy-start(bf16[4,256,128]{2,1,0:T(8,128)(2,1)} %get-tuple-element.25.refs_1_.refs_3_) | copy-start | bytes 786436
  30.2 26.3 %copy-start.2 = (bf16[1,256,64]{2,1,0:T(8,128)(2,1)S(1)}, bf16[1,256,64]{2,1,0:T(8,128)(2,1)}, u32[]{:S(2)}) copy-start(bf16[1,256,64]{2,1,0:T(8,128)(2,1)} %constant.35.clone.refs_12_.refs_10_) | copy-start | bytes 98308
  30.2 26.3 %copy-start.3 = (bf16[1,256,64]{2,1,0:T(8,128)(2,1)S(1)}, bf16[1,256,64]{2,1,0:T(8,128)(2,1)}, u32[]{:S(2)}) copy-start(bf16[1,256,64]{2,1,0:T(8,128)(2,1)} %constant.36.clone.refs_13_.refs_11_) | copy-start | bytes 98308
  30.2 26.3 %copy-start.4 = (bf16[1,256,128]{2,1,0:T(8,128)(2,1)S(1)}, bf16[1,256,128]{2,1,0:T(8,128)(2,1)}, u32[]{:S(2)}) copy-start(bf16[1,256,128]{2,1,0:T(8,128)(2,1)} %get-tuple-element.29.refs_7_.refs_5_) | copy-start | bytes 196612
  30.2 26.3 %copy-start.6 = (f32[192,256]{1,0:T(8,128)S(1)}, f32[192,256]{1,0:T(8,128)}, u32[]{:S(2)}) copy-start(f32[192,256]{1,0:T(8,128)} %constant.34.clone.refs_11_) | copy-start | bytes 589828
  30.2 44.4 %collective-permute-start = (bf16[3,4,16,2,4,256]{5,4,3,2,1,0:T(4,128)(2,1)S(1)}, bf16[3,4,16,2,4,256]{5,4,3,2,1,0:T(4,128)(2,1)S(1)}, u32[]{:S(2)}, u32[]{:S(2)}) collective-permute-start(bf16[3,4,16,2,4,256]{5,4,3,2,1,0:T(4,128)(2,1)S(1)} %get-tuple-element.19), channel_id=1, source_target_pairs={{0,1},{1,0},{2,3},{3,2},{4,5},{5,4},{6,7},{7,6},{8,9},{9,8},{10,11... | collective-permute-start | bytes 2359304 | tf_op jit(solution)/shard_map/ppermute | solution.py:411
  31.8 42.4 %copy-start.11 = (f32[64,256]{1,0:T(8,128)S(1)}, f32[64,256]{1,0:T(8,128)}, u32[]{:S(2)}) copy-start(f32[64,256]{1,0:T(8,128)} %constant.37.clone.refs_9_) | copy-start | bytes 196612
  31.8 42.8 %collective-permute-start.1 = (bf16[3,4,16,2,4,256]{5,4,3,2,1,0:T(4,128)(2,1)S(1)}, bf16[3,4,16,2,4,256]{5,4,3,2,1,0:T(4,128)(2,1)S(1)}, u32[]{:S(2)}, u32[]{:S(2)}) collective-permute-start(bf16[3,4,16,2,4,256]{5,4,3,2,1,0:T(4,128)(2,1)S(1)} %get-tuple-element.20), channel_id=1, source_target_pairs={{0,2},{1,3},{2,0},{3,1},{4,6},{5,7},{6,4},{7,5},{8,10},{9,11},{10,... | collective-permute-start | bytes 2359304 | tf_op jit(solution)/shard_map/ppermute | solution.py:411
  33.4 41.2 %collective-permute-start.2 = (bf16[3,4,16,2,4,256]{5,4,3,2,1,0:T(4,128)(2,1)S(1)}, bf16[3,4,16,2,4,256]{5,4,3,2,1,0:T(4,128)(2,1)S(1)}, u32[]{:S(2)}, u32[]{:S(2)}) collective-permute-start(bf16[3,4,16,2,4,256]{5,4,3,2,1,0:T(4,128)(2,1)S(1)} %get-tuple-element.21), channel_id=1, source_target_pairs={{0,3},{1,2},{2,1},{3,0},{4,7},{5,6},{6,5},{7,4},{8,11},{9,10},{10,... | collective-permute-start | bytes 2359304 | tf_op jit(solution)/shard_map/ppermute | solution.py:411
  33.6 2.5 %collective-permute-start.9 = (bf16[1,4,16,2,4,256]{5,4,3,2,1,0:T(4,128)(2,1)S(1)}, bf16[1,4,16,2,4,256]{5,4,3,2,1,0:T(4,128)(2,1)S(1)}, u32[]{:S(2)}, u32[]{:S(2)}) collective-permute-start(bf16[1,4,16,2,4,256]{5,4,3,2,1,0:T(4,128)(2,1)S(1)} %get-tuple-element.27), channel_id=1, source_target_pairs={{0,1},{1,0},{2,3},{3,2},{4,5},{5,4},{6,7},{7,6},{8,9},{9,8},{10,11... | collective-permute-start | bytes 786440 | tf_op jit(solution)/shard_map/ppermute | solution.py:412
  34.1 9.2 %collective-permute-start.7 = (bf16[4,256,128]{2,1,0:T(8,128)(2,1)S(1)}, bf16[4,256,128]{2,1,0:T(8,128)(2,1)S(1)}, u32[]{:S(2)}, u32[]{:S(2)}) collective-permute-start(bf16[4,256,128]{2,1,0:T(8,128)(2,1)S(1)} %collective-permute-done.6.refs_2_.refs_4_), channel_id=1, source_target_pairs={{0,8},{1,9},{2,10},{3,11},{4,0},{5,1},{6,2},{7,3},{8,12},{9,13},{1... | collective-permute-start | bytes 786440 | tf_op jit(solution)/shard_map/ppermute | solution.py:425
  36.1 11.3 %collective-permute-start.4 = (bf16[3,256,128]{2,1,0:T(8,128)(2,1)S(1)}, bf16[3,256,128]{2,1,0:T(8,128)(2,1)S(1)}, u32[]{:S(2)}, u32[]{:S(2)}) collective-permute-start(bf16[3,256,128]{2,1,0:T(8,128)(2,1)S(1)} %collective-permute-done.3.refs_2_), channel_id=1, source_target_pairs={{0,8},{1,9},{2,10},{3,11},{4,0},{5,1},{6,2},{7,3},{8,12},{9,13},{1... | collective-permute-start | bytes 589832 | tf_op jit(solution)/shard_map/ppermute | solution.py:425
  43.2 9.0 %collective-permute-start.8 = (bf16[4,256,128]{2,1,0:T(8,128)(2,1)S(1)}, bf16[4,256,128]{2,1,0:T(8,128)(2,1)S(1)}, u32[]{:S(2)}, u32[]{:S(2)}) collective-permute-start(bf16[4,256,128]{2,1,0:T(8,128)(2,1)S(1)} %collective-permute-done.7.refs_3_.refs_5_), channel_id=1, source_target_pairs={{0,8},{1,9},{2,10},{3,11},{4,0},{5,1},{6,2},{7,3},{8,12},{9,13},{1... | collective-permute-start | bytes 786440 | tf_op jit(solution)/shard_map/ppermute | solution.py:425
  47.5 26.7 %collective-permute-start.14 = (bf16[1,4,16,2,4,256]{5,4,3,2,1,0:T(4,128)(2,1)S(1)}, bf16[1,4,16,2,4,256]{5,4,3,2,1,0:T(4,128)(2,1)S(1)}, u32[]{:S(2)}, u32[]{:S(2)}) collective-permute-start(bf16[1,4,16,2,4,256]{5,4,3,2,1,0:T(4,128)(2,1)S(1)} %get-tuple-element.30), channel_id=1, source_target_pairs={{0,2},{1,3},{2,0},{3,1},{4,6},{5,7},{6,4},{7,5},{8,10},{9,11},{10,... | collective-permute-start | bytes 786440 | tf_op jit(solution)/shard_map/ppermute | solution.py:412
  52.2 25.4 %collective-permute-start.5 = (bf16[3,256,128]{2,1,0:T(8,128)(2,1)S(1)}, bf16[3,256,128]{2,1,0:T(8,128)(2,1)S(1)}, u32[]{:S(2)}, u32[]{:S(2)}) collective-permute-start(bf16[3,256,128]{2,1,0:T(8,128)(2,1)S(1)} %collective-permute-done.4.refs_3_), channel_id=1, source_target_pairs={{0,8},{1,9},{2,10},{3,11},{4,0},{5,1},{6,2},{7,3},{8,12},{9,13},{1... | collective-permute-start | bytes 589832 | tf_op jit(solution)/shard_map/ppermute | solution.py:425
  57.3 20.3 %copy-start.12 = (bf16[4,12,64]{2,1,0:T(8,128)(2,1)}, bf16[4,12,64]{2,1,0:T(8,128)(2,1)S(1)}, u32[]{:S(2)}) copy-start(bf16[4,12,64]{2,1,0:T(8,128)(2,1)S(1)} %predict.6) | copy-start | bytes 18436
  57.3 18.2 %copy-start.1 = (f32[256,128]{1,0:T(8,128)S(1)}, f32[256,128]{1,0:T(8,128)}, u32[]{:S(2)}) copy-start(f32[256,128]{1,0:T(8,128)} %constant.29.clone.refs_5_) | copy-start | bytes 393220
  57.3 18.2 %copy-start.9 = (bf16[3,128,64]{2,1,0:T(8,128)(2,1)S(1)}, bf16[3,128,64]{2,1,0:T(8,128)(2,1)}, u32[]{:S(2)}) copy-start(bf16[3,128,64]{2,1,0:T(8,128)(2,1)} %constant.30.clone.refs_6_) | copy-start | bytes 147460
  57.3 18.2 %copy-start.10 = (bf16[3,128,64]{2,1,0:T(8,128)(2,1)S(1)}, bf16[3,128,64]{2,1,0:T(8,128)(2,1)}, u32[]{:S(2)}) copy-start(bf16[3,128,64]{2,1,0:T(8,128)(2,1)} %constant.31.clone.refs_7_) | copy-start | bytes 147460
  74.7 3.0 %copy-start.5 = (bf16[3,256,128]{2,1,0:T(8,128)(2,1)S(1)}, bf16[3,256,128]{2,1,0:T(8,128)(2,1)}, u32[]{:S(2)}) copy-start(bf16[3,256,128]{2,1,0:T(8,128)(2,1)} %get-tuple-element.24.refs_1_) | copy-start | bytes 589828
  74.7 3.0 %copy-start.7 = (bf16[3,128,64]{2,1,0:T(8,128)(2,1)S(1)}, bf16[3,128,64]{2,1,0:T(8,128)(2,1)}, u32[]{:S(2)}) copy-start(bf16[3,128,64]{2,1,0:T(8,128)(2,1)} %constant.32.clone.refs_6_) | copy-start | bytes 147460
  74.7 3.0 %copy-start.8 = (bf16[3,128,64]{2,1,0:T(8,128)(2,1)S(1)}, bf16[3,128,64]{2,1,0:T(8,128)(2,1)}, u32[]{:S(2)}) copy-start(bf16[3,128,64]{2,1,0:T(8,128)(2,1)} %constant.33.clone.refs_7_) | copy-start | bytes 147460
  75.6 13.7 %copy-start.13 = (bf16[256,64]{1,0:T(8,128)(2,1)S(1)}, bf16[256,64]{1,0:T(8,128)(2,1)}, u32[]{:S(2)}) copy-start(bf16[256,64]{1,0:T(8,128)(2,1)} %constant.38.clone) | copy-start | bytes 98308
  77.7 2.0 %slice-start = ((bf16[4,12,64]{2,1,0:T(8,128)(2,1)}), bf16[4,8,64]{2,1,0:T(8,128)(2,1)S(1)}, s32[]{:S(2)}) async-start(bf16[4,12,64]{2,1,0:T(8,128)(2,1)} %copy-done.12), calls=%async_computation.1 | async-start | bytes 16384 | tf_op jit(solution)/shard_map/slice | solution.py:444
